TPU v7x, 256 devices: a whole 4x4x8 slice. The times are simulated.
256 devices in a mesh: prompt: 8 (over x, y_lo), tensor: 32 (over z, y_hi, core).
Axes of the slice: x: 4, y: 4 (y_hi: 2, y_lo: 2; y = y_hi * 2 + y_lo), z: 8, core: 2. Of those that a mesh axis runs over, the one named last changes fastest.
Arguments:
- tokens: bfloat16 [8, 128, 8192], P('prompt')
- gate_weight: bfloat16 [8192, 28672], P('prompt', 'tensor'), may hold values from -0.0625 to 0.0625
- up_weight: bfloat16 [8192, 28672], P('prompt', 'tensor'), may hold values from -0.0625 to 0.0625
- down_weight: bfloat16 [28672, 8192], P('tensor', 'prompt')
- norm_gain: float32 [8192], P('prompt'), may hold values from 0.1 to 1.9
- unembed: bfloat16 [8192, 86016], P('prompt', 'tensor'), may hold values from -0.5 to 0.5
- guidance: float32 [8], replicated, may hold values from -1.5 to 2.5
- logit_bias: float32 [128, 86016], P('prompt', 'tensor'), may hold values from -2 to 322
Outputs:
- log_probs: float32 [128, 86016], P('prompt', 'tensor')
All inputs are finite; a program needn't handle non-finite values.
Results may differ from a plain program's by a relative error of at most 0.0025.
Values may be sent and summed in bfloat16 or wider, within the bound.
No kernel may reach another device: no remote copies, remote signals or barrier semaphores. Data moves between devices by JAX's collectives and lax.ppermute only.
A program may use at most 64 MiB of HBM per device.

v0:
```python
import jax
import jax.numpy as jnp
from jax import lax
from jax.sharding import Mesh
from jax.sharding import PartitionSpec as P


D = 8192
EPS = 1e-05
NX, NY, NZ, NW, NC = 4, 2, 8, 2, 2
AXES = ("x", "y", "z", "w", "c")
PROMPT = ("x", "y")
TENSOR = ("z", "w", "c")
BF, F32 = jnp.bfloat16, jnp.float32


def shifted(array, axis, size, step):
    return lax.ppermute(array, axis, [(i, (i + step) % size) for i in range(size)])


def wide(array):
    return array.astype(F32)


def tokens_for_block(tokens, c):
    half = tokens.shape[0] // NC
    share = D // (NX * NY)
    mine = lax.dynamic_slice_in_dim(tokens, c * half, half, 0)
    blocks = mine.reshape(half, NX * NY, share).transpose(1, 0, 2)
    own = lax.all_to_all(blocks, PROMPT, 0, 0, tiled=True)
    other = shifted(own, "c", NC, 1)
    shape = (NX, NY, half, share)
    return own.reshape(shape), other.reshape(shape)


def at(array, index, axis):
    return lax.dynamic_index_in_dim(array, index, axis, keepdims=False)


def products(rows, weights):
    flat = rows.reshape(-1, rows.shape[-1])
    outs = [jnp.dot(flat, weight, preferred_element_type=F32) for weight in weights]
    return [out.reshape(*rows.shape[:-1], -1) for out in outs]


def joined(pair):
    return jnp.stack([part.astype(BF) for part in pair])


def step(tokens, gate_weight, up_weight, down_weight, norm_gain, unembed, guidance, logit_bias):
    x, y, z, _, c = (lax.axis_index(axis) for axis in AXES)
    tokens = tokens[0]
    own, other = tokens_for_block(tokens, c)
    both = (gate_weight, up_weight)

    def toward(d):
        return (x + d) % NX

    pa = products(own, both)
    swap_a = shifted(joined([at(p, 1 - y, 1) for p in pa]), "y", NY, 1)
    pb = products(other, both)
    got_b = [shifted(joined([at(p, toward(d), 0) for p in pb]), "x", NX, d) for d in (2, 1, 3)]
    swap_a, got_b = lax.optimization_barrier((swap_a, got_b))
    sum_a = [at(p, y, 1) + wide(got) for p, got in zip(pa, swap_a)]
    got_a = [shifted(joined([at(p, toward(d), 0) for p in sum_a]), "x", NX, d) for d in (2, 1, 3)]
    sum_b = [at(p, x, 0) + sum(wide(got[i]) for got in got_b) for i, p in enumerate(pb)]
    swap_b = shifted(joined([at(p, 1 - y, 0) for p in sum_b]), "y", NY, 1)
    gate_b, up_b = [at(p, y, 0) + wide(got) for p, got in zip(sum_b, swap_b)]
    hidden_b = (jax.nn.silu(gate_b) * up_b).astype(BF)
    gate_a, up_a = [at(p, x, 0) + sum(wide(g[i]) for g in got_a) for i, p in enumerate(sum_a)]
    hidden_a = (jax.nn.silu(gate_a) * up_a).astype(BF)

    line_b = [hidden_b] + [None] * (NX - 1)
    for d in (2, 1, 3):
        line_b[d] = shifted(hidden_b, "x", NX, -d)
    line_b = jnp.stack(line_b)
    all_b = jnp.stack([line_b, shifted(line_b, "y", NY, 1)], axis=1)
    pair_a = jnp.stack([hidden_a, shifted(hidden_a, "y", NY, 1)])
    all_a = [pair_a] + [None] * (NX - 1)
    for d in (2, 1, 3):
        all_a[d] = shifted(pair_a, "x", NX, -d)
    all_a = jnp.stack(all_a)

    (down_b,) = products(all_b, (down_weight,))
    passed = shifted(down_b.astype(BF), "c", NC, 1)
    (down_a,) = products(all_a, (down_weight,))
    share = down_a.shape[-1]
    part = down_a + wide(passed)
    part = part.reshape(NX * NY, NZ, -1, share)

    def piece(k):
        return lax.dynamic_index_in_dim(part, (z + k) % NZ, 1, keepdims=False)

    def sent(block, step):
        return shifted(block.astype(BF), "z", NZ, step)

    far = sent(piece(4), 4)
    relay_up, relay_down = sent(piece(3), 1), sent(piece(5), -1)
    one_up, one_down = sent(piece(1), 1), sent(piece(7), -1)
    two_up = sent(piece(2) + wide(relay_up), 2)
    two_down = sent(piece(6) + wide(relay_down), -2)
    mine = piece(0) + sum(wide(got) for got in (far, one_up, one_down, two_up, two_down))
    mine = mine.astype(BF)
    branch = wide(mine) + wide(shifted(mine, "w", NW, 1))

    residual = at(own.reshape(NX, NY, NZ, -1, share), z, 2)
    residual = jnp.concatenate([residual, residual])
    residual = lax.dynamic_slice_in_dim(residual, x, NX, 0)
    residual = jnp.where(y == 0, residual, residual[:, ::-1]).reshape(NX * NY, -1, share)
    state = wide(residual) + branch
    partial_square = jnp.sum(state * state, axis=2)
    offsets = jnp.arange(NX * NY)
    variant_at = ((x + offsets // NY) % NX) * NY + ((offsets % NY) ^ y)
    placed_at = (variant_at[None, :] == offsets[:, None]).astype(F32)
    by_variant = jnp.sum(placed_at[:, :, None] * partial_square[None], axis=1)
    everyone = lax.all_to_all(
        jnp.broadcast_to(by_variant[None], (NX * NY, *by_variant.shape)),
        PROMPT, 0, 0, tiled=True,
    )
    square = everyone.sum(axis=0)
    scale = lax.rsqrt(square / D + EPS) * guidance[:, None]
    scale = jnp.sum(placed_at[:, :, None] * scale[:, None], axis=0)
    mixed = (jnp.sum(state * scale[:, :, None], axis=0) * norm_gain).astype(BF)

    before = shifted(mixed, "z", NZ, 1)
    after = shifted(mixed, "z", NZ, -1)
    three = jnp.stack([before, mixed, after])
    low = shifted(three, "z", NZ, 3)
    high = shifted(three[:2], "z", NZ, -3)
    ring = jnp.concatenate([mixed[None], after[None], high, low, before[None]])
    ring = jnp.roll(ring, z, axis=0).reshape(-1, share)
    peer = shifted(ring, "c", NC, 1)
    first = jnp.where(c == 0, ring, peer)
    second = jnp.where(c == 0, peer, ring)
    rows = jnp.concatenate([first, second])

    product = jnp.dot(rows, unembed, preferred_element_type=F32).astype(BF)
    tiles = product.reshape(NX * NY, -1, product.shape[-1])
    tiles = lax.all_to_all(tiles, PROMPT, 0, 0, tiled=True)
    scores = jnp.sum(wide(tiles), axis=0) + logit_bias
    top = jnp.max(scores, axis=1, keepdims=True)
    part_lse = top[:, 0] + jnp.log(jnp.sum(jnp.exp(scores - top), axis=1))
    shards = NZ * NW * NC
    part_lse = lax.all_to_all(
        jnp.broadcast_to(part_lse[None, None], (shards, 1, part_lse.shape[0])),
        TENSOR, 0, 0, tiled=True,
    )
    lse = jax.nn.logsumexp(part_lse[:, 0], axis=0)
    return scores - lse[:, None]


def solution(mesh):
    finer = Mesh(mesh.devices.reshape(NX, NY, NZ, NW, NC), AXES)
    placed = (
        P(PROMPT, None, None),
        P(PROMPT, TENSOR),
        P(PROMPT, TENSOR),
        P(TENSOR, PROMPT),
        P(PROMPT),
        P(PROMPT, TENSOR),
        P(),
        P(PROMPT, TENSOR),
    )
    return jax.shard_map(
        step, mesh=finer, in_specs=placed, out_specs=P(PROMPT, TENSOR), check_vma=False
    )
```

profile of v0, /device:TPU:1, one launch (start us, length us, event | category | flops | bytes accessed | tf_op | source)
XLA Modules:
  0.0 222.9 jit_solution(12908852310271349636)
XLA Ops:
  2.9 20.0 %all_to_all.20 = bf16[8,64,1024]{2,1,0:T(8,128)(2,1)S(1)} all-to-all(bf16[8,64,1024]{2,1,0:T(8,128)(2,1)S(1)} %copy.53), channel_id=1, replica_groups=mesh['x'=4,'y'=2,'z'=8,'w'=2,'c'=2] {'x','y'}, dimensions={0} | all-to-all | bytes 2097152 | tf_op jit(solution)/shard_map/all_to_all | solution.py:30
  24.8 2.9 %fusion.6 = f32[4,2,64,896]{3,2,1,0:T(8,128)S(1)} fusion(bf16[4,2,64,1024]{3,2,1,0:T(8,128)(2,1)S(1)} %bitcast.182, bf16[1024,896]{1,0:T(8,128)(2,1)} %param.10), kind=kOutput, calls=%fused_computation.8 | convolution fusion | flops 939524096 | bytes 4718592 | tf_op jit(solution)/shard_map/dot_general | solution.py:42
  31.6 2.5 %fusion.4 = f32[4,2,64,896]{3,2,1,0:T(8,128)S(1)} fusion(bf16[4,2,64,1024]{3,2,1,0:T(8,128)(2,1)} %bitcast.12, bf16[1024,896]{1,0:T(8,128)(2,1)S(1)} %copy-done.10), kind=kOutput, calls=%fused_computation.6 | convolution fusion | flops 939524096 | bytes 4718592 | tf_op jit(solution)/shard_map/dot_general | solution.py:42
  34.1 3.1 %fusion.8 = f32[4,2,64,896]{3,2,1,0:T(8,128)S(1)} fusion(bf16[4,2,64,1024]{3,2,1,0:T(8,128)(2,1)} %bitcast.12, bf16[1024,896]{1,0:T(8,128)(2,1)S(1)} %copy-done.11), kind=kOutput, calls=%fused_computation.10 | convolution fusion | flops 939524096 | bytes 4718592 | tf_op jit(solution)/shard_map/dot_general | solution.py:42
  41.8 2.5 %collective-permute-start.4 = (bf16[2,2,64,896]{3,2,1,0:T(8,128)(2,1)}, bf16[2,2,64,896]{3,2,1,0:T(8,128)(2,1)}, u32[]{:S(2)}, u32[]{:S(2)}) collective-permute-start(bf16[2,2,64,896]{3,2,1,0:T(8,128)(2,1)} %pad_maximum_fusion.4), channel_id=1, source_target_pairs={{0,192},{64,0},{128,64},{192,128},{1,193},{65,1},{129,65},{193,129... | collective-permute-start | bytes 1376264 | tf_op jit(solution)/shard_map/ppermute | solution.py:18
  44.2 8.5 %collective-permute-done = bf16[2,4,64,896]{3,2,1,0:T(8,128)(2,1)} collective-permute-done((bf16[2,4,64,896]{3,2,1,0:T(8,128)(2,1)}, bf16[2,4,64,896]{3,2,1,0:T(8,128)(2,1)}, u32[]{:S(2)}, u32[]{:S(2)}) %collective-permute-start) | collective-permute-done | bytes 917536 | tf_op jit(solution)/shard_map/ppermute | solution.py:18
  52.7 10.1 %collective-permute-done.3 = bf16[2,2,64,896]{3,2,1,0:T(8,128)(2,1)} collective-permute-done((bf16[2,2,64,896]{3,2,1,0:T(8,128)(2,1)}, bf16[2,2,64,896]{3,2,1,0:T(8,128)(2,1)}, u32[]{:S(2)}, u32[]{:S(2)}) %collective-permute-start.3) | collective-permute-done | bytes 458784 | tf_op jit(solution)/shard_map/ppermute | solution.py:18
  67.2 4.4 %collective-permute-done.12 = bf16[2,64,896]{2,1,0:T(8,128)(2,1)S(1)} collective-permute-done((bf16[2,64,896]{2,1,0:T(8,128)(2,1)S(1)}, bf16[2,64,896]{2,1,0:T(8,128)(2,1)S(1)}, u32[]{:S(2)}, u32[]{:S(2)}) %collective-permute-start.12) | collective-permute-done | bytes 229408 | tf_op jit(solution)/shard_map/ppermute | solution.py:18
  75.1 3.4 %collective-permute-done.15 = bf16[64,896]{1,0:T(8,128)(2,1)S(1)} collective-permute-done((bf16[64,896]{1,0:T(8,128)(2,1)S(1)}, bf16[64,896]{1,0:T(8,128)(2,1)S(1)}, u32[]{:S(2)}, u32[]{:S(2)}) %collective-permute-start.15) | collective-permute-done | bytes 114720 | tf_op jit(solution)/shard_map/ppermute | solution.py:18
  83.5 5.7 %collective-permute-done.16 = bf16[4,64,896]{2,1,0:T(8,128)(2,1)S(1)} collective-permute-done((bf16[4,64,896]{2,1,0:T(8,128)(2,1)S(1)}, bf16[4,64,896]{2,1,0:T(8,128)(2,1)S(1)}, u32[]{:S(2)}, u32[]{:S(2)}) %collective-permute-start.16) | collective-permute-done | bytes 458784 | tf_op jit(solution)/shard_map/ppermute | solution.py:18
  91.4 3.3 %collective-permute-start.17 = (bf16[4,2,64,1024]{3,2,1,0:T(8,128)(2,1)}, bf16[4,2,64,1024]{3,2,1,0:T(8,128)(2,1)}, u32[]{:S(2)}, u32[]{:S(2)}) collective-permute-start(bf16[4,2,64,1024]{3,2,1,0:T(8,128)(2,1)} %fusion.14), channel_id=1, source_target_pairs={{0,1},{1,0},{2,3},{3,2},{4,5},{5,4},{6,7},{7,6},{8,9},{9,8},{10,11... | collective-permute-start | bytes 3145736 | tf_op jit(solution)/shard_map/ppermute | solution.py:18
  95.7 7.7 %collective-permute-done.5 = bf16[2,64,896]{2,1,0:T(8,128)(2,1)S(1)} collective-permute-done((bf16[2,64,896]{2,1,0:T(8,128)(2,1)S(1)}, bf16[2,64,896]{2,1,0:T(8,128)(2,1)S(1)}, u32[]{:S(2)}, u32[]{:S(2)}) %collective-permute-start.5) | collective-permute-done | bytes 229408 | tf_op jit(solution)/shard_map/ppermute | solution.py:18
  104.8 2.5 %collective-permute-done.8 = bf16[64,896]{1,0:T(8,128)(2,1)S(1)} collective-permute-done((bf16[64,896]{1,0:T(8,128)(2,1)S(1)}, bf16[64,896]{1,0:T(8,128)(2,1)S(1)}, u32[]{:S(2)}, u32[]{:S(2)}) %collective-permute-start.8) | collective-permute-done | bytes 114720 | tf_op jit(solution)/shard_map/ppermute | solution.py:18
  109.0 3.2 %collective-permute-start.9 = (bf16[2,64,896]{2,1,0:T(8,128)(2,1)}, bf16[2,64,896]{2,1,0:T(8,128)(2,1)}, u32[]{:S(2)}, u32[]{:S(2)}) collective-permute-start(bf16[2,64,896]{2,1,0:T(8,128)(2,1)} %get-tuple-element.45), channel_id=1, source_target_pairs={{0,192},{64,0},{128,64},{192,128},{1,193},{65,1},{129,65},{193,129... | collective-permute-start | bytes 688136 | tf_op jit(solution)/shard_map/ppermute | solution.py:18
  112.2 2.6 %collective-permute-done.10 = bf16[2,64,896]{2,1,0:T(8,128)(2,1)} collective-permute-done((bf16[2,64,896]{2,1,0:T(8,128)(2,1)}, bf16[2,64,896]{2,1,0:T(8,128)(2,1)}, u32[]{:S(2)}, u32[]{:S(2)}) %collective-permute-start.10) | collective-permute-done | bytes 229408 | tf_op jit(solution)/shard_map/ppermute | solution.py:18
  114.8 7.5 %collective-permute-done.9 = bf16[2,64,896]{2,1,0:T(8,128)(2,1)} collective-permute-done((bf16[2,64,896]{2,1,0:T(8,128)(2,1)}, bf16[2,64,896]{2,1,0:T(8,128)(2,1)}, u32[]{:S(2)}, u32[]{:S(2)}) %collective-permute-start.9) | collective-permute-done | bytes 229408 | tf_op jit(solution)/shard_map/ppermute | solution.py:18
  122.3 3.3 %convert_add_fusion = f32[4,2,64,1024]{3,2,1,0:T(8,128)S(1)} fusion(bf16[4,2,64,1024]{3,2,1,0:T(8,128)(2,1)} %collective-permute-done.17, bf16[896,1024]{1,0:T(8,128)(2,1)} %param.11, bf16[1,2,64,896]{3,2,1,0:T(8,128)(2,1)} %bitcast.24, bf16[1,2,64,896]{3,2,1,0:T(8,128)(2,1)} %bitcast.23, bf16[1,2,64,896]{3,2,1,0:T(8,128)(2,1)} %bitcast.22, ...), kind=kOutput, calls=%fused_computation.1 | convolution fusion | flops 941948928 | bytes 5898240 | tf_op jit(solution)/shard_map/dot_general | solution.py:42
  125.7 5.7 %collective-permute-start.23 = (bf16[8,8,1024]{2,1,0:T(8,128)(2,1)S(1)}, bf16[8,8,1024]{2,1,0:T(8,128)(2,1)S(1)}, u32[]{:S(2)}, u32[]{:S(2)}) collective-permute-start(bf16[8,8,1024]{2,1,0:T(8,128)(2,1)S(1)} %get-tuple-element.20), channel_id=1, source_target_pairs={{0,28},{4,0},{8,4},{12,8},{16,12},{20,16},{24,20},{28,24},{1,29},{... | collective-permute-start | bytes 393224 | tf_op jit(solution)/shard_map/ppermute | solution.py:18
  131.4 2.8 %collective-permute-start.18 = (bf16[8,8,1024]{2,1,0:T(8,128)(2,1)S(1)}, bf16[8,8,1024]{2,1,0:T(8,128)(2,1)S(1)}, u32[]{:S(2)}, u32[]{:S(2)}) collective-permute-start(bf16[8,8,1024]{2,1,0:T(8,128)(2,1)S(1)} %get-tuple-element.17), channel_id=1, source_target_pairs={{0,16},{4,20},{8,24},{12,28},{16,0},{20,4},{24,8},{28,12},{1,17},{... | collective-permute-start | bytes 393224 | tf_op jit(solution)/shard_map/ppermute | solution.py:18
  135.7 3.3 %collective-permute-done.21 = bf16[8,8,1024]{2,1,0:T(8,128)(2,1)S(1)} collective-permute-done((bf16[8,8,1024]{2,1,0:T(8,128)(2,1)S(1)}, bf16[8,8,1024]{2,1,0:T(8,128)(2,1)S(1)}, u32[]{:S(2)}, u32[]{:S(2)}) %collective-permute-start.21) | collective-permute-done | bytes 131104 | tf_op jit(solution)/shard_map/ppermute | solution.py:18
  139.3 3.6 %collective-permute-start.24 = (bf16[8,8,1024]{2,1,0:T(8,128)(2,1)S(1)}, bf16[8,8,1024]{2,1,0:T(8,128)(2,1)S(1)}, u32[]{:S(2)}, u32[]{:S(2)}) collective-permute-start(bf16[8,8,1024]{2,1,0:T(8,128)(2,1)S(1)} %get-tuple-element.23), channel_id=1, source_target_pairs={{0,24},{4,28},{8,0},{12,4},{16,8},{20,12},{24,16},{28,20},{1,25},{... | collective-permute-start | bytes 393224 | tf_op jit(solution)/shard_map/ppermute | solution.py:18
  143.5 3.3 %collective-permute-done.19 = bf16[8,8,1024]{2,1,0:T(8,128)(2,1)S(1)} collective-permute-done((bf16[8,8,1024]{2,1,0:T(8,128)(2,1)S(1)}, bf16[8,8,1024]{2,1,0:T(8,128)(2,1)S(1)}, u32[]{:S(2)}, u32[]{:S(2)}) %collective-permute-start.19) | collective-permute-done | bytes 131104 | tf_op jit(solution)/shard_map/ppermute | solution.py:18
  148.8 2.7 %collective-permute-start.25 = (bf16[8,8,1024]{2,1,0:T(8,128)(2,1)S(1)}, bf16[8,8,1024]{2,1,0:T(8,128)(2,1)S(1)}, u32[]{:S(2)}, u32[]{:S(2)}) collective-permute-start(bf16[8,8,1024]{2,1,0:T(8,128)(2,1)S(1)} %fusion.32), channel_id=1, source_target_pairs={{0,2},{2,0},{1,3},{3,1},{4,6},{6,4},{5,7},{7,5},{8,10},{10,8},{9,1... | collective-permute-start | bytes 393224 | tf_op jit(solution)/shard_map/ppermute | solution.py:18
  151.5 2.7 %collective-permute-done.25 = bf16[8,8,1024]{2,1,0:T(8,128)(2,1)S(1)} collective-permute-done((bf16[8,8,1024]{2,1,0:T(8,128)(2,1)S(1)}, bf16[8,8,1024]{2,1,0:T(8,128)(2,1)S(1)}, u32[]{:S(2)}, u32[]{:S(2)}) %collective-permute-start.25) | collective-permute-done | bytes 131104 | tf_op jit(solution)/shard_map/ppermute | solution.py:18
  155.0 4.7 %all-to-all-start.1 = ((f32[8,8,8]{2,1,0:T(8,128)}), f32[8,8,8]{2,1,0:T(8,128)S(1)}, u32[]{:S(2)}, u32[]{:S(2)}) async-start(f32[8,8,8]{2,1,0:T(8,128)} %broadcast_in_dim.6), calls=%async_computation.1 | async-start | bytes 65536 | tf_op jit(solution)/shard_map/all_to_all | solution.py:116
  159.7 5.1 %all-to-all-done.1 = f32[8,8,8]{2,1,0:T(8,128)S(1)} async-done(((f32[8,8,8]{2,1,0:T(8,128)}), f32[8,8,8]{2,1,0:T(8,128)S(1)}, u32[]{:S(2)}, u32[]{:S(2)}) %all-to-all-start.1) | async-done | bytes 2080 | tf_op jit(solution)/shard_map/all_to_all | solution.py:116
  165.1 2.4 %collective-permute-start.27 = (bf16[8,1024]{1,0:T(8,128)(2,1)S(1)}, bf16[8,1024]{1,0:T(8,128)(2,1)S(1)}, u32[]{:S(2)}, u32[]{:S(2)}) collective-permute-start(bf16[8,1024]{1,0:T(8,128)(2,1)S(1)} %multiply_convert_fusion.2), channel_id=1, source_target_pairs={{0,4},{4,8},{8,12},{12,16},{16,20},{20,24},{24,28},{28,0},{1,5},{5... | collective-permute-start | bytes 49160 | tf_op jit(solution)/shard_map/ppermute | solution.py:18
  175.0 3.9 %collective-permute-done.29 = bf16[3,8,1024]{2,1,0:T(8,128)(2,1)S(1)} collective-permute-done((bf16[3,8,1024]{2,1,0:T(8,128)(2,1)S(1)}, bf16[3,8,1024]{2,1,0:T(8,128)(2,1)S(1)}, u32[]{:S(2)}, u32[]{:S(2)}) %collective-permute-start.29) | collective-permute-done | bytes 49184 | tf_op jit(solution)/shard_map/ppermute | solution.py:18
  179.0 7.0 %collective-permute-start.30 = (bf16[64,1024]{1,0:T(8,128)(2,1)S(1)}, bf16[64,1024]{1,0:T(8,128)(2,1)S(1)}, u32[]{:S(2)}, u32[]{:S(2)}) collective-permute-start(bf16[64,1024]{1,0:T(8,128)(2,1)S(1)} %dynamic-slice_bitcast_fusion), channel_id=1, source_target_pairs={{0,1},{1,0},{2,3},{3,2},{4,5},{5,4},{6,7},{7,6},{8,9},{9,8},{10,11... | collective-permute-start | bytes 393224 | tf_op jit(solution)/shard_map/ppermute | solution.py:18
  187.0 3.5 %convolution_convert_fusion = bf16[128,2688]{1,0:T(8,128)(2,1)S(1)} fusion(bf16[1024,2688]{1,0:T(8,128)(2,1)} %param.13, bf16[64,1024]{1,0:T(8,128)(2,1)S(1)} %get-tuple-element.43, bf16[64,1024]{1,0:T(8,128)(2,1)S(1)} %get-tuple-element.42), kind=kOutput, calls=%fused_computation | convolution fusion | flops 705511424 | bytes 6455296 | tf_op jit(solution)/shard_map/dot_general | solution.py:137
  190.5 13.5 %all_to_all.21 = bf16[8,16,2688]{2,1,0:T(8,128)(2,1)S(1)} all-to-all(bf16[8,16,2688]{2,1,0:T(8,128)(2,1)S(1)} %bitcast.181), channel_id=1, replica_groups=mesh['x'=4,'y'=2,'z'=8,'w'=2,'c'=2] {'x','y'}, dimensions={0} | all-to-all | bytes 1376256 | tf_op jit(solution)/shard_map/all_to_all | solution.py:139
  204.5 17.5 %all_to_all.22 = f32[32,1,16]{2,1,0:T(1,128)S(1)} all-to-all(f32[32,1,16]{2,1,0:T(1,128)S(1)} %broadcast_in_dim.8), channel_id=1, replica_groups=mesh['x'=4,'y'=2,'z'=8,'w'=2,'c'=2] {'z','w','c'}, dimensions={0} | all-to-all | bytes 4096 | tf_op jit(solution)/shard_map/all_to_all | solution.py:144
  (133 shorter events, 47.7 us)
Async XLA Ops:
  22.9 8.7 %collective-permute-start.1 = (bf16[8,64,1024]{2,1,0:T(8,128)(2,1)S(1)}, bf16[8,64,1024]{2,1,0:T(8,128)(2,1)}, u32[]{:S(2)}, u32[]{:S(2)}) collective-permute-start(bf16[8,64,1024]{2,1,0:T(8,128)(2,1)S(1)} %all_to_all.20), channel_id=1, source_target_pairs={{0,1},{1,0},{2,3},{3,2},{4,5},{5,4},{6,7},{7,6},{8,9},{9,8},{10,11... | collective-permute-start | bytes 3145736 | tf_op jit(solution)/shard_map/ppermute | solution.py:18
  30.5 22.2 %collective-permute-start = (bf16[2,4,64,896]{3,2,1,0:T(8,128)(2,1)}, bf16[2,4,64,896]{3,2,1,0:T(8,128)(2,1)}, u32[]{:S(2)}, u32[]{:S(2)}) collective-permute-start(bf16[2,4,64,896]{3,2,1,0:T(8,128)(2,1)} %pad_maximum_fusion), channel_id=1, source_target_pairs={{0,32},{32,0},{1,33},{33,1},{2,34},{34,2},{3,35},{35,3},{4,36},{36... | collective-permute-start | bytes 2752520 | tf_op jit(solution)/shard_map/ppermute | solution.py:18
  38.7 14.0 %collective-permute-start.2 = (bf16[2,2,64,896]{3,2,1,0:T(8,128)(2,1)}, bf16[2,2,64,896]{3,2,1,0:T(8,128)(2,1)}, u32[]{:S(2)}, u32[]{:S(2)}) collective-permute-start(bf16[2,2,64,896]{3,2,1,0:T(8,128)(2,1)} %pad_maximum_fusion.2), channel_id=1, source_target_pairs={{0,128},{64,192},{128,0},{192,64},{1,129},{65,193},{129,1},{193,65... | collective-permute-start | bytes 1376264 | tf_op jit(solution)/shard_map/ppermute | solution.py:18
  40.8 22.1 %collective-permute-start.3 = (bf16[2,2,64,896]{3,2,1,0:T(8,128)(2,1)}, bf16[2,2,64,896]{3,2,1,0:T(8,128)(2,1)}, u32[]{:S(2)}, u32[]{:S(2)}) collective-permute-start(bf16[2,2,64,896]{3,2,1,0:T(8,128)(2,1)} %pad_maximum_fusion.3), channel_id=1, source_target_pairs={{0,64},{64,128},{128,192},{192,0},{1,65},{65,129},{129,193},{193,1... | collective-permute-start | bytes 1376264 | tf_op jit(solution)/shard_map/ppermute | solution.py:18
  41.8 21.1 %collective-permute-start.4 = (bf16[2,2,64,896]{3,2,1,0:T(8,128)(2,1)}, bf16[2,2,64,896]{3,2,1,0:T(8,128)(2,1)}, u32[]{:S(2)}, u32[]{:S(2)}) collective-permute-start(bf16[2,2,64,896]{3,2,1,0:T(8,128)(2,1)} %pad_maximum_fusion.4), channel_id=1, source_target_pairs={{0,192},{64,0},{128,64},{192,128},{1,193},{65,1},{129,65},{193,129... | collective-permute-start | bytes 1376264 | tf_op jit(solution)/shard_map/ppermute | solution.py:18
  64.8 6.8 %collective-permute-start.12 = (bf16[2,64,896]{2,1,0:T(8,128)(2,1)S(1)}, bf16[2,64,896]{2,1,0:T(8,128)(2,1)S(1)}, u32[]{:S(2)}, u32[]{:S(2)}) collective-permute-start(bf16[2,64,896]{2,1,0:T(8,128)(2,1)S(1)} %pad_maximum_fusion.10), channel_id=1, source_target_pairs={{0,32},{32,0},{1,33},{33,1},{2,34},{34,2},{3,35},{35,3},{4,36},{36... | collective-permute-start | bytes 688136 | tf_op jit(solution)/shard_map/ppermute | solution.py:18
  71.7 6.8 %collective-permute-start.15 = (bf16[64,896]{1,0:T(8,128)(2,1)S(1)}, bf16[64,896]{1,0:T(8,128)(2,1)S(1)}, u32[]{:S(2)}, u32[]{:S(2)}) collective-permute-start(bf16[64,896]{1,0:T(8,128)(2,1)S(1)} %fusion.33), channel_id=1, source_target_pairs={{0,64},{64,128},{128,192},{192,0},{1,65},{65,129},{129,193},{193,1... | collective-permute-start | bytes 344072 | tf_op jit(solution)/shard_map/ppermute | solution.py:18
  72.0 6.5 %collective-permute-start.14 = (bf16[64,896]{1,0:T(8,128)(2,1)S(1)}, bf16[64,896]{1,0:T(8,128)(2,1)S(1)}, u32[]{:S(2)}, u32[]{:S(2)}) collective-permute-start(bf16[64,896]{1,0:T(8,128)(2,1)S(1)} %fusion.33), channel_id=1, source_target_pairs={{0,128},{64,192},{128,0},{192,64},{1,129},{65,193},{129,1},{193,65... | collective-permute-start | bytes 344072 | tf_op jit(solution)/shard_map/ppermute | solution.py:18
  73.8 5.4 %collective-permute-start.13 = (bf16[64,896]{1,0:T(8,128)(2,1)S(1)}, bf16[64,896]{1,0:T(8,128)(2,1)S(1)}, u32[]{:S(2)}, u32[]{:S(2)}) collective-permute-start(bf16[64,896]{1,0:T(8,128)(2,1)S(1)} %fusion.33), channel_id=1, source_target_pairs={{0,192},{64,0},{128,64},{192,128},{1,193},{65,1},{129,65},{193,129... | collective-permute-start | bytes 344072 | tf_op jit(solution)/shard_map/ppermute | solution.py:18
  79.2 9.9 %collective-permute-start.16 = (bf16[4,64,896]{2,1,0:T(8,128)(2,1)S(1)}, bf16[4,64,896]{2,1,0:T(8,128)(2,1)S(1)}, u32[]{:S(2)}, u32[]{:S(2)}) collective-permute-start(bf16[4,64,896]{2,1,0:T(8,128)(2,1)S(1)} %get-tuple-element.41), channel_id=1, source_target_pairs={{0,32},{32,0},{1,33},{33,1},{2,34},{34,2},{3,35},{35,3},{4,36},{36... | collective-permute-start | bytes 1376264 | tf_op jit(solution)/shard_map/ppermute | solution.py:18
  80.6 15.1 %collective-permute-start.6 = (bf16[2,64,896]{2,1,0:T(8,128)(2,1)S(1)}, bf16[2,64,896]{2,1,0:T(8,128)(2,1)S(1)}, u32[]{:S(2)}, u32[]{:S(2)}) collective-permute-start(bf16[2,64,896]{2,1,0:T(8,128)(2,1)S(1)} %pad_maximum_fusion.7), channel_id=1, source_target_pairs={{0,64},{64,128},{128,192},{192,0},{1,65},{65,129},{129,193},{193,1... | collective-permute-start | bytes 688136 | tf_op jit(solution)/shard_map/ppermute | solution.py:18
  81.8 14.0 %collective-permute-start.7 = (bf16[2,64,896]{2,1,0:T(8,128)(2,1)S(1)}, bf16[2,64,896]{2,1,0:T(8,128)(2,1)S(1)}, u32[]{:S(2)}, u32[]{:S(2)}) collective-permute-start(bf16[2,64,896]{2,1,0:T(8,128)(2,1)S(1)} %pad_maximum_fusion.8), channel_id=1, source_target_pairs={{0,192},{64,0},{128,64},{192,128},{1,193},{65,1},{129,65},{193,129... | collective-permute-start | bytes 688136 | tf_op jit(solution)/shard_map/ppermute | solution.py:18
  91.4 30.9 %collective-permute-start.17 = (bf16[4,2,64,1024]{3,2,1,0:T(8,128)(2,1)}, bf16[4,2,64,1024]{3,2,1,0:T(8,128)(2,1)}, u32[]{:S(2)}, u32[]{:S(2)}) collective-permute-start(bf16[4,2,64,1024]{3,2,1,0:T(8,128)(2,1)} %fusion.14), channel_id=1, source_target_pairs={{0,1},{1,0},{2,3},{3,2},{4,5},{5,4},{6,7},{7,6},{8,9},{9,8},{10,11... | collective-permute-start | bytes 3145736 | tf_op jit(solution)/shard_map/ppermute | solution.py:18
  94.7 8.7 %collective-permute-start.5 = (bf16[2,64,896]{2,1,0:T(8,128)(2,1)S(1)}, bf16[2,64,896]{2,1,0:T(8,128)(2,1)S(1)}, u32[]{:S(2)}, u32[]{:S(2)}) collective-permute-start(bf16[2,64,896]{2,1,0:T(8,128)(2,1)S(1)} %pad_maximum_fusion.6), channel_id=1, source_target_pairs={{0,128},{64,192},{128,0},{192,64},{1,129},{65,193},{129,1},{193,65... | collective-permute-start | bytes 688136 | tf_op jit(solution)/shard_map/ppermute | solution.py:18
  103.6 3.7 %collective-permute-start.8 = (bf16[64,896]{1,0:T(8,128)(2,1)S(1)}, bf16[64,896]{1,0:T(8,128)(2,1)S(1)}, u32[]{:S(2)}, u32[]{:S(2)}) collective-permute-start(bf16[64,896]{1,0:T(8,128)(2,1)S(1)} %fusion.37), channel_id=1, source_target_pairs={{0,32},{32,0},{1,33},{33,1},{2,34},{34,2},{3,35},{35,3},{4,36},{36... | collective-permute-start | bytes 344072 | tf_op jit(solution)/shard_map/ppermute | solution.py:18
  108.1 6.7 %collective-permute-start.10 = (bf16[2,64,896]{2,1,0:T(8,128)(2,1)}, bf16[2,64,896]{2,1,0:T(8,128)(2,1)}, u32[]{:S(2)}, u32[]{:S(2)}) collective-permute-start(bf16[2,64,896]{2,1,0:T(8,128)(2,1)} %get-tuple-element.45), channel_id=1, source_target_pairs={{0,128},{64,192},{128,0},{192,64},{1,129},{65,193},{129,1},{193,65... | collective-permute-start | bytes 688136 | tf_op jit(solution)/shard_map/ppermute | solution.py:18
  109.0 13.3 %collective-permute-start.9 = (bf16[2,64,896]{2,1,0:T(8,128)(2,1)}, bf16[2,64,896]{2,1,0:T(8,128)(2,1)}, u32[]{:S(2)}, u32[]{:S(2)}) collective-permute-start(bf16[2,64,896]{2,1,0:T(8,128)(2,1)} %get-tuple-element.45), channel_id=1, source_target_pairs={{0,192},{64,0},{128,64},{192,128},{1,193},{65,1},{129,65},{193,129... | collective-permute-start | bytes 688136 | tf_op jit(solution)/shard_map/ppermute | solution.py:18
  112.2 10.1 %collective-permute-start.11 = (bf16[2,64,896]{2,1,0:T(8,128)(2,1)}, bf16[2,64,896]{2,1,0:T(8,128)(2,1)}, u32[]{:S(2)}, u32[]{:S(2)}) collective-permute-start(bf16[2,64,896]{2,1,0:T(8,128)(2,1)} %get-tuple-element.45), channel_id=1, source_target_pairs={{0,64},{64,128},{128,192},{192,0},{1,65},{65,129},{129,193},{193,1... | collective-permute-start | bytes 688136 | tf_op jit(solution)/shard_map/ppermute | solution.py:18
  125.7 9.9 %collective-permute-start.23 = (bf16[8,8,1024]{2,1,0:T(8,128)(2,1)S(1)}, bf16[8,8,1024]{2,1,0:T(8,128)(2,1)S(1)}, u32[]{:S(2)}, u32[]{:S(2)}) collective-permute-start(bf16[8,8,1024]{2,1,0:T(8,128)(2,1)S(1)} %get-tuple-element.20), channel_id=1, source_target_pairs={{0,28},{4,0},{8,4},{12,8},{16,12},{20,16},{24,20},{28,24},{1,29},{... | collective-permute-start | bytes 393224 | tf_op jit(solution)/shard_map/ppermute | solution.py:18
  131.4 7.6 %collective-permute-start.21 = (bf16[8,8,1024]{2,1,0:T(8,128)(2,1)S(1)}, bf16[8,8,1024]{2,1,0:T(8,128)(2,1)S(1)}, u32[]{:S(2)}, u32[]{:S(2)}) collective-permute-start(bf16[8,8,1024]{2,1,0:T(8,128)(2,1)S(1)} %get-tuple-element.21), channel_id=1, source_target_pairs={{0,4},{4,8},{8,12},{12,16},{16,20},{20,24},{24,28},{28,0},{1,5},{5... | collective-permute-start | bytes 393224 | tf_op jit(solution)/shard_map/ppermute | solution.py:18
  131.4 11.6 %collective-permute-start.18 = (bf16[8,8,1024]{2,1,0:T(8,128)(2,1)S(1)}, bf16[8,8,1024]{2,1,0:T(8,128)(2,1)S(1)}, u32[]{:S(2)}, u32[]{:S(2)}) collective-permute-start(bf16[8,8,1024]{2,1,0:T(8,128)(2,1)S(1)} %get-tuple-element.17), channel_id=1, source_target_pairs={{0,16},{4,20},{8,24},{12,28},{16,0},{20,4},{24,8},{28,12},{1,17},{... | collective-permute-start | bytes 393224 | tf_op jit(solution)/shard_map/ppermute | solution.py:18
  134.2 9.3 %collective-permute-start.20 = (bf16[8,8,1024]{2,1,0:T(8,128)(2,1)S(1)}, bf16[8,8,1024]{2,1,0:T(8,128)(2,1)S(1)}, u32[]{:S(2)}, u32[]{:S(2)}) collective-permute-start(bf16[8,8,1024]{2,1,0:T(8,128)(2,1)S(1)} %get-tuple-element.18), channel_id=1, source_target_pairs={{0,28},{4,0},{8,4},{12,8},{16,12},{20,16},{24,20},{28,24},{1,29},{... | collective-permute-start | bytes 393224 | tf_op jit(solution)/shard_map/ppermute | solution.py:18
  135.5 11.3 %collective-permute-start.19 = (bf16[8,8,1024]{2,1,0:T(8,128)(2,1)S(1)}, bf16[8,8,1024]{2,1,0:T(8,128)(2,1)S(1)}, u32[]{:S(2)}, u32[]{:S(2)}) collective-permute-start(bf16[8,8,1024]{2,1,0:T(8,128)(2,1)S(1)} %get-tuple-element.19), channel_id=1, source_target_pairs={{0,4},{4,8},{8,12},{12,16},{16,20},{20,24},{24,28},{28,0},{1,5},{5... | collective-permute-start | bytes 393224 | tf_op jit(solution)/shard_map/ppermute | solution.py:18
  139.0 8.0 %collective-permute-start.22 = (bf16[8,8,1024]{2,1,0:T(8,128)(2,1)S(1)}, bf16[8,8,1024]{2,1,0:T(8,128)(2,1)S(1)}, u32[]{:S(2)}, u32[]{:S(2)}) collective-permute-start(bf16[8,8,1024]{2,1,0:T(8,128)(2,1)S(1)} %get-tuple-element.22), channel_id=1, source_target_pairs={{0,8},{4,12},{8,16},{12,20},{16,24},{20,28},{24,0},{28,4},{1,9},{5... | collective-permute-start | bytes 393224 | tf_op jit(solution)/shard_map/ppermute | solution.py:18
  139.3 9.3 %collective-permute-start.24 = (bf16[8,8,1024]{2,1,0:T(8,128)(2,1)S(1)}, bf16[8,8,1024]{2,1,0:T(8,128)(2,1)S(1)}, u32[]{:S(2)}, u32[]{:S(2)}) collective-permute-start(bf16[8,8,1024]{2,1,0:T(8,128)(2,1)S(1)} %get-tuple-element.23), channel_id=1, source_target_pairs={{0,24},{4,28},{8,0},{12,4},{16,8},{20,12},{24,16},{28,20},{1,25},{... | collective-permute-start | bytes 393224 | tf_op jit(solution)/shard_map/ppermute | solution.py:18
  148.8 5.4 %collective-permute-start.25 = (bf16[8,8,1024]{2,1,0:T(8,128)(2,1)S(1)}, bf16[8,8,1024]{2,1,0:T(8,128)(2,1)S(1)}, u32[]{:S(2)}, u32[]{:S(2)}) collective-permute-start(bf16[8,8,1024]{2,1,0:T(8,128)(2,1)S(1)} %fusion.32), channel_id=1, source_target_pairs={{0,2},{2,0},{1,3},{3,1},{4,6},{6,4},{5,7},{7,5},{8,10},{10,8},{9,1... | collective-permute-start | bytes 393224 | tf_op jit(solution)/shard_map/ppermute | solution.py:18
  155.0 9.8 %all-to-all-start.1 = ((f32[8,8,8]{2,1,0:T(8,128)}), f32[8,8,8]{2,1,0:T(8,128)S(1)}, u32[]{:S(2)}, u32[]{:S(2)}) async-start(f32[8,8,8]{2,1,0:T(8,128)} %broadcast_in_dim.6), calls=%async_computation.1 | async-start | bytes 65536 | tf_op jit(solution)/shard_map/all_to_all | solution.py:116
  165.1 5.4 %collective-permute-start.27 = (bf16[8,1024]{1,0:T(8,128)(2,1)S(1)}, bf16[8,1024]{1,0:T(8,128)(2,1)S(1)}, u32[]{:S(2)}, u32[]{:S(2)}) collective-permute-start(bf16[8,1024]{1,0:T(8,128)(2,1)S(1)} %multiply_convert_fusion.2), channel_id=1, source_target_pairs={{0,4},{4,8},{8,12},{12,16},{16,20},{20,24},{24,28},{28,0},{1,5},{5... | collective-permute-start | bytes 49160 | tf_op jit(solution)/shard_map/ppermute | solution.py:18
  167.5 5.4 %collective-permute-start.26 = (bf16[8,1024]{1,0:T(8,128)(2,1)S(1)}, bf16[8,1024]{1,0:T(8,128)(2,1)S(1)}, u32[]{:S(2)}, u32[]{:S(2)}) collective-permute-start(bf16[8,1024]{1,0:T(8,128)(2,1)S(1)} %multiply_convert_fusion.2), channel_id=1, source_target_pairs={{0,28},{4,0},{8,4},{12,8},{16,12},{20,16},{24,20},{28,24},{1,29},{... | collective-permute-start | bytes 49160 | tf_op jit(solution)/shard_map/ppermute | solution.py:18
  170.5 4.6 %collective-permute-start.28 = (bf16[2,8,1024]{2,1,0:T(8,128)(2,1)S(1)}, bf16[2,8,1024]{2,1,0:T(8,128)(2,1)S(1)}, u32[]{:S(2)}, u32[]{:S(2)}) collective-permute-start(bf16[2,8,1024]{2,1,0:T(8,128)(2,1)S(1)} %pad_maximum_fusion.12), channel_id=1, source_target_pairs={{0,20},{4,24},{8,28},{12,0},{16,4},{20,8},{24,12},{28,16},{1,21},{... | collective-permute-start | bytes 98312 | tf_op jit(solution)/shard_map/ppermute | solution.py:18
  172.9 6.0 %collective-permute-start.29 = (bf16[3,8,1024]{2,1,0:T(8,128)(2,1)S(1)}, bf16[3,8,1024]{2,1,0:T(8,128)(2,1)S(1)}, u32[]{:S(2)}, u32[]{:S(2)}) collective-permute-start(bf16[3,8,1024]{2,1,0:T(8,128)(2,1)S(1)} %pad_maximum_fusion.11), channel_id=1, source_target_pairs={{0,12},{4,16},{8,20},{12,24},{16,28},{20,0},{24,4},{28,8},{1,13},{... | collective-permute-start | bytes 147464 | tf_op jit(solution)/shard_map/ppermute | solution.py:18
  179.0 8.0 %collective-permute-start.30 = (bf16[64,1024]{1,0:T(8,128)(2,1)S(1)}, bf16[64,1024]{1,0:T(8,128)(2,1)S(1)}, u32[]{:S(2)}, u32[]{:S(2)}) collective-permute-start(bf16[64,1024]{1,0:T(8,128)(2,1)S(1)} %dynamic-slice_bitcast_fusion), channel_id=1, source_target_pairs={{0,1},{1,0},{2,3},{3,2},{4,5},{5,4},{6,7},{7,6},{8,9},{9,8},{10,11... | collective-permute-start | bytes 393224 | tf_op jit(solution)/shard_map/ppermute | solution.py:18
  (13 other events, 150.0 us)
where the time goes:
time: 223 us
  waiting for transfers between devices  76.9 us (34%)
  starting transfers between devices  60.6 us (27%)
  blocking collectives  51 us (23%)
  matrix products  18.8 us (8%)
  other arithmetic  10.7 us (5%)
  local copies, waits for them, and re-layouts  4.54 us (2%)
    ppermute x31, waiting for transfers between devices, shifted(): lax.ppermute(array, axis, [(i, (i + step) % size) for i in range(size)])  71.8 us
    ppermute x31, starting transfers between devices, shifted(): lax.ppermute(array, axis, [(i, (i + step) % size) for i in range(size)])  55.9 us
    all_to_all x1, blocking collectives, tokens_for_block(): own = lax.all_to_all(blocks, PROMPT, 0, 0, tiled=True)  20 us
    all_to_all x1, blocking collectives, step(): lax.all_to_all(jnp.broadcast_to(part_lse[None, None], (shards, 1, part_ls...  17.5 us
    dot_general x6, matrix products, products(): jnp.dot(flat, weight, preferred_element_type=F32)  15.3 us
    all_to_all x1, blocking collectives, step(): tiles = lax.all_to_all(tiles, PROMPT, 0, 0, tiled=True)  13.5 us
    all_to_all x1, waiting for transfers between devices, step(): lax.all_to_all(jnp.broadcast_to(by_variant[None], (NX * NY, *by_variant.s...  5.07 us
    all_to_all x1, starting transfers between devices, step(): lax.all_to_all(jnp.broadcast_to(by_variant[None], (NX * NY, *by_variant.s...  4.7 us
  transfers between devices with their start and end apart: 32, of which 21 were waited for; matrix products, arithmetic and copies ran while one was open for 9% of the time, Pallas kernels for 0%

commit v1 on v0

v1 whole, which is shorter than its diff:
```python
import jax
import jax.numpy as jnp
from jax import lax
from jax.sharding import Mesh
from jax.sharding import PartitionSpec as P


D = 8192
EPS = 1e-05
NX, NY, NZ, NW, NC = 4, 2, 8, 2, 2
AXES = ("x", "y", "z", "w", "c")
PROMPT = ("x", "y")
TENSOR = ("z", "w", "c")
BF, F32 = jnp.bfloat16, jnp.float32


def shifted(array, axis, size, step):
    return lax.ppermute(array, axis, [(i, (i + step) % size) for i in range(size)])


def paired(array, axis, size, bit):
    return lax.ppermute(array, axis, [(i, i ^ bit) for i in range(size)])


def flipped_if(bit, array, axis):
    return jnp.where(bit == 0, array, jnp.flip(array, axis))


def wide(array):
    return array.astype(F32)


def tokens_for_block(tokens, x, y, c):
    half = tokens.shape[0] // NC
    share = D // (NX * NY)
    mine = lax.dynamic_slice_in_dim(tokens, c * half, half, 0)
    blocks = mine.reshape(half, NX * NY, share).transpose(1, 0, 2)
    own = lax.all_to_all(blocks, PROMPT, 0, 0, tiled=True)
    own = own.reshape(2, 2, NY, half, share)
    for axis, bit in enumerate((x // 2, x % 2, y)):
        own = flipped_if(bit, own, axis)
    own = lax.optimization_barrier(own.reshape(NX, NY, half, share))
    return own, paired(own, "c", NC, 1)


def at(array, index, axis):
    return lax.dynamic_index_in_dim(array, index, axis, keepdims=False)


def products(rows, weights):
    flat = rows.reshape(-1, rows.shape[-1])
    outs = [jnp.dot(flat, weight, preferred_element_type=F32) for weight in weights]
    return [out.reshape(*rows.shape[:-1], -1) for out in outs]


def joined(pair):
    return jnp.stack([part.astype(BF) for part in pair])


def step(tokens, gate_weight, up_weight, down_weight, norm_gain, unembed, guidance, logit_bias):
    x, y, z, _, c = (lax.axis_index(axis) for axis in AXES)
    tokens = tokens[0]
    own, other = tokens_for_block(tokens, x, y, c)
    both = (gate_weight, up_weight)

    pa = products(own, both)
    got_a = [paired(joined([p[d] for p in pa]), "x", NX, d) for d in TURNS]
    pb = products(other, both)
    swap_b = paired(joined([p[:, 1] for p in pb]), "y", NY, 1)
    got_a, swap_b = lax.optimization_barrier((got_a, swap_b))
    sum_a = [p[0] + sum(wide(got[i]) for got in got_a) for i, p in enumerate(pa)]
    swap_a = paired(joined([p[1] for p in sum_a]), "y", NY, 1)
    sum_b = [p[:, 0] + wide(got) for p, got in zip(pb, swap_b)]
    got_b = [paired(joined([p[d] for p in sum_b]), "x", NX, d) for d in TURNS]
    gate_a, up_a = [p[0] + wide(got) for p, got in zip(sum_a, swap_a)]
    hidden_a = (jax.nn.silu(gate_a) * up_a).astype(BF)
    gate_b, up_b = [p[0] + sum(wide(got[i]) for got in got_b) for i, p in enumerate(sum_b)]
    hidden_b = (jax.nn.silu(gate_b) * up_b).astype(BF)

    line_a = [hidden_a] + [None] * (NX - 1)
    for d in TURNS:
        line_a[d] = paired(hidden_a, "x", NX, d)
    line_a = jnp.stack(line_a)
    all_a = jnp.stack([line_a, paired(line_a, "y", NY, 1)], axis=1)
    pair_b = jnp.stack([hidden_b, paired(hidden_b, "y", NY, 1)])
    all_b = [pair_b] + [None] * (NX - 1)
    for d in TURNS:
        all_b[d] = paired(pair_b, "x", NX, d)
    all_b = jnp.stack(all_b)

    (down_a,) = products(all_a, (down_weight,))
    passed = paired(down_a.astype(BF), "c", NC, 1)
    (down_b,) = products(all_b, (down_weight,))
    part = down_b + wide(passed)
    share = part.shape[-1]
    part = part.reshape(NX * NY, NZ, -1, share)

    def piece(k):
        return lax.dynamic_index_in_dim(part, (z + k) % NZ, 1, keepdims=False)

    def sent(block, step):
        return shifted(block.astype(BF), "z", NZ, step)

    far = sent(piece(4), 4)
    relay_up, relay_down = sent(piece(3), 1), sent(piece(5), -1)
    one_up, one_down = sent(piece(1), 1), sent(piece(7), -1)
    two_up = sent(piece(2) + wide(relay_up), 2)
    two_down = sent(piece(6) + wide(relay_down), -2)
    mine = piece(0) + sum(wide(got) for got in (far, one_up, one_down, two_up, two_down))
    mine = mine.astype(BF)
    branch = wide(mine) + wide(shifted(mine, "w", NW, 1))

    residual = at(other.reshape(NX * NY, NZ, -1, share), z, 1)
    state = wide(residual) + branch
    partial_square = jnp.sum(state * state, axis=2)
    offsets = jnp.arange(NX * NY)
    variant_at = offsets ^ (x * NY + y)
    placed_at = (variant_at[None, :] == offsets[:, None]).astype(F32)
    by_variant = jnp.sum(placed_at[:, :, None] * partial_square[None], axis=1)
    everyone = lax.all_to_all(
        jnp.broadcast_to(by_variant[None], (NX * NY, *by_variant.shape)),
        PROMPT, 0, 0, tiled=True,
    )
    square = everyone.sum(axis=0)
    scale = lax.rsqrt(square / D + EPS) * guidance[:, None]
    scale = jnp.sum(placed_at[:, :, None] * scale[:, None], axis=0)
    mixed = (jnp.sum(state * scale[:, :, None], axis=0) * norm_gain).astype(BF)

    ring = mixed
    for bit in (1, 2, 4):
        peer = paired(ring, "z", NZ, bit)
        low = (z & bit) == 0
        ring = jnp.concatenate([jnp.where(low, ring, peer), jnp.where(low, peer, ring)])
    peer = paired(ring, "c", NC, 1)
    first = jnp.where(c == 0, peer, ring)
    second = jnp.where(c == 0, ring, peer)
    rows = jnp.concatenate([first, second])

    product = jnp.dot(rows, unembed, preferred_element_type=F32).astype(BF)
    tiles = product.reshape(NX * NY, -1, product.shape[-1])
    tiles = lax.all_to_all(tiles, PROMPT, 0, 0, tiled=True)
    scores = jnp.sum(wide(tiles), axis=0) + logit_bias
    top = jnp.max(scores, axis=1, keepdims=True)
    part_lse = top[:, 0] + jnp.log(jnp.sum(jnp.exp(scores - top), axis=1))
    shards = NZ * NW * NC
    part_lse = lax.all_to_all(
        jnp.broadcast_to(part_lse[None, None], (shards, 1, part_lse.shape[0])),
        TENSOR, 0, 0, tiled=True,
    )
    lse = jax.nn.logsumexp(part_lse[:, 0], axis=0)
    return scores - lse[:, None]


TURNS = (2, 1, 3)


def solution(mesh):
    finer = Mesh(mesh.devices.reshape(NX, NY, NZ, NW, NC), AXES)
    placed = (
        P(PROMPT, None, None),
        P(PROMPT, TENSOR),
        P(PROMPT, TENSOR),
        P(TENSOR, PROMPT),
        P(PROMPT),
        P(PROMPT, TENSOR),
        P(),
        P(PROMPT, TENSOR),
    )
    return jax.shard_map(
        step, mesh=finer, in_specs=placed, out_specs=P(PROMPT, TENSOR), check_vma=False
    )
```

time: 223 us -> 212 us (0.951)
  blocking collectives: 51 us -> 41.4 us
  waiting for transfers between devices: 76.9 us -> 82.5 us
  matrix products: 18.8 us -> 13.8 us
  other arithmetic: 10.7 us -> 8.14 us
    ppermute x31 -> x8, waiting for transfers between devices: 71.8 us -> 12.8 us  [shifted(): lax.ppermute(array, axis, [(i, (i + step) % size) for i in range(size)])]
    ppermute x0 -> x22, waiting for transfers between devices: none -> 54.4 us  [paired(): return lax.ppermute(array, axis, [(i, i ^ bit) for i in range(size)])]
    ppermute x31 -> x8, starting transfers between devices: 55.9 us -> 16.5 us  [shifted(): lax.ppermute(array, axis, [(i, (i + step) % size) for i in range(size)])]
    ppermute x0 -> x22, starting transfers between devices: none -> 36.5 us  [paired(): return lax.ppermute(array, axis, [(i, i ^ bit) for i in range(size)])]
    all_to_all x1, blocking collectives: 20 us -> 9.36 us  [step(): lax.all_to_all(jnp.broadcast_to(by_variant[None], (NX * NY, *by_variant.s...]
    all_to_all x1, waiting for transfers between devices: 5.07 us -> 15.3 us  [tokens_for_block(): own = lax.all_to_all(blocks, PROMPT, 0, 0, tiled=True)]
    dot_general x6, matrix products: 15.3 us -> 10.3 us  [products(): jnp.dot(flat, weight, preferred_element_type=F32)]
    another operation x8, other arithmetic: 3.99 us -> 0.36 us  [joined(): return jnp.stack([part.astype(BF) for part in pair])]
  transfers between devices with their start and end apart: 32 -> 31, of which waited for: 21 -> 18; matrix products, arithmetic and copies ran while one was open for 9% -> 3% of each run, Pallas kernels for 0% -> 0%
where the time goes in v1:
time: 212 us; the launch traced here: 211 us
  waiting for transfers between devices  82.5 us (39%)
  starting transfers between devices  58.9 us (28%)
  blocking collectives  41.4 us (20%)
  matrix products  13.8 us (7%)
  other arithmetic  8.14 us (4%)
  local copies, waits for them, and re-layouts  5.85 us (3%)
    ppermute x22, waiting for transfers between devices, paired(): return lax.ppermute(array, axis, [(i, i ^ bit) for i in range(size)])  54.4 us
    ppermute x22, starting transfers between devices, paired(): return lax.ppermute(array, axis, [(i, i ^ bit) for i in range(size)])  36.5 us
    all_to_all x1, blocking collectives, step(): lax.all_to_all(jnp.broadcast_to(part_lse[None, None], (shards, 1, part_ls...  18.6 us
    ppermute x8, starting transfers between devices, shifted(): lax.ppermute(array, axis, [(i, (i + step) % size) for i in range(size)])  16.5 us
    all_to_all x1, waiting for transfers between devices, tokens_for_block(): own = lax.all_to_all(blocks, PROMPT, 0, 0, tiled=True)  15.3 us
    all_to_all x1, blocking collectives, step(): tiles = lax.all_to_all(tiles, PROMPT, 0, 0, tiled=True)  13.5 us
    ppermute x8, waiting for transfers between devices, shifted(): lax.ppermute(array, axis, [(i, (i + step) % size) for i in range(size)])  12.8 us
    dot_general x6, matrix products, products(): jnp.dot(flat, weight, preferred_element_type=F32)  10.3 us
  transfers between devices with their start and end apart: 31, of which 18 were waited for; matrix products, arithmetic and copies ran while one was open for 3% of the time, Pallas kernels for 0%

profile of v1, /device:TPU:1, one launch (start us, length us, event | category | flops | bytes accessed | tf_op | source)
XLA Modules:
  0.0 211.1 jit_solution(89905866702346853)
XLA Ops:
  3.9 5.9 %all-to-all-start = ((bf16[8,64,1024]{2,1,0:T(8,128)(2,1)}), bf16[8,64,1024]{2,1,0:T(8,128)(2,1)S(1)}, u32[]{:S(2)}, u32[]{:S(2)}) async-start(bf16[8,64,1024]{2,1,0:T(8,128)(2,1)} %copy.49), calls=%async_computation | async-start | bytes 2097152 | tf_op jit(solution)/shard_map/all_to_all | solution.py:38
  9.7 15.3 %all-to-all-done = bf16[8,64,1024]{2,1,0:T(8,128)(2,1)S(1)} async-done(((bf16[8,64,1024]{2,1,0:T(8,128)(2,1)}), bf16[8,64,1024]{2,1,0:T(8,128)(2,1)S(1)}, u32[]{:S(2)}, u32[]{:S(2)}) %all-to-all-start) | async-done | bytes 1048608 | tf_op jit(solution)/shard_map/all_to_all | solution.py:38
  35.4 1.9 collective-permute-start.3
  37.3 8.9 %collective-permute-done.1 = bf16[2,2,64,896]{3,2,1,0:T(8,128)(2,1)S(1)} collective-permute-done((bf16[2,2,64,896]{3,2,1,0:T(8,128)(2,1)S(1)}, bf16[2,2,64,896]{3,2,1,0:T(8,128)(2,1)S(1)}, u32[]{:S(2)}, u32[]{:S(2)}) %collective-permute-start.1) | collective-permute-done | bytes 458784 | tf_op jit(solution)/shard_map/ppermute | solution.py:22
  46.2 8.3 %collective-permute-done.2 = bf16[2,2,64,896]{3,2,1,0:T(8,128)(2,1)S(1)} collective-permute-done((bf16[2,2,64,896]{3,2,1,0:T(8,128)(2,1)S(1)}, bf16[2,2,64,896]{3,2,1,0:T(8,128)(2,1)S(1)}, u32[]{:S(2)}, u32[]{:S(2)}) %collective-permute-start.2) | collective-permute-done | bytes 458784 | tf_op jit(solution)/shard_map/ppermute | solution.py:22
  54.5 3.0 %collective-permute-done.3 = bf16[2,2,64,896]{3,2,1,0:T(8,128)(2,1)S(1)} collective-permute-done((bf16[2,2,64,896]{3,2,1,0:T(8,128)(2,1)S(1)}, bf16[2,2,64,896]{3,2,1,0:T(8,128)(2,1)S(1)}, u32[]{:S(2)}, u32[]{:S(2)}) %collective-permute-start.3) | collective-permute-done | bytes 458784 | tf_op jit(solution)/shard_map/ppermute | solution.py:22
  59.2 5.3 %collective-permute-done.12 = bf16[2,64,896]{2,1,0:T(8,128)(2,1)S(1)} collective-permute-done((bf16[2,64,896]{2,1,0:T(8,128)(2,1)S(1)}, bf16[2,64,896]{2,1,0:T(8,128)(2,1)S(1)}, u32[]{:S(2)}, u32[]{:S(2)}) %collective-permute-start.12) | collective-permute-done | bytes 229408 | tf_op jit(solution)/shard_map/ppermute | solution.py:22
  72.2 2.2 %collective-permute-start.16 = (bf16[4,64,896]{2,1,0:T(8,128)(2,1)S(1)}, bf16[4,64,896]{2,1,0:T(8,128)(2,1)S(1)}, u32[]{:S(2)}, u32[]{:S(2)}) collective-permute-start(bf16[4,64,896]{2,1,0:T(8,128)(2,1)S(1)} %get-tuple-element.43), channel_id=1, source_target_pairs={{0,32},{32,0},{1,33},{33,1},{2,34},{34,2},{3,35},{35,3},{4,36},{36... | collective-permute-start | bytes 1376264 | tf_op jit(solution)/shard_map/ppermute | solution.py:22
  74.8 3.9 %collective-permute-start.5 = (bf16[2,64,896]{2,1,0:T(8,128)(2,1)S(1)}, bf16[2,64,896]{2,1,0:T(8,128)(2,1)S(1)}, u32[]{:S(2)}, u32[]{:S(2)}) collective-permute-start(bf16[2,64,896]{2,1,0:T(8,128)(2,1)S(1)} %pad_maximum_fusion.6), channel_id=1, source_target_pairs={{0,128},{64,192},{128,0},{192,64},{1,129},{65,193},{129,1},{193,65... | collective-permute-start | bytes 688136 | tf_op jit(solution)/shard_map/ppermute | solution.py:22
  78.7 4.3 %collective-permute-done.16 = bf16[4,64,896]{2,1,0:T(8,128)(2,1)S(1)} collective-permute-done((bf16[4,64,896]{2,1,0:T(8,128)(2,1)S(1)}, bf16[4,64,896]{2,1,0:T(8,128)(2,1)S(1)}, u32[]{:S(2)}, u32[]{:S(2)}) %collective-permute-start.16) | collective-permute-done | bytes 458784 | tf_op jit(solution)/shard_map/ppermute | solution.py:22
  83.0 2.3 %fusion.10 = bf16[4,2,64,1024]{3,2,1,0:T(8,128)(2,1)} fusion(bf16[896,1024]{1,0:T(8,128)(2,1)S(1)} %copy-done.8, bf16[4,1,64,896]{3,2,0,1:T(8,128)(2,1)S(1)} %bitcast.190, bf16[4,1,64,896]{3,2,0,1:T(8,128)(2,1)S(1)} %get-tuple-element.42), kind=kOutput, calls=%fused_computation.13 | convolution fusion | flops 940507136 | bytes 3801088 | tf_op jit(solution)/shard_map/dot_general | solution.py:52
  85.3 2.9 %collective-permute-start.17 = (bf16[4,2,64,1024]{3,2,1,0:T(8,128)(2,1)}, bf16[4,2,64,1024]{3,2,1,0:T(8,128)(2,1)}, u32[]{:S(2)}, u32[]{:S(2)}) collective-permute-start(bf16[4,2,64,1024]{3,2,1,0:T(8,128)(2,1)} %fusion.10), channel_id=1, source_target_pairs={{0,1},{1,0},{2,3},{3,2},{4,5},{5,4},{6,7},{7,6},{8,9},{9,8},{10,11... | collective-permute-start | bytes 3145736 | tf_op jit(solution)/shard_map/ppermute | solution.py:22
  90.0 2.0 collective-permute-done.8
  93.8 1.7 collective-permute-start.9
  95.4 9.5 %collective-permute-done.11 = bf16[2,64,896]{2,1,0:T(8,128)(2,1)S(1)} collective-permute-done((bf16[2,64,896]{2,1,0:T(8,128)(2,1)S(1)}, bf16[2,64,896]{2,1,0:T(8,128)(2,1)S(1)}, u32[]{:S(2)}, u32[]{:S(2)}) %collective-permute-start.11) | collective-permute-done | bytes 229408 | tf_op jit(solution)/shard_map/ppermute | solution.py:22
  104.9 3.0 %convert_add_fusion = f32[4,2,64,1024]{3,2,1,0:T(8,128)S(1)} fusion(bf16[4,2,64,1024]{3,2,1,0:T(8,128)(2,1)} %collective-permute-done.17, bf16[896,1024]{1,0:T(8,128)(2,1)} %param.11, bf16[1,2,64,896]{3,2,1,0:T(8,128)(2,1)S(1)} %bitcast.191, bf16[1,2,64,896]{3,2,1,0:T(8,128)(2,1)S(1)} %bitcast.192, bf16[1,2,64,896]{3,2,1,0:T(8,128)(2,1)S(1)} %bitcast.193, ...), kind=kOutput, calls=%fused_computation.1 | convolution fusion | flops 941948928 | bytes 5898240 | tf_op jit(solution)/shard_map/dot_general | solution.py:52
  109.4 1.7 collective-permute-start.21
  111.1 4.0 %collective-permute-start.23 = (bf16[8,8,1024]{2,1,0:T(8,128)(2,1)S(1)}, bf16[8,8,1024]{2,1,0:T(8,128)(2,1)S(1)}, u32[]{:S(2)}, u32[]{:S(2)}) collective-permute-start(bf16[8,8,1024]{2,1,0:T(8,128)(2,1)S(1)} %get-tuple-element.23), channel_id=1, source_target_pairs={{0,28},{4,0},{8,4},{12,8},{16,12},{20,16},{24,20},{28,24},{1,29},{... | collective-permute-start | bytes 393224 | tf_op jit(solution)/shard_map/ppermute | solution.py:18
  116.6 3.9 %collective-permute-start.18 = (bf16[8,8,1024]{2,1,0:T(8,128)(2,1)S(1)}, bf16[8,8,1024]{2,1,0:T(8,128)(2,1)S(1)}, u32[]{:S(2)}, u32[]{:S(2)}) collective-permute-start(bf16[8,8,1024]{2,1,0:T(8,128)(2,1)S(1)} %get-tuple-element.19), channel_id=1, source_target_pairs={{0,16},{4,20},{8,24},{12,28},{16,0},{20,4},{24,8},{28,12},{1,17},{... | collective-permute-start | bytes 393224 | tf_op jit(solution)/shard_map/ppermute | solution.py:18
  121.7 2.4 %collective-permute-start.22 = (bf16[8,8,1024]{2,1,0:T(8,128)(2,1)S(1)}, bf16[8,8,1024]{2,1,0:T(8,128)(2,1)S(1)}, u32[]{:S(2)}, u32[]{:S(2)}) collective-permute-start(bf16[8,8,1024]{2,1,0:T(8,128)(2,1)S(1)} %get-tuple-element.24), channel_id=1, source_target_pairs={{0,8},{4,12},{8,16},{12,20},{16,24},{20,28},{24,0},{28,4},{1,9},{5... | collective-permute-start | bytes 393224 | tf_op jit(solution)/shard_map/ppermute | solution.py:18
  125.5 8.7 %collective-permute-done.24 = bf16[8,8,1024]{2,1,0:T(8,128)(2,1)S(1)} collective-permute-done((bf16[8,8,1024]{2,1,0:T(8,128)(2,1)S(1)}, bf16[8,8,1024]{2,1,0:T(8,128)(2,1)S(1)}, u32[]{:S(2)}, u32[]{:S(2)}) %collective-permute-start.24) | collective-permute-done | bytes 131104 | tf_op jit(solution)/shard_map/ppermute | solution.py:18
  135.2 2.9 %collective-permute-start.25 = (bf16[8,8,1024]{2,1,0:T(8,128)(2,1)S(1)}, bf16[8,8,1024]{2,1,0:T(8,128)(2,1)S(1)}, u32[]{:S(2)}, u32[]{:S(2)}) collective-permute-start(bf16[8,8,1024]{2,1,0:T(8,128)(2,1)S(1)} %fusion.31), channel_id=1, source_target_pairs={{0,2},{2,0},{1,3},{3,1},{4,6},{6,4},{5,7},{7,5},{8,10},{10,8},{9,1... | collective-permute-start | bytes 393224 | tf_op jit(solution)/shard_map/ppermute | solution.py:18
  138.2 2.7 %collective-permute-done.25 = bf16[8,8,1024]{2,1,0:T(8,128)(2,1)S(1)} collective-permute-done((bf16[8,8,1024]{2,1,0:T(8,128)(2,1)S(1)}, bf16[8,8,1024]{2,1,0:T(8,128)(2,1)S(1)}, u32[]{:S(2)}, u32[]{:S(2)}) %collective-permute-start.25) | collective-permute-done | bytes 131104 | tf_op jit(solution)/shard_map/ppermute | solution.py:18
  142.0 9.4 %all_to_all.20 = f32[8,8,8]{2,1,0:T(8,128)S(1)} all-to-all(f32[8,8,8]{2,1,0:T(8,128)S(1)} %broadcast_in_dim.4), channel_id=1, replica_groups=mesh['x'=4,'y'=2,'z'=8,'w'=2,'c'=2] {'x','y'}, dimensions={0} | all-to-all | bytes 4096 | tf_op jit(solution)/shard_map/all_to_all | solution.py:120
  152.6 2.3 %collective-permute-start.26 = (bf16[8,1024]{1,0:T(8,128)(2,1)S(1)}, bf16[8,1024]{1,0:T(8,128)(2,1)S(1)}, u32[]{:S(2)}, u32[]{:S(2)}) collective-permute-start(bf16[8,1024]{1,0:T(8,128)(2,1)S(1)} %multiply_convert_fusion.2), channel_id=1, source_target_pairs={{0,4},{4,0},{8,12},{12,8},{16,20},{20,16},{24,28},{28,24},{1,5},{5... | collective-permute-start | bytes 49160 | tf_op jit(solution)/shard_map/ppermute | solution.py:22
  157.1 2.7 %collective-permute-done.27 = bf16[16,1024]{1,0:T(8,128)(2,1)S(1)} collective-permute-done((bf16[16,1024]{1,0:T(8,128)(2,1)S(1)}, bf16[16,1024]{1,0:T(8,128)(2,1)S(1)}, u32[]{:S(2)}, u32[]{:S(2)}) %collective-permute-start.27) | collective-permute-done | bytes 32800 | tf_op jit(solution)/shard_map/ppermute | solution.py:22
  159.8 2.9 %collective-permute-start.28 = (bf16[32,1024]{1,0:T(8,128)(2,1)S(1)}, bf16[32,1024]{1,0:T(8,128)(2,1)S(1)}, u32[]{:S(2)}, u32[]{:S(2)}) collective-permute-start(bf16[32,1024]{1,0:T(8,128)(2,1)S(1)} %pad_maximum_fusion.12), channel_id=1, source_target_pairs={{0,16},{4,20},{8,24},{12,28},{16,0},{20,4},{24,8},{28,12},{1,17},{... | collective-permute-start | bytes 196616 | tf_op jit(solution)/shard_map/ppermute | solution.py:22
  162.8 4.2 %collective-permute-done.28 = bf16[32,1024]{1,0:T(8,128)(2,1)S(1)} collective-permute-done((bf16[32,1024]{1,0:T(8,128)(2,1)S(1)}, bf16[32,1024]{1,0:T(8,128)(2,1)S(1)}, u32[]{:S(2)}, u32[]{:S(2)}) %collective-permute-start.28) | collective-permute-done | bytes 65568 | tf_op jit(solution)/shard_map/ppermute | solution.py:22
  167.0 6.1 %collective-permute-start.29 = (bf16[64,1024]{1,0:T(8,128)(2,1)S(1)}, bf16[64,1024]{1,0:T(8,128)(2,1)S(1)}, u32[]{:S(2)}, u32[]{:S(2)}) collective-permute-start(bf16[64,1024]{1,0:T(8,128)(2,1)S(1)} %pad_maximum_fusion.11), channel_id=1, source_target_pairs={{0,1},{1,0},{2,3},{3,2},{4,5},{5,4},{6,7},{7,6},{8,9},{9,8},{10,11... | collective-permute-start | bytes 393224 | tf_op jit(solution)/shard_map/ppermute | solution.py:22
  174.1 3.5 %convolution_convert_fusion = bf16[128,2688]{1,0:T(8,128)(2,1)S(1)} fusion(bf16[1024,2688]{1,0:T(8,128)(2,1)} %param.13, bf16[64,1024]{1,0:T(8,128)(2,1)S(1)} %get-tuple-element.45, bf16[64,1024]{1,0:T(8,128)(2,1)S(1)} %get-tuple-element.44), kind=kOutput, calls=%fused_computation | convolution fusion | flops 705511424 | bytes 6455296 | tf_op jit(solution)/shard_map/dot_general | solution.py:139
  177.6 13.5 %all_to_all.21 = bf16[8,16,2688]{2,1,0:T(8,128)(2,1)S(1)} all-to-all(bf16[8,16,2688]{2,1,0:T(8,128)(2,1)S(1)} %bitcast.168), channel_id=1, replica_groups=mesh['x'=4,'y'=2,'z'=8,'w'=2,'c'=2] {'x','y'}, dimensions={0} | all-to-all | bytes 1376256 | tf_op jit(solution)/shard_map/all_to_all | solution.py:141
  191.6 18.6 %all_to_all.22 = f32[32,1,16]{2,1,0:T(1,128)S(1)} all-to-all(f32[32,1,16]{2,1,0:T(1,128)S(1)} %broadcast_in_dim.5), channel_id=1, replica_groups=mesh['x'=4,'y'=2,'z'=8,'w'=2,'c'=2] {'z','w','c'}, dimensions={0} | all-to-all | bytes 4096 | tf_op jit(solution)/shard_map/all_to_all | solution.py:146
  (119 shorter events, 40.8 us)
Async XLA Ops:
  3.9 21.1 %all-to-all-start = ((bf16[8,64,1024]{2,1,0:T(8,128)(2,1)}), bf16[8,64,1024]{2,1,0:T(8,128)(2,1)S(1)}, u32[]{:S(2)}, u32[]{:S(2)}) async-start(bf16[8,64,1024]{2,1,0:T(8,128)(2,1)} %copy.49), calls=%async_computation | async-start | bytes 2097152 | tf_op jit(solution)/shard_map/all_to_all | solution.py:38
  25.8 4.4 %collective-permute-start = (bf16[4,2,64,1024]{3,2,1,0:T(8,128)(2,1)S(1)}, bf16[4,2,64,1024]{3,2,1,0:T(8,128)(2,1)S(1)}, u32[]{:S(2)}, u32[]{:S(2)}) collective-permute-start(bf16[4,2,64,1024]{3,2,1,0:T(8,128)(2,1)S(1)} %bitcast.171), channel_id=1, source_target_pairs={{0,1},{1,0},{2,3},{3,2},{4,5},{5,4},{6,7},{7,6},{8,9},{9,8},{10,11... | collective-permute-start | bytes 3145736 | tf_op jit(solution)/shard_map/ppermute | solution.py:22
  33.0 24.5 %collective-permute-start.4 = (bf16[2,4,64,896]{3,2,1,0:T(8,128)(2,1)S(1)}, bf16[2,4,64,896]{3,2,1,0:T(8,128)(2,1)S(1)}, u32[]{:S(2)}, u32[]{:S(2)}) collective-permute-start(bf16[2,4,64,896]{3,2,1,0:T(8,128)(2,1)S(1)} %pad_maximum_fusion), channel_id=1, source_target_pairs={{0,32},{32,0},{1,33},{33,1},{2,34},{34,2},{3,35},{35,3},{4,36},{36... | collective-permute-start | bytes 2752520 | tf_op jit(solution)/shard_map/ppermute | solution.py:22
  33.6 12.6 %collective-permute-start.1 = (bf16[2,2,64,896]{3,2,1,0:T(8,128)(2,1)S(1)}, bf16[2,2,64,896]{3,2,1,0:T(8,128)(2,1)S(1)}, u32[]{:S(2)}, u32[]{:S(2)}) collective-permute-start(bf16[2,2,64,896]{3,2,1,0:T(8,128)(2,1)S(1)} %pad_maximum_fusion.2), channel_id=1, source_target_pairs={{0,128},{64,192},{128,0},{192,64},{1,129},{65,193},{129,1},{193,65... | collective-permute-start | bytes 1376264 | tf_op jit(solution)/shard_map/ppermute | solution.py:22
  34.4 20.1 %collective-permute-start.2 = (bf16[2,2,64,896]{3,2,1,0:T(8,128)(2,1)S(1)}, bf16[2,2,64,896]{3,2,1,0:T(8,128)(2,1)S(1)}, u32[]{:S(2)}, u32[]{:S(2)}) collective-permute-start(bf16[2,2,64,896]{3,2,1,0:T(8,128)(2,1)S(1)} %pad_maximum_fusion.3), channel_id=1, source_target_pairs={{0,64},{64,0},{128,192},{192,128},{1,65},{65,1},{129,193},{193,129... | collective-permute-start | bytes 1376264 | tf_op jit(solution)/shard_map/ppermute | solution.py:22
  35.4 22.1 %collective-permute-start.3 = (bf16[2,2,64,896]{3,2,1,0:T(8,128)(2,1)S(1)}, bf16[2,2,64,896]{3,2,1,0:T(8,128)(2,1)S(1)}, u32[]{:S(2)}, u32[]{:S(2)}) collective-permute-start(bf16[2,2,64,896]{3,2,1,0:T(8,128)(2,1)S(1)} %pad_maximum_fusion.4), channel_id=1, source_target_pairs={{0,192},{64,128},{128,64},{192,0},{1,193},{65,129},{129,65},{193,1... | collective-permute-start | bytes 1376264 | tf_op jit(solution)/shard_map/ppermute | solution.py:22
  57.8 6.8 %collective-permute-start.12 = (bf16[2,64,896]{2,1,0:T(8,128)(2,1)S(1)}, bf16[2,64,896]{2,1,0:T(8,128)(2,1)S(1)}, u32[]{:S(2)}, u32[]{:S(2)}) collective-permute-start(bf16[2,64,896]{2,1,0:T(8,128)(2,1)S(1)} %pad_maximum_fusion.10), channel_id=1, source_target_pairs={{0,32},{32,0},{1,33},{33,1},{2,34},{34,2},{3,35},{35,3},{4,36},{36... | collective-permute-start | bytes 688136 | tf_op jit(solution)/shard_map/ppermute | solution.py:22
  64.6 5.0 %collective-permute-start.15 = (bf16[64,896]{1,0:T(8,128)(2,1)S(1)}, bf16[64,896]{1,0:T(8,128)(2,1)S(1)}, u32[]{:S(2)}, u32[]{:S(2)}) collective-permute-start(bf16[64,896]{1,0:T(8,128)(2,1)S(1)} %fusion.32), channel_id=1, source_target_pairs={{0,192},{64,128},{128,64},{192,0},{1,193},{65,129},{129,65},{193,1... | collective-permute-start | bytes 344072 | tf_op jit(solution)/shard_map/ppermute | solution.py:22
  65.6 5.3 %collective-permute-start.14 = (bf16[64,896]{1,0:T(8,128)(2,1)S(1)}, bf16[64,896]{1,0:T(8,128)(2,1)S(1)}, u32[]{:S(2)}, u32[]{:S(2)}) collective-permute-start(bf16[64,896]{1,0:T(8,128)(2,1)S(1)} %fusion.32), channel_id=1, source_target_pairs={{0,128},{64,192},{128,0},{192,64},{1,129},{65,193},{129,1},{193,65... | collective-permute-start | bytes 344072 | tf_op jit(solution)/shard_map/ppermute | solution.py:22
  66.8 5.3 %collective-permute-start.13 = (bf16[64,896]{1,0:T(8,128)(2,1)S(1)}, bf16[64,896]{1,0:T(8,128)(2,1)S(1)}, u32[]{:S(2)}, u32[]{:S(2)}) collective-permute-start(bf16[64,896]{1,0:T(8,128)(2,1)S(1)} %fusion.32), channel_id=1, source_target_pairs={{0,64},{64,0},{128,192},{192,128},{1,65},{65,1},{129,193},{193,129... | collective-permute-start | bytes 344072 | tf_op jit(solution)/shard_map/ppermute | solution.py:22
  72.2 10.8 %collective-permute-start.16 = (bf16[4,64,896]{2,1,0:T(8,128)(2,1)S(1)}, bf16[4,64,896]{2,1,0:T(8,128)(2,1)S(1)}, u32[]{:S(2)}, u32[]{:S(2)}) collective-permute-start(bf16[4,64,896]{2,1,0:T(8,128)(2,1)S(1)} %get-tuple-element.43), channel_id=1, source_target_pairs={{0,32},{32,0},{1,33},{33,1},{2,34},{34,2},{3,35},{35,3},{4,36},{36... | collective-permute-start | bytes 1376264 | tf_op jit(solution)/shard_map/ppermute | solution.py:22
  74.5 13.7 %collective-permute-start.7 = (bf16[2,64,896]{2,1,0:T(8,128)(2,1)S(1)}, bf16[2,64,896]{2,1,0:T(8,128)(2,1)S(1)}, u32[]{:S(2)}, u32[]{:S(2)}) collective-permute-start(bf16[2,64,896]{2,1,0:T(8,128)(2,1)S(1)} %pad_maximum_fusion.8), channel_id=1, source_target_pairs={{0,192},{64,128},{128,64},{192,0},{1,193},{65,129},{129,65},{193,1... | collective-permute-start | bytes 688136 | tf_op jit(solution)/shard_map/ppermute | solution.py:22
  74.6 13.5 %collective-permute-start.6 = (bf16[2,64,896]{2,1,0:T(8,128)(2,1)S(1)}, bf16[2,64,896]{2,1,0:T(8,128)(2,1)S(1)}, u32[]{:S(2)}, u32[]{:S(2)}) collective-permute-start(bf16[2,64,896]{2,1,0:T(8,128)(2,1)S(1)} %pad_maximum_fusion.7), channel_id=1, source_target_pairs={{0,64},{64,0},{128,192},{192,128},{1,65},{65,1},{129,193},{193,129... | collective-permute-start | bytes 688136 | tf_op jit(solution)/shard_map/ppermute | solution.py:22
  74.8 13.4 %collective-permute-start.5 = (bf16[2,64,896]{2,1,0:T(8,128)(2,1)S(1)}, bf16[2,64,896]{2,1,0:T(8,128)(2,1)S(1)}, u32[]{:S(2)}, u32[]{:S(2)}) collective-permute-start(bf16[2,64,896]{2,1,0:T(8,128)(2,1)S(1)} %pad_maximum_fusion.6), channel_id=1, source_target_pairs={{0,128},{64,192},{128,0},{192,64},{1,129},{65,193},{129,1},{193,65... | collective-permute-start | bytes 688136 | tf_op jit(solution)/shard_map/ppermute | solution.py:22
  85.3 19.6 %collective-permute-start.17 = (bf16[4,2,64,1024]{3,2,1,0:T(8,128)(2,1)}, bf16[4,2,64,1024]{3,2,1,0:T(8,128)(2,1)}, u32[]{:S(2)}, u32[]{:S(2)}) collective-permute-start(bf16[4,2,64,1024]{3,2,1,0:T(8,128)(2,1)} %fusion.10), channel_id=1, source_target_pairs={{0,1},{1,0},{2,3},{3,2},{4,5},{5,4},{6,7},{7,6},{8,9},{9,8},{10,11... | collective-permute-start | bytes 3145736 | tf_op jit(solution)/shard_map/ppermute | solution.py:22
  88.3 3.7 %collective-permute-start.8 = (bf16[64,896]{1,0:T(8,128)(2,1)S(1)}, bf16[64,896]{1,0:T(8,128)(2,1)S(1)}, u32[]{:S(2)}, u32[]{:S(2)}) collective-permute-start(bf16[64,896]{1,0:T(8,128)(2,1)S(1)} %fusion.36), channel_id=1, source_target_pairs={{0,32},{32,0},{1,33},{33,1},{2,34},{34,2},{3,35},{35,3},{4,36},{36... | collective-permute-start | bytes 344072 | tf_op jit(solution)/shard_map/ppermute | solution.py:22
  92.1 12.8 %collective-permute-start.11 = (bf16[2,64,896]{2,1,0:T(8,128)(2,1)S(1)}, bf16[2,64,896]{2,1,0:T(8,128)(2,1)S(1)}, u32[]{:S(2)}, u32[]{:S(2)}) collective-permute-start(bf16[2,64,896]{2,1,0:T(8,128)(2,1)S(1)} %get-tuple-element.47), channel_id=1, source_target_pairs={{0,192},{64,128},{128,64},{192,0},{1,193},{65,129},{129,65},{193,1... | collective-permute-start | bytes 688136 | tf_op jit(solution)/shard_map/ppermute | solution.py:22
  92.5 12.4 %collective-permute-start.10 = (bf16[2,64,896]{2,1,0:T(8,128)(2,1)S(1)}, bf16[2,64,896]{2,1,0:T(8,128)(2,1)S(1)}, u32[]{:S(2)}, u32[]{:S(2)}) collective-permute-start(bf16[2,64,896]{2,1,0:T(8,128)(2,1)S(1)} %get-tuple-element.47), channel_id=1, source_target_pairs={{0,128},{64,192},{128,0},{192,64},{1,129},{65,193},{129,1},{193,65... | collective-permute-start | bytes 688136 | tf_op jit(solution)/shard_map/ppermute | solution.py:22
  93.8 11.2 %collective-permute-start.9 = (bf16[2,64,896]{2,1,0:T(8,128)(2,1)S(1)}, bf16[2,64,896]{2,1,0:T(8,128)(2,1)S(1)}, u32[]{:S(2)}, u32[]{:S(2)}) collective-permute-start(bf16[2,64,896]{2,1,0:T(8,128)(2,1)S(1)} %get-tuple-element.47), channel_id=1, source_target_pairs={{0,64},{64,0},{128,192},{192,128},{1,65},{65,1},{129,193},{193,129... | collective-permute-start | bytes 688136 | tf_op jit(solution)/shard_map/ppermute | solution.py:22
  109.4 43.1 %copy-start.4 = (f32[1024]{0:T(1024)S(1)}, f32[1024]{0:T(1024)}, u32[]{:S(2)}) copy-start(f32[1024]{0:T(1024)} %param.12) | copy-start | bytes 12292
  109.4 11.1 %collective-permute-start.21 = (bf16[8,8,1024]{2,1,0:T(8,128)(2,1)S(1)}, bf16[8,8,1024]{2,1,0:T(8,128)(2,1)S(1)}, u32[]{:S(2)}, u32[]{:S(2)}) collective-permute-start(bf16[8,8,1024]{2,1,0:T(8,128)(2,1)S(1)} %get-tuple-element.20), channel_id=1, source_target_pairs={{0,4},{4,8},{8,12},{12,16},{16,20},{20,24},{24,28},{28,0},{1,5},{5... | collective-permute-start | bytes 393224 | tf_op jit(solution)/shard_map/ppermute | solution.py:18
  111.1 9.4 %collective-permute-start.23 = (bf16[8,8,1024]{2,1,0:T(8,128)(2,1)S(1)}, bf16[8,8,1024]{2,1,0:T(8,128)(2,1)S(1)}, u32[]{:S(2)}, u32[]{:S(2)}) collective-permute-start(bf16[8,8,1024]{2,1,0:T(8,128)(2,1)S(1)} %get-tuple-element.23), channel_id=1, source_target_pairs={{0,28},{4,0},{8,4},{12,8},{16,12},{20,16},{24,20},{28,24},{1,29},{... | collective-permute-start | bytes 393224 | tf_op jit(solution)/shard_map/ppermute | solution.py:18
  115.2 8.9 %collective-permute-start.20 = (bf16[8,8,1024]{2,1,0:T(8,128)(2,1)S(1)}, bf16[8,8,1024]{2,1,0:T(8,128)(2,1)S(1)}, u32[]{:S(2)}, u32[]{:S(2)}) collective-permute-start(bf16[8,8,1024]{2,1,0:T(8,128)(2,1)S(1)} %get-tuple-element.21), channel_id=1, source_target_pairs={{0,28},{4,0},{8,4},{12,8},{16,12},{20,16},{24,20},{28,24},{1,29},{... | collective-permute-start | bytes 393224 | tf_op jit(solution)/shard_map/ppermute | solution.py:18
  116.5 7.6 %collective-permute-start.19 = (bf16[8,8,1024]{2,1,0:T(8,128)(2,1)S(1)}, bf16[8,8,1024]{2,1,0:T(8,128)(2,1)S(1)}, u32[]{:S(2)}, u32[]{:S(2)}) collective-permute-start(bf16[8,8,1024]{2,1,0:T(8,128)(2,1)S(1)} %get-tuple-element.22), channel_id=1, source_target_pairs={{0,4},{4,8},{8,12},{12,16},{16,20},{20,24},{24,28},{28,0},{1,5},{5... | collective-permute-start | bytes 393224 | tf_op jit(solution)/shard_map/ppermute | solution.py:18
  116.6 8.9 %collective-permute-start.18 = (bf16[8,8,1024]{2,1,0:T(8,128)(2,1)S(1)}, bf16[8,8,1024]{2,1,0:T(8,128)(2,1)S(1)}, u32[]{:S(2)}, u32[]{:S(2)}) collective-permute-start(bf16[8,8,1024]{2,1,0:T(8,128)(2,1)S(1)} %get-tuple-element.19), channel_id=1, source_target_pairs={{0,16},{4,20},{8,24},{12,28},{16,0},{20,4},{24,8},{28,12},{1,17},{... | collective-permute-start | bytes 393224 | tf_op jit(solution)/shard_map/ppermute | solution.py:18
  121.7 12.5 %collective-permute-start.24 = (bf16[8,8,1024]{2,1,0:T(8,128)(2,1)S(1)}, bf16[8,8,1024]{2,1,0:T(8,128)(2,1)S(1)}, u32[]{:S(2)}, u32[]{:S(2)}) collective-permute-start(bf16[8,8,1024]{2,1,0:T(8,128)(2,1)S(1)} %get-tuple-element.25), channel_id=1, source_target_pairs={{0,24},{4,28},{8,0},{12,4},{16,8},{20,12},{24,16},{28,20},{1,25},{... | collective-permute-start | bytes 393224 | tf_op jit(solution)/shard_map/ppermute | solution.py:18
  121.7 12.4 %collective-permute-start.22 = (bf16[8,8,1024]{2,1,0:T(8,128)(2,1)S(1)}, bf16[8,8,1024]{2,1,0:T(8,128)(2,1)S(1)}, u32[]{:S(2)}, u32[]{:S(2)}) collective-permute-start(bf16[8,8,1024]{2,1,0:T(8,128)(2,1)S(1)} %get-tuple-element.24), channel_id=1, source_target_pairs={{0,8},{4,12},{8,16},{12,20},{16,24},{20,28},{24,0},{28,4},{1,9},{5... | collective-permute-start | bytes 393224 | tf_op jit(solution)/shard_map/ppermute | solution.py:18
  135.2 5.6 %collective-permute-start.25 = (bf16[8,8,1024]{2,1,0:T(8,128)(2,1)S(1)}, bf16[8,8,1024]{2,1,0:T(8,128)(2,1)S(1)}, u32[]{:S(2)}, u32[]{:S(2)}) collective-permute-start(bf16[8,8,1024]{2,1,0:T(8,128)(2,1)S(1)} %fusion.31), channel_id=1, source_target_pairs={{0,2},{2,0},{1,3},{3,1},{4,6},{6,4},{5,7},{7,5},{8,10},{10,8},{9,1... | collective-permute-start | bytes 393224 | tf_op jit(solution)/shard_map/ppermute | solution.py:18
  152.6 3.5 %collective-permute-start.26 = (bf16[8,1024]{1,0:T(8,128)(2,1)S(1)}, bf16[8,1024]{1,0:T(8,128)(2,1)S(1)}, u32[]{:S(2)}, u32[]{:S(2)}) collective-permute-start(bf16[8,1024]{1,0:T(8,128)(2,1)S(1)} %multiply_convert_fusion.2), channel_id=1, source_target_pairs={{0,4},{4,0},{8,12},{12,8},{16,20},{20,16},{24,28},{28,24},{1,5},{5... | collective-permute-start | bytes 49160 | tf_op jit(solution)/shard_map/ppermute | solution.py:22
  156.1 3.8 %collective-permute-start.27 = (bf16[16,1024]{1,0:T(8,128)(2,1)S(1)}, bf16[16,1024]{1,0:T(8,128)(2,1)S(1)}, u32[]{:S(2)}, u32[]{:S(2)}) collective-permute-start(bf16[16,1024]{1,0:T(8,128)(2,1)S(1)} %pad_maximum_fusion.13), channel_id=1, source_target_pairs={{0,8},{4,12},{8,0},{12,4},{16,24},{20,28},{24,16},{28,20},{1,9},{5... | collective-permute-start | bytes 98312 | tf_op jit(solution)/shard_map/ppermute | solution.py:22
  159.8 7.1 %collective-permute-start.28 = (bf16[32,1024]{1,0:T(8,128)(2,1)S(1)}, bf16[32,1024]{1,0:T(8,128)(2,1)S(1)}, u32[]{:S(2)}, u32[]{:S(2)}) collective-permute-start(bf16[32,1024]{1,0:T(8,128)(2,1)S(1)} %pad_maximum_fusion.12), channel_id=1, source_target_pairs={{0,16},{4,20},{8,24},{12,28},{16,0},{20,4},{24,8},{28,12},{1,17},{... | collective-permute-start | bytes 196616 | tf_op jit(solution)/shard_map/ppermute | solution.py:22
  167.0 7.1 %collective-permute-start.29 = (bf16[64,1024]{1,0:T(8,128)(2,1)S(1)}, bf16[64,1024]{1,0:T(8,128)(2,1)S(1)}, u32[]{:S(2)}, u32[]{:S(2)}) collective-permute-start(bf16[64,1024]{1,0:T(8,128)(2,1)S(1)} %pad_maximum_fusion.11), channel_id=1, source_target_pairs={{0,1},{1,0},{2,3},{3,2},{4,5},{5,4},{6,7},{7,6},{8,9},{9,8},{10,11... | collective-permute-start | bytes 393224 | tf_op jit(solution)/shard_map/ppermute | solution.py:22
  (8 other events, 74.5 us)

commit v2 on v1

--- a/solution.py
+++ b/solution.py
@@ -1,6 +1,8 @@
 import jax
 import jax.numpy as jnp
 from jax import lax
+from jax.experimental import pallas as pl
+from jax.experimental.pallas import tpu as pltpu
 from jax.sharding import Mesh
 from jax.sharding import PartitionSpec as P
 
@@ -22,25 +24,43 @@
     return lax.ppermute(array, axis, [(i, i ^ bit) for i in range(size)])
 
 
-def flipped_if(bit, array, axis):
-    return jnp.where(bit == 0, array, jnp.flip(array, axis))
-
-
 def wide(array):
     return array.astype(F32)
 
 
-def tokens_for_block(tokens, x, y, c):
+def paired_prompt(array, k):
+    return lax.ppermute(array, PROMPT, [(p, p ^ k) for p in range(NX * NY)])
+
+
+def blocks_kernel(place_ref, rows_ref, out_ref):
+    share = out_ref.shape[2]
+    for k in range(NX * NY):
+        start = pl.multiple_of((place_ref[0] ^ k) * share, share)
+        out_ref[k] = rows_ref[:, pl.ds(start, share)]
+
+
+def blocks_for(tokens, place, c):
     half = tokens.shape[0] // NC
     share = D // (NX * NY)
-    mine = lax.dynamic_slice_in_dim(tokens, c * half, half, 0)
-    blocks = mine.reshape(half, NX * NY, share).transpose(1, 0, 2)
-    own = lax.all_to_all(blocks, PROMPT, 0, 0, tiled=True)
-    own = own.reshape(2, 2, NY, half, share)
-    for axis, bit in enumerate((x // 2, x % 2, y)):
-        own = flipped_if(bit, own, axis)
-    own = lax.optimization_barrier(own.reshape(NX, NY, half, share))
-    return own, paired(own, "c", NC, 1)
+    return pl.pallas_call(
+        blocks_kernel,
+        out_shape=jax.ShapeDtypeStruct((NX * NY, half, share), tokens.dtype),
+        grid_spec=pltpu.PrefetchScalarGridSpec(
+            num_scalar_prefetch=1,
+            grid=(1,),
+            in_specs=[pl.BlockSpec((half, D), lambda i, where: (where[1], 0))],
+            out_specs=pl.BlockSpec((NX * NY, half, share), lambda i, where: (0, 0, 0)),
+        ),
+    )(jnp.stack([place, c]).astype(jnp.int32), tokens)
+
+
+def tokens_for_block(tokens, place, c):
+    blocks = blocks_for(tokens, place, c)
+    own = [blocks[0]] + [None] * (NX * NY - 1)
+    for k in (4, 5, 2, 3, 6, 7, 1):
+        own[k] = paired_prompt(blocks[k], k)
+    other = paired(jnp.stack(own), "c", NC, 1)
+    return own, other.reshape(NX, NY, *own[0].shape)
 
 
 def at(array, index, axis):
@@ -60,21 +80,29 @@
 def step(tokens, gate_weight, up_weight, down_weight, norm_gain, unembed, guidance, logit_bias):
     x, y, z, _, c = (lax.axis_index(axis) for axis in AXES)
     tokens = tokens[0]
-    own, other = tokens_for_block(tokens, x, y, c)
+    own, other = tokens_for_block(tokens, x * NY + y, c)
     both = (gate_weight, up_weight)
 
-    pa = products(own, both)
-    got_a = [paired(joined([p[d] for p in pa]), "x", NX, d) for d in TURNS]
+    def own_products(*offsets):
+        rows = jnp.stack([jnp.stack(own[NY * d : NY * d + NY]) for d in offsets])
+        return zip(offsets, zip(*products(rows, both)))
+
+    pa, got_a = {}, []
+    for offsets in ((2,), (1, 3), (0,)):
+        pa.update(own_products(*offsets))
+    got_a = [paired(joined(pa[d]), "x", NX, d) for d in TURNS]
     pb = products(other, both)
-    swap_b = paired(joined([p[:, 1] for p in pb]), "y", NY, 1)
-    got_a, swap_b = lax.optimization_barrier((got_a, swap_b))
-    sum_a = [p[0] + sum(wide(got[i]) for got in got_a) for i, p in enumerate(pa)]
+    swap_b = paired(joined([p[1:, 1] for p in pb]), "y", NY, 1)
+    got_a, swap_b, pa[0] = lax.optimization_barrier((got_a, swap_b, pa[0]))
+    sum_a = [p + sum(wide(got[i]) for got in got_a) for i, p in enumerate(pa[0])]
     swap_a = paired(joined([p[1] for p in sum_a]), "y", NY, 1)
-    sum_b = [p[:, 0] + wide(got) for p, got in zip(pb, swap_b)]
-    got_b = [paired(joined([p[d] for p in sum_b]), "x", NX, d) for d in TURNS]
+    sum_b = [p[1:, 0] + wide(got) for p, got in zip(pb, swap_b)]
+    got_b = [paired(joined([p[d - 1] for p in sum_b]), "x", NX, d) for d in TURNS]
+    last_b = paired(joined([p[0, 1] for p in pb]), "y", NY, 1)
+    got_b = got_b + [last_b]
     gate_a, up_a = [p[0] + wide(got) for p, got in zip(sum_a, swap_a)]
     hidden_a = (jax.nn.silu(gate_a) * up_a).astype(BF)
-    gate_b, up_b = [p[0] + sum(wide(got[i]) for got in got_b) for i, p in enumerate(sum_b)]
+    gate_b, up_b = [p[0, 0] + sum(wide(got[i]) for got in got_b) for i, p in enumerate(pb)]
     hidden_b = (jax.nn.silu(gate_b) * up_b).astype(BF)
 
     line_a = [hidden_a] + [None] * (NX - 1)
@@ -126,11 +154,8 @@
     scale = jnp.sum(placed_at[:, :, None] * scale[:, None], axis=0)
     mixed = (jnp.sum(state * scale[:, :, None], axis=0) * norm_gain).astype(BF)
 
-    ring = mixed
-    for bit in (1, 2, 4):
-        peer = paired(ring, "z", NZ, bit)
-        low = (z & bit) == 0
-        ring = jnp.concatenate([jnp.where(low, ring, peer), jnp.where(low, peer, ring)])
+    ring = jnp.broadcast_to(mixed[None], (NZ, *mixed.shape))
+    ring = lax.all_to_all(ring, "z", 0, 0, tiled=True).reshape(-1, share)
     peer = paired(ring, "c", NC, 1)
     first = jnp.where(c == 0, peer, ring)
     second = jnp.where(c == 0, ring, peer)
@@ -152,6 +177,7 @@
 
 
 TURNS = (2, 1, 3)
+TURNS = (2, 1, 3)
 
 
 def solution(mesh):

time: 212 us -> 201 us (0.948)
  waiting for transfers between devices: 82.5 us -> 54.3 us
  blocking collectives: 41.4 us -> 55.3 us
  starting transfers between devices: 58.9 us -> 62.9 us
  Pallas kernels: 0 us -> 2.97 us
  local copies, waits for them, and re-layouts: 5.85 us -> 3.31 us
    all_to_all x1 -> x0, waiting for transfers between devices: 15.3 us -> none  [tokens_for_block(): own = lax.all_to_all(blocks, PROMPT, 0, 0, tiled=True)]
    ppermute x22 -> x20, waiting for transfers between devices: 54.4 us -> 40.1 us  [paired(): return lax.ppermute(array, axis, [(i, i ^ bit) for i in range(size)])]
    all_to_all x0 -> x1, blocking collectives: none -> 13.4 us  [step(): ring = lax.all_to_all(ring, 'z', 0, 0, tiled=True).reshape(-1, share)]
    ppermute x0 -> x7, starting transfers between devices: none -> 10.2 us  [paired_prompt(): return lax.ppermute(array, PROMPT, [(p, p ^ k) for p in range(NX * NY)])]
    all_to_all x1 -> x0, starting transfers between devices: 5.85 us -> none  [tokens_for_block(): own = lax.all_to_all(blocks, PROMPT, 0, 0, tiled=True)]
    ppermute x0 -> x7, waiting for transfers between devices: none -> 4.78 us  [paired_prompt(): return lax.ppermute(array, PROMPT, [(p, p ^ k) for p in range(NX * NY)])]
    all_to_all x1, blocking collectives: 9.36 us -> 13.2 us  [step(): lax.all_to_all(jnp.broadcast_to(by_variant[None], (NX * NY, *by_variant.s...]
    all_to_all x1, blocking collectives: 18.6 us -> 15.1 us  [step(): lax.all_to_all(jnp.broadcast_to(part_lse[None, None], (shards, 1, part_ls...]
  transfers between devices with their start and end apart: 31 -> 35, of which waited for: 18 -> 16; matrix products, arithmetic and copies ran while one was open for 3% -> 5% of each run, Pallas kernels for 0% -> 0%
where the time goes in v2:
time: 201 us
  starting transfers between devices  62.9 us (31%)
  blocking collectives  55.3 us (28%)
  waiting for transfers between devices  54.3 us (27%)
  matrix products  13.8 us (7%)
  other arithmetic  7.91 us (4%)
  local copies, waits for them, and re-layouts  3.31 us (2%)
  Pallas kernels  2.97 us (1%)
    ppermute x20, waiting for transfers between devices, paired(): return lax.ppermute(array, axis, [(i, i ^ bit) for i in range(size)])  40.1 us
    ppermute x20, starting transfers between devices, paired(): return lax.ppermute(array, axis, [(i, i ^ bit) for i in range(size)])  35.6 us
    ppermute x8, starting transfers between devices, shifted(): lax.ppermute(array, axis, [(i, (i + step) % size) for i in range(size)])  17.1 us
    all_to_all x1, blocking collectives, step(): lax.all_to_all(jnp.broadcast_to(part_lse[None, None], (shards, 1, part_ls...  15.1 us
    all_to_all x1, blocking collectives, step(): tiles = lax.all_to_all(tiles, PROMPT, 0, 0, tiled=True)  13.5 us
    all_to_all x1, blocking collectives, step(): ring = lax.all_to_all(ring, 'z', 0, 0, tiled=True).reshape(-1, share)  13.4 us
    all_to_all x1, blocking collectives, step(): lax.all_to_all(jnp.broadcast_to(by_variant[None], (NX * NY, *by_variant.s...  13.2 us
    dot_general x10, matrix products, products(): jnp.dot(flat, weight, preferred_element_type=F32)  10.3 us
  transfers between devices with their start and end apart: 35, of which 16 were waited for; matrix products, arithmetic and copies ran while one was open for 5% of the time, Pallas kernels for 0%

profile of v2, /device:TPU:1, one launch (start us, length us, event | category | flops | bytes accessed | tf_op | source)
XLA Modules:
  0.0 201.1 jit_solution(5802065720169265919)
XLA Ops:
  0.6 3.0 %shard_map.82 = bf16[8,64,1024]{2,1,0:T(8,128)(2,1)} custom-call(s32[2]{0:T(128)} %pad_add_fusion.place_ref, bf16[128,8192]{1,0:T(8,128)(2,1)} %bitcast.236), custom_call_target="tpu_custom_call" | custom-call | tf_op jit(solution)/shard_map/pallas_call | solution.py:45
  5.1 3.1 %collective-permute-start.2 = (bf16[64,1024]{1,0:T(8,128)(2,1)S(1)}, bf16[64,1024]{1,0:T(8,128)(2,1)S(1)}, u32[]{:S(2)}, u32[]{:S(2)}) collective-permute-start(bf16[64,1024]{1,0:T(8,128)(2,1)S(1)} %get-tuple-element.34), channel_id=1, source_target_pairs={{0,96},{32,64},{64,32},{96,0},{128,224},{160,192},{192,160},{224,1... | collective-permute-start | bytes 393224 | tf_op jit(solution)/shard_map/ppermute | solution.py:32
  8.5 2.4 %collective-permute-start.6 = (bf16[64,1024]{1,0:T(8,128)(2,1)S(1)}, bf16[64,1024]{1,0:T(8,128)(2,1)S(1)}, u32[]{:S(2)}, u32[]{:S(2)}) collective-permute-start(bf16[64,1024]{1,0:T(8,128)(2,1)S(1)} %get-tuple-element.30), channel_id=1, source_target_pairs={{0,224},{32,192},{64,160},{96,128},{128,96},{160,64},{192,32},{224... | collective-permute-start | bytes 393224 | tf_op jit(solution)/shard_map/ppermute | solution.py:32
  11.0 2.6 %collective-permute-start.4 = (bf16[64,1024]{1,0:T(8,128)(2,1)S(1)}, bf16[64,1024]{1,0:T(8,128)(2,1)S(1)}, u32[]{:S(2)}, u32[]{:S(2)}) collective-permute-start(bf16[64,1024]{1,0:T(8,128)(2,1)S(1)} %get-tuple-element.32), channel_id=1, source_target_pairs={{0,160},{32,128},{64,224},{96,192},{128,32},{160,0},{192,96},{224,... | collective-permute-start | bytes 393224 | tf_op jit(solution)/shard_map/ppermute | solution.py:32
  18.8 2.2 %collective-permute-done = bf16[64,1024]{1,0:T(8,128)(2,1)S(1)} collective-permute-done((bf16[64,1024]{1,0:T(8,128)(2,1)S(1)}, bf16[64,1024]{1,0:T(8,128)(2,1)S(1)}, u32[]{:S(2)}, u32[]{:S(2)}) %collective-permute-start) | collective-permute-done | bytes 131104 | tf_op jit(solution)/shard_map/ppermute | solution.py:32
  22.2 4.9 %collective-permute-start.7 = (bf16[8,64,1024]{2,1,0:T(8,128)(2,1)S(1)}, bf16[8,64,1024]{2,1,0:T(8,128)(2,1)S(1)}, u32[]{:S(2)}, u32[]{:S(2)}) collective-permute-start(bf16[8,64,1024]{2,1,0:T(8,128)(2,1)S(1)} %constant_dynamic-update-slice_fusion), channel_id=1, source_target_pairs={{0,1},{1,0},{2,3},{3,2},{4,5},{5,4},{6,7},{7,6},{8,9},{9,8},{10,11... | collective-permute-start | bytes 3145736 | tf_op jit(solution)/shard_map/ppermute | solution.py:24
  34.6 1.8 collective-permute-start.8
  37.3 13.0 %collective-permute-done.10 = bf16[2,2,64,896]{3,2,1,0:T(8,128)(2,1)S(1)} collective-permute-done((bf16[2,2,64,896]{3,2,1,0:T(8,128)(2,1)S(1)}, bf16[2,2,64,896]{3,2,1,0:T(8,128)(2,1)S(1)}, u32[]{:S(2)}, u32[]{:S(2)}) %collective-permute-start.10) | collective-permute-done | bytes 458784 | tf_op jit(solution)/shard_map/ppermute | solution.py:24
  51.8 8.0 %collective-permute-done.20 = bf16[2,64,896]{2,1,0:T(8,128)(2,1)S(1)} collective-permute-done((bf16[2,64,896]{2,1,0:T(8,128)(2,1)S(1)}, bf16[2,64,896]{2,1,0:T(8,128)(2,1)S(1)}, u32[]{:S(2)}, u32[]{:S(2)}) %collective-permute-start.20) | collective-permute-done | bytes 229408 | tf_op jit(solution)/shard_map/ppermute | solution.py:24
  61.3 1.7 collective-permute-start.22
  64.8 1.7 collective-permute-done.22
  72.7 4.9 %collective-permute-done.24 = bf16[4,64,896]{2,1,0:T(8,128)(2,1)S(1)} collective-permute-done((bf16[4,64,896]{2,1,0:T(8,128)(2,1)S(1)}, bf16[4,64,896]{2,1,0:T(8,128)(2,1)S(1)}, u32[]{:S(2)}, u32[]{:S(2)}) %collective-permute-start.24) | collective-permute-done | bytes 458784 | tf_op jit(solution)/shard_map/ppermute | solution.py:24
  78.8 3.2 %collective-permute-start.25 = (bf16[4,2,64,1024]{3,2,1,0:T(8,128)(2,1)S(1)}, bf16[4,2,64,1024]{3,2,1,0:T(8,128)(2,1)}, u32[]{:S(2)}, u32[]{:S(2)}) collective-permute-start(bf16[4,2,64,1024]{3,2,1,0:T(8,128)(2,1)S(1)} %fusion.18), channel_id=1, source_target_pairs={{0,1},{1,0},{2,3},{3,2},{4,5},{5,4},{6,7},{7,6},{8,9},{9,8},{10,11... | collective-permute-start | bytes 3145736 | tf_op jit(solution)/shard_map/ppermute | solution.py:24
  83.8 2.2 %collective-permute-done.16 = bf16[64,896]{1,0:T(8,128)(2,1)S(1)} collective-permute-done((bf16[64,896]{1,0:T(8,128)(2,1)S(1)}, bf16[64,896]{1,0:T(8,128)(2,1)S(1)}, u32[]{:S(2)}, u32[]{:S(2)}) %collective-permute-start.16) | collective-permute-done | bytes 114720 | tf_op jit(solution)/shard_map/ppermute | solution.py:24
  86.0 2.6 %collective-permute-start.18 = (bf16[2,64,896]{2,1,0:T(8,128)(2,1)S(1)}, bf16[2,64,896]{2,1,0:T(8,128)(2,1)}, u32[]{:S(2)}, u32[]{:S(2)}) collective-permute-start(bf16[2,64,896]{2,1,0:T(8,128)(2,1)S(1)} %get-tuple-element.54), channel_id=1, source_target_pairs={{0,128},{64,192},{128,0},{192,64},{1,129},{65,193},{129,1},{193,65... | collective-permute-start | bytes 688136 | tf_op jit(solution)/shard_map/ppermute | solution.py:24
  88.6 1.6 collective-permute-start.19
  90.2 2.4 %collective-permute-done.18 = bf16[2,64,896]{2,1,0:T(8,128)(2,1)} collective-permute-done((bf16[2,64,896]{2,1,0:T(8,128)(2,1)S(1)}, bf16[2,64,896]{2,1,0:T(8,128)(2,1)}, u32[]{:S(2)}, u32[]{:S(2)}) %collective-permute-start.18) | collective-permute-done | bytes 229408 | tf_op jit(solution)/shard_map/ppermute | solution.py:24
  92.6 4.4 %collective-permute-done.17 = bf16[2,64,896]{2,1,0:T(8,128)(2,1)} collective-permute-done((bf16[2,64,896]{2,1,0:T(8,128)(2,1)S(1)}, bf16[2,64,896]{2,1,0:T(8,128)(2,1)}, u32[]{:S(2)}, u32[]{:S(2)}) %collective-permute-start.17) | collective-permute-done | bytes 229408 | tf_op jit(solution)/shard_map/ppermute | solution.py:24
  97.0 3.3 %convert_add_fusion = f32[4,2,64,1024]{3,2,1,0:T(8,128)S(1)} fusion(bf16[4,2,64,1024]{3,2,1,0:T(8,128)(2,1)} %collective-permute-done.25, bf16[896,1024]{1,0:T(8,128)(2,1)} %param.11, bf16[1,2,64,896]{3,2,1,0:T(8,128)(2,1)} %bitcast.53, bf16[1,2,64,896]{3,2,1,0:T(8,128)(2,1)} %bitcast.52, bf16[1,2,64,896]{3,2,1,0:T(8,128)(2,1)} %bitcast.51, ...), kind=kOutput, calls=%fused_computation.1 | convolution fusion | flops 941948928 | bytes 5898240 | tf_op jit(solution)/shard_map/dot_general | solution.py:72
  102.5 4.1 %collective-permute-start.31 = (bf16[8,8,1024]{2,1,0:T(8,128)(2,1)S(1)}, bf16[8,8,1024]{2,1,0:T(8,128)(2,1)S(1)}, u32[]{:S(2)}, u32[]{:S(2)}) collective-permute-start(bf16[8,8,1024]{2,1,0:T(8,128)(2,1)S(1)} %get-tuple-element.23), channel_id=1, source_target_pairs={{0,28},{4,0},{8,4},{12,8},{16,12},{20,16},{24,20},{28,24},{1,29},{... | collective-permute-start | bytes 393224 | tf_op jit(solution)/shard_map/ppermute | solution.py:20
  106.6 4.0 %collective-permute-start.26 = (bf16[8,8,1024]{2,1,0:T(8,128)(2,1)S(1)}, bf16[8,8,1024]{2,1,0:T(8,128)(2,1)S(1)}, u32[]{:S(2)}, u32[]{:S(2)}) collective-permute-start(bf16[8,8,1024]{2,1,0:T(8,128)(2,1)S(1)} %get-tuple-element.19), channel_id=1, source_target_pairs={{0,16},{4,20},{8,24},{12,28},{16,0},{20,4},{24,8},{28,12},{1,17},{... | collective-permute-start | bytes 393224 | tf_op jit(solution)/shard_map/ppermute | solution.py:20
  113.2 3.6 %collective-permute-start.32 = (bf16[8,8,1024]{2,1,0:T(8,128)(2,1)S(1)}, bf16[8,8,1024]{2,1,0:T(8,128)(2,1)S(1)}, u32[]{:S(2)}, u32[]{:S(2)}) collective-permute-start(bf16[8,8,1024]{2,1,0:T(8,128)(2,1)S(1)} %get-tuple-element.25), channel_id=1, source_target_pairs={{0,24},{4,28},{8,0},{12,4},{16,8},{20,12},{24,16},{28,20},{1,25},{... | collective-permute-start | bytes 393224 | tf_op jit(solution)/shard_map/ppermute | solution.py:20
  116.8 5.3 %collective-permute-done.30 = bf16[8,8,1024]{2,1,0:T(8,128)(2,1)S(1)} collective-permute-done((bf16[8,8,1024]{2,1,0:T(8,128)(2,1)S(1)}, bf16[8,8,1024]{2,1,0:T(8,128)(2,1)S(1)}, u32[]{:S(2)}, u32[]{:S(2)}) %collective-permute-start.30) | collective-permute-done | bytes 131104 | tf_op jit(solution)/shard_map/ppermute | solution.py:20
  122.1 1.8 collective-permute-done.32
  125.0 3.1 %collective-permute-start.33 = (bf16[8,8,1024]{2,1,0:T(8,128)(2,1)S(1)}, bf16[8,8,1024]{2,1,0:T(8,128)(2,1)S(1)}, u32[]{:S(2)}, u32[]{:S(2)}) collective-permute-start(bf16[8,8,1024]{2,1,0:T(8,128)(2,1)S(1)} %fusion.50), channel_id=1, source_target_pairs={{0,2},{2,0},{1,3},{3,1},{4,6},{6,4},{5,7},{7,5},{8,10},{10,8},{9,1... | collective-permute-start | bytes 393224 | tf_op jit(solution)/shard_map/ppermute | solution.py:20
  128.1 2.4 %collective-permute-done.33 = bf16[8,8,1024]{2,1,0:T(8,128)(2,1)S(1)} collective-permute-done((bf16[8,8,1024]{2,1,0:T(8,128)(2,1)S(1)}, bf16[8,8,1024]{2,1,0:T(8,128)(2,1)S(1)}, u32[]{:S(2)}, u32[]{:S(2)}) %collective-permute-start.33) | collective-permute-done | bytes 131104 | tf_op jit(solution)/shard_map/ppermute | solution.py:20
  131.6 13.2 %all_to_all.20 = f32[8,8,8]{2,1,0:T(8,128)S(1)} all-to-all(f32[8,8,8]{2,1,0:T(8,128)S(1)} %broadcast_in_dim.6), channel_id=1, replica_groups=mesh['x'=4,'y'=2,'z'=8,'w'=2,'c'=2] {'x','y'}, dimensions={0} | all-to-all | bytes 4096 | tf_op jit(solution)/shard_map/all_to_all | solution.py:148
  146.0 13.4 %all_to_all.21 = bf16[8,8,1024]{2,1,0:T(8,128)(2,1)S(1)} all-to-all(bf16[8,8,1024]{2,1,0:T(8,128)(2,1)S(1)} %broadcast_in_dim.7), channel_id=1, replica_groups=mesh['x'=4,'y'=2,'z'=8,'w'=2,'c'=2] {'z'}, dimensions={0} | all-to-all | bytes 262144 | tf_op jit(solution)/shard_map/all_to_all | solution.py:158
  159.4 7.1 %collective-permute-start.34 = (bf16[64,1024]{1,0:T(8,128)(2,1)S(1)}, bf16[64,1024]{1,0:T(8,128)(2,1)S(1)}, u32[]{:S(2)}, u32[]{:S(2)}) collective-permute-start(bf16[64,1024]{1,0:T(8,128)(2,1)S(1)} %bitcast.250), channel_id=1, source_target_pairs={{0,1},{1,0},{2,3},{3,2},{4,5},{5,4},{6,7},{7,6},{8,9},{9,8},{10,11... | collective-permute-start | bytes 393224 | tf_op jit(solution)/shard_map/ppermute | solution.py:24
  167.6 3.5 %convolution_convert_fusion = bf16[128,2688]{1,0:T(8,128)(2,1)S(1)} fusion(bf16[1024,2688]{1,0:T(8,128)(2,1)} %param.13, bf16[64,1024]{1,0:T(8,128)(2,1)S(1)} %get-tuple-element.52, bf16[64,1024]{1,0:T(8,128)(2,1)S(1)} %get-tuple-element.51), kind=kOutput, calls=%fused_computation | convolution fusion | flops 705511424 | bytes 6455296 | tf_op jit(solution)/shard_map/dot_general | solution.py:164
  171.1 13.5 %all_to_all.22 = bf16[8,16,2688]{2,1,0:T(8,128)(2,1)S(1)} all-to-all(bf16[8,16,2688]{2,1,0:T(8,128)(2,1)S(1)} %bitcast.235), channel_id=1, replica_groups=mesh['x'=4,'y'=2,'z'=8,'w'=2,'c'=2] {'x','y'}, dimensions={0} | all-to-all | bytes 1376256 | tf_op jit(solution)/shard_map/all_to_all | solution.py:166
  185.1 15.1 %all_to_all.23 = f32[32,1,16]{2,1,0:T(1,128)S(1)} all-to-all(f32[32,1,16]{2,1,0:T(1,128)S(1)} %broadcast_in_dim.8), channel_id=1, replica_groups=mesh['x'=4,'y'=2,'z'=8,'w'=2,'c'=2] {'z','w','c'}, dimensions={0} | all-to-all | bytes 4096 | tf_op jit(solution)/shard_map/all_to_all | solution.py:171
  (133 shorter events, 41.6 us)
Async XLA Ops:
  5.1 8.5 %collective-permute-start.2 = (bf16[64,1024]{1,0:T(8,128)(2,1)S(1)}, bf16[64,1024]{1,0:T(8,128)(2,1)S(1)}, u32[]{:S(2)}, u32[]{:S(2)}) collective-permute-start(bf16[64,1024]{1,0:T(8,128)(2,1)S(1)} %get-tuple-element.34), channel_id=1, source_target_pairs={{0,96},{32,64},{64,32},{96,0},{128,224},{160,192},{192,160},{224,1... | collective-permute-start | bytes 393224 | tf_op jit(solution)/shard_map/ppermute | solution.py:32
  8.3 6.8 %collective-permute-start.1 = (bf16[64,1024]{1,0:T(8,128)(2,1)S(1)}, bf16[64,1024]{1,0:T(8,128)(2,1)S(1)}, u32[]{:S(2)}, u32[]{:S(2)}) collective-permute-start(bf16[64,1024]{1,0:T(8,128)(2,1)S(1)} %get-tuple-element.35), channel_id=1, source_target_pairs={{0,64},{32,96},{64,0},{96,32},{128,192},{160,224},{192,128},{224,1... | collective-permute-start | bytes 393224 | tf_op jit(solution)/shard_map/ppermute | solution.py:32
  8.5 6.9 %collective-permute-start.6 = (bf16[64,1024]{1,0:T(8,128)(2,1)S(1)}, bf16[64,1024]{1,0:T(8,128)(2,1)S(1)}, u32[]{:S(2)}, u32[]{:S(2)}) collective-permute-start(bf16[64,1024]{1,0:T(8,128)(2,1)S(1)} %get-tuple-element.30), channel_id=1, source_target_pairs={{0,224},{32,192},{64,160},{96,128},{128,96},{160,64},{192,32},{224... | collective-permute-start | bytes 393224 | tf_op jit(solution)/shard_map/ppermute | solution.py:32
  10.9 6.0 %collective-permute-start.5 = (bf16[64,1024]{1,0:T(8,128)(2,1)S(1)}, bf16[64,1024]{1,0:T(8,128)(2,1)S(1)}, u32[]{:S(2)}, u32[]{:S(2)}) collective-permute-start(bf16[64,1024]{1,0:T(8,128)(2,1)S(1)} %get-tuple-element.31), channel_id=1, source_target_pairs={{0,192},{32,224},{64,128},{96,160},{128,64},{160,96},{192,0},{224,... | collective-permute-start | bytes 393224 | tf_op jit(solution)/shard_map/ppermute | solution.py:32
  11.0 11.1 %collective-permute-start.4 = (bf16[64,1024]{1,0:T(8,128)(2,1)S(1)}, bf16[64,1024]{1,0:T(8,128)(2,1)S(1)}, u32[]{:S(2)}, u32[]{:S(2)}) collective-permute-start(bf16[64,1024]{1,0:T(8,128)(2,1)S(1)} %get-tuple-element.32), channel_id=1, source_target_pairs={{0,160},{32,128},{64,224},{96,192},{128,32},{160,0},{192,96},{224,... | collective-permute-start | bytes 393224 | tf_op jit(solution)/shard_map/ppermute | solution.py:32
  13.6 8.5 %collective-permute-start.3 = (bf16[64,1024]{1,0:T(8,128)(2,1)S(1)}, bf16[64,1024]{1,0:T(8,128)(2,1)S(1)}, u32[]{:S(2)}, u32[]{:S(2)}) collective-permute-start(bf16[64,1024]{1,0:T(8,128)(2,1)S(1)} %get-tuple-element.33), channel_id=1, source_target_pairs={{0,128},{32,160},{64,192},{96,224},{128,0},{160,32},{192,64},{224,... | collective-permute-start | bytes 393224 | tf_op jit(solution)/shard_map/ppermute | solution.py:32
  15.1 5.9 %collective-permute-start = (bf16[64,1024]{1,0:T(8,128)(2,1)S(1)}, bf16[64,1024]{1,0:T(8,128)(2,1)S(1)}, u32[]{:S(2)}, u32[]{:S(2)}) collective-permute-start(bf16[64,1024]{1,0:T(8,128)(2,1)S(1)} %get-tuple-element.36), channel_id=1, source_target_pairs={{0,32},{32,0},{64,96},{96,64},{128,160},{160,128},{192,224},{224,1... | collective-permute-start | bytes 393224 | tf_op jit(solution)/shard_map/ppermute | solution.py:32
  18.6 18.7 %collective-permute-start.9 = (bf16[2,2,64,896]{3,2,1,0:T(8,128)(2,1)S(1)}, bf16[2,2,64,896]{3,2,1,0:T(8,128)(2,1)S(1)}, u32[]{:S(2)}, u32[]{:S(2)}) collective-permute-start(bf16[2,2,64,896]{3,2,1,0:T(8,128)(2,1)S(1)} %pad_maximum_fusion.4), channel_id=1, source_target_pairs={{0,64},{64,0},{128,192},{192,128},{1,65},{65,1},{129,193},{193,129... | collective-permute-start | bytes 1376264 | tf_op jit(solution)/shard_map/ppermute | solution.py:24
  22.2 8.3 %collective-permute-start.7 = (bf16[8,64,1024]{2,1,0:T(8,128)(2,1)S(1)}, bf16[8,64,1024]{2,1,0:T(8,128)(2,1)S(1)}, u32[]{:S(2)}, u32[]{:S(2)}) collective-permute-start(bf16[8,64,1024]{2,1,0:T(8,128)(2,1)S(1)} %constant_dynamic-update-slice_fusion), channel_id=1, source_target_pairs={{0,1},{1,0},{2,3},{3,2},{4,5},{5,4},{6,7},{7,6},{8,9},{9,8},{10,11... | collective-permute-start | bytes 3145736 | tf_op jit(solution)/shard_map/ppermute | solution.py:24
  27.1 23.2 %collective-permute-start.10 = (bf16[2,2,64,896]{3,2,1,0:T(8,128)(2,1)S(1)}, bf16[2,2,64,896]{3,2,1,0:T(8,128)(2,1)S(1)}, u32[]{:S(2)}, u32[]{:S(2)}) collective-permute-start(bf16[2,2,64,896]{3,2,1,0:T(8,128)(2,1)S(1)} %pad_maximum_fusion.5), channel_id=1, source_target_pairs={{0,192},{64,128},{128,64},{192,0},{1,193},{65,129},{129,65},{193,1... | collective-permute-start | bytes 1376264 | tf_op jit(solution)/shard_map/ppermute | solution.py:24
  33.2 17.1 %collective-permute-start.11 = (bf16[2,3,64,896]{3,2,1,0:T(8,128)(2,1)S(1)}, bf16[2,3,64,896]{3,2,1,0:T(8,128)(2,1)S(1)}, u32[]{:S(2)}, u32[]{:S(2)}) collective-permute-start(bf16[2,3,64,896]{3,2,1,0:T(8,128)(2,1)S(1)} %pad_maximum_fusion.1), channel_id=1, source_target_pairs={{0,32},{32,0},{1,33},{33,1},{2,34},{34,2},{3,35},{35,3},{4,36},{36... | collective-permute-start | bytes 2064392 | tf_op jit(solution)/shard_map/ppermute | solution.py:24
  34.6 15.7 %collective-permute-start.8 = (bf16[2,2,64,896]{3,2,1,0:T(8,128)(2,1)S(1)}, bf16[2,2,64,896]{3,2,1,0:T(8,128)(2,1)S(1)}, u32[]{:S(2)}, u32[]{:S(2)}) collective-permute-start(bf16[2,2,64,896]{3,2,1,0:T(8,128)(2,1)S(1)} %pad_maximum_fusion.3), channel_id=1, source_target_pairs={{0,128},{64,192},{128,0},{192,64},{1,129},{65,193},{129,1},{193,65... | collective-permute-start | bytes 1376264 | tf_op jit(solution)/shard_map/ppermute | solution.py:24
  36.5 45.5 %collective-permute-start.15 = (bf16[2,64,896]{2,1,0:T(8,128)(2,1)S(1)}, bf16[2,64,896]{2,1,0:T(8,128)(2,1)S(1)}, u32[]{:S(2)}, u32[]{:S(2)}) collective-permute-start(bf16[2,64,896]{2,1,0:T(8,128)(2,1)S(1)} %pad_maximum_fusion.12), channel_id=1, source_target_pairs={{0,32},{32,0},{1,33},{33,1},{2,34},{34,2},{3,35},{35,3},{4,36},{36... | collective-permute-start | bytes 688136 | tf_op jit(solution)/shard_map/ppermute | solution.py:24
  50.6 9.2 %collective-permute-start.20 = (bf16[2,64,896]{2,1,0:T(8,128)(2,1)S(1)}, bf16[2,64,896]{2,1,0:T(8,128)(2,1)S(1)}, u32[]{:S(2)}, u32[]{:S(2)}) collective-permute-start(bf16[2,64,896]{2,1,0:T(8,128)(2,1)S(1)} %pad_maximum_fusion.14), channel_id=1, source_target_pairs={{0,32},{32,0},{1,33},{33,1},{2,34},{34,2},{3,35},{35,3},{4,36},{36... | collective-permute-start | bytes 688136 | tf_op jit(solution)/shard_map/ppermute | solution.py:24
  61.3 5.2 %collective-permute-start.22 = (bf16[64,896]{1,0:T(8,128)(2,1)S(1)}, bf16[64,896]{1,0:T(8,128)(2,1)S(1)}, u32[]{:S(2)}, u32[]{:S(2)}) collective-permute-start(bf16[64,896]{1,0:T(8,128)(2,1)S(1)} %fusion.51), channel_id=1, source_target_pairs={{0,128},{64,192},{128,0},{192,64},{1,129},{65,193},{129,1},{193,65... | collective-permute-start | bytes 344072 | tf_op jit(solution)/shard_map/ppermute | solution.py:24
  67.7 9.9 %collective-permute-start.24 = (bf16[4,64,896]{2,1,0:T(8,128)(2,1)S(1)}, bf16[4,64,896]{2,1,0:T(8,128)(2,1)S(1)}, u32[]{:S(2)}, u32[]{:S(2)}) collective-permute-start(bf16[4,64,896]{2,1,0:T(8,128)(2,1)S(1)} %get-tuple-element.40), channel_id=1, source_target_pairs={{0,32},{32,0},{1,33},{33,1},{2,34},{34,2},{3,35},{35,3},{4,36},{36... | collective-permute-start | bytes 1376264 | tf_op jit(solution)/shard_map/ppermute | solution.py:24
  69.1 12.9 %collective-permute-start.13 = (bf16[2,64,896]{2,1,0:T(8,128)(2,1)S(1)}, bf16[2,64,896]{2,1,0:T(8,128)(2,1)S(1)}, u32[]{:S(2)}, u32[]{:S(2)}) collective-permute-start(bf16[2,64,896]{2,1,0:T(8,128)(2,1)S(1)} %pad_maximum_fusion.10), channel_id=1, source_target_pairs={{0,64},{64,0},{128,192},{192,128},{1,65},{65,1},{129,193},{193,129... | collective-permute-start | bytes 688136 | tf_op jit(solution)/shard_map/ppermute | solution.py:24
  70.4 11.7 %collective-permute-start.14 = (bf16[2,64,896]{2,1,0:T(8,128)(2,1)S(1)}, bf16[2,64,896]{2,1,0:T(8,128)(2,1)S(1)}, u32[]{:S(2)}, u32[]{:S(2)}) collective-permute-start(bf16[2,64,896]{2,1,0:T(8,128)(2,1)S(1)} %pad_maximum_fusion.11), channel_id=1, source_target_pairs={{0,192},{64,128},{128,64},{192,0},{1,193},{65,129},{129,65},{193,1... | collective-permute-start | bytes 688136 | tf_op jit(solution)/shard_map/ppermute | solution.py:24
  71.3 10.8 %collective-permute-start.12 = (bf16[2,64,896]{2,1,0:T(8,128)(2,1)S(1)}, bf16[2,64,896]{2,1,0:T(8,128)(2,1)S(1)}, u32[]{:S(2)}, u32[]{:S(2)}) collective-permute-start(bf16[2,64,896]{2,1,0:T(8,128)(2,1)S(1)} %pad_maximum_fusion.9), channel_id=1, source_target_pairs={{0,128},{64,192},{128,0},{192,64},{1,129},{65,193},{129,1},{193,65... | collective-permute-start | bytes 688136 | tf_op jit(solution)/shard_map/ppermute | solution.py:24
  78.8 18.2 %collective-permute-start.25 = (bf16[4,2,64,1024]{3,2,1,0:T(8,128)(2,1)S(1)}, bf16[4,2,64,1024]{3,2,1,0:T(8,128)(2,1)}, u32[]{:S(2)}, u32[]{:S(2)}) collective-permute-start(bf16[4,2,64,1024]{3,2,1,0:T(8,128)(2,1)S(1)} %fusion.18), channel_id=1, source_target_pairs={{0,1},{1,0},{2,3},{3,2},{4,5},{5,4},{6,7},{7,6},{8,9},{9,8},{10,11... | collective-permute-start | bytes 3145736 | tf_op jit(solution)/shard_map/ppermute | solution.py:24
  86.0 6.6 %collective-permute-start.18 = (bf16[2,64,896]{2,1,0:T(8,128)(2,1)S(1)}, bf16[2,64,896]{2,1,0:T(8,128)(2,1)}, u32[]{:S(2)}, u32[]{:S(2)}) collective-permute-start(bf16[2,64,896]{2,1,0:T(8,128)(2,1)S(1)} %get-tuple-element.54), channel_id=1, source_target_pairs={{0,128},{64,192},{128,0},{192,64},{1,129},{65,193},{129,1},{193,65... | collective-permute-start | bytes 688136 | tf_op jit(solution)/shard_map/ppermute | solution.py:24
  88.6 8.4 %collective-permute-start.17 = (bf16[2,64,896]{2,1,0:T(8,128)(2,1)S(1)}, bf16[2,64,896]{2,1,0:T(8,128)(2,1)}, u32[]{:S(2)}, u32[]{:S(2)}) collective-permute-start(bf16[2,64,896]{2,1,0:T(8,128)(2,1)S(1)} %get-tuple-element.54), channel_id=1, source_target_pairs={{0,64},{64,0},{128,192},{192,128},{1,65},{65,1},{129,193},{193,129... | collective-permute-start | bytes 688136 | tf_op jit(solution)/shard_map/ppermute | solution.py:24
  88.6 8.4 %collective-permute-start.19 = (bf16[2,64,896]{2,1,0:T(8,128)(2,1)S(1)}, bf16[2,64,896]{2,1,0:T(8,128)(2,1)}, u32[]{:S(2)}, u32[]{:S(2)}) collective-permute-start(bf16[2,64,896]{2,1,0:T(8,128)(2,1)S(1)} %get-tuple-element.54), channel_id=1, source_target_pairs={{0,192},{64,128},{128,64},{192,0},{1,193},{65,129},{129,65},{193,1... | collective-permute-start | bytes 688136 | tf_op jit(solution)/shard_map/ppermute | solution.py:24
  101.7 10.3 %collective-permute-start.29 = (bf16[8,8,1024]{2,1,0:T(8,128)(2,1)S(1)}, bf16[8,8,1024]{2,1,0:T(8,128)(2,1)S(1)}, u32[]{:S(2)}, u32[]{:S(2)}) collective-permute-start(bf16[8,8,1024]{2,1,0:T(8,128)(2,1)S(1)} %get-tuple-element.20), channel_id=1, source_target_pairs={{0,4},{4,8},{8,12},{12,16},{16,20},{20,24},{24,28},{28,0},{1,5},{5... | collective-permute-start | bytes 393224 | tf_op jit(solution)/shard_map/ppermute | solution.py:20
  102.5 9.5 %collective-permute-start.31 = (bf16[8,8,1024]{2,1,0:T(8,128)(2,1)S(1)}, bf16[8,8,1024]{2,1,0:T(8,128)(2,1)S(1)}, u32[]{:S(2)}, u32[]{:S(2)}) collective-permute-start(bf16[8,8,1024]{2,1,0:T(8,128)(2,1)S(1)} %get-tuple-element.23), channel_id=1, source_target_pairs={{0,28},{4,0},{8,4},{12,8},{16,12},{20,16},{24,20},{28,24},{1,29},{... | collective-permute-start | bytes 393224 | tf_op jit(solution)/shard_map/ppermute | solution.py:20
  106.6 10.2 %collective-permute-start.26 = (bf16[8,8,1024]{2,1,0:T(8,128)(2,1)S(1)}, bf16[8,8,1024]{2,1,0:T(8,128)(2,1)S(1)}, u32[]{:S(2)}, u32[]{:S(2)}) collective-permute-start(bf16[8,8,1024]{2,1,0:T(8,128)(2,1)S(1)} %get-tuple-element.19), channel_id=1, source_target_pairs={{0,16},{4,20},{8,24},{12,28},{16,0},{20,4},{24,8},{28,12},{1,17},{... | collective-permute-start | bytes 393224 | tf_op jit(solution)/shard_map/ppermute | solution.py:20
  110.6 6.2 %collective-permute-start.28 = (bf16[8,8,1024]{2,1,0:T(8,128)(2,1)S(1)}, bf16[8,8,1024]{2,1,0:T(8,128)(2,1)S(1)}, u32[]{:S(2)}, u32[]{:S(2)}) collective-permute-start(bf16[8,8,1024]{2,1,0:T(8,128)(2,1)S(1)} %get-tuple-element.21), channel_id=1, source_target_pairs={{0,28},{4,0},{8,4},{12,8},{16,12},{20,16},{24,20},{28,24},{1,29},{... | collective-permute-start | bytes 393224 | tf_op jit(solution)/shard_map/ppermute | solution.py:20
  110.6 6.2 %collective-permute-start.27 = (bf16[8,8,1024]{2,1,0:T(8,128)(2,1)S(1)}, bf16[8,8,1024]{2,1,0:T(8,128)(2,1)S(1)}, u32[]{:S(2)}, u32[]{:S(2)}) collective-permute-start(bf16[8,8,1024]{2,1,0:T(8,128)(2,1)S(1)} %get-tuple-element.22), channel_id=1, source_target_pairs={{0,4},{4,8},{8,12},{12,16},{16,20},{20,24},{24,28},{28,0},{1,5},{5... | collective-permute-start | bytes 393224 | tf_op jit(solution)/shard_map/ppermute | solution.py:20
  113.2 8.9 %collective-permute-start.30 = (bf16[8,8,1024]{2,1,0:T(8,128)(2,1)S(1)}, bf16[8,8,1024]{2,1,0:T(8,128)(2,1)S(1)}, u32[]{:S(2)}, u32[]{:S(2)}) collective-permute-start(bf16[8,8,1024]{2,1,0:T(8,128)(2,1)S(1)} %get-tuple-element.24), channel_id=1, source_target_pairs={{0,8},{4,12},{8,16},{12,20},{16,24},{20,28},{24,0},{28,4},{1,9},{5... | collective-permute-start | bytes 393224 | tf_op jit(solution)/shard_map/ppermute | solution.py:20
  113.2 10.7 %collective-permute-start.32 = (bf16[8,8,1024]{2,1,0:T(8,128)(2,1)S(1)}, bf16[8,8,1024]{2,1,0:T(8,128)(2,1)S(1)}, u32[]{:S(2)}, u32[]{:S(2)}) collective-permute-start(bf16[8,8,1024]{2,1,0:T(8,128)(2,1)S(1)} %get-tuple-element.25), channel_id=1, source_target_pairs={{0,24},{4,28},{8,0},{12,4},{16,8},{20,12},{24,16},{28,20},{1,25},{... | collective-permute-start | bytes 393224 | tf_op jit(solution)/shard_map/ppermute | solution.py:20
  125.0 5.5 %collective-permute-start.33 = (bf16[8,8,1024]{2,1,0:T(8,128)(2,1)S(1)}, bf16[8,8,1024]{2,1,0:T(8,128)(2,1)S(1)}, u32[]{:S(2)}, u32[]{:S(2)}) collective-permute-start(bf16[8,8,1024]{2,1,0:T(8,128)(2,1)S(1)} %fusion.50), channel_id=1, source_target_pairs={{0,2},{2,0},{1,3},{3,1},{4,6},{6,4},{5,7},{7,5},{8,10},{10,8},{9,1... | collective-permute-start | bytes 393224 | tf_op jit(solution)/shard_map/ppermute | solution.py:20
  159.4 8.1 %collective-permute-start.34 = (bf16[64,1024]{1,0:T(8,128)(2,1)S(1)}, bf16[64,1024]{1,0:T(8,128)(2,1)S(1)}, u32[]{:S(2)}, u32[]{:S(2)}) collective-permute-start(bf16[64,1024]{1,0:T(8,128)(2,1)S(1)} %bitcast.250), channel_id=1, source_target_pairs={{0,1},{1,0},{2,3},{3,2},{4,5},{5,4},{6,7},{7,6},{8,9},{9,8},{10,11... | collective-permute-start | bytes 393224 | tf_op jit(solution)/shard_map/ppermute | solution.py:24
  (11 other events, 158.2 us)

commit v3 on v1

--- a/solution.py
+++ b/solution.py
@@ -1,6 +1,7 @@
 import jax
 import jax.numpy as jnp
 from jax import lax
+from jax.experimental import pallas as pl
 from jax.sharding import Mesh
 from jax.sharding import PartitionSpec as P
 
@@ -22,25 +23,33 @@
     return lax.ppermute(array, axis, [(i, i ^ bit) for i in range(size)])
 
 
-def flipped_if(bit, array, axis):
-    return jnp.where(bit == 0, array, jnp.flip(array, axis))
-
-
 def wide(array):
     return array.astype(F32)
 
 
-def tokens_for_block(tokens, x, y, c):
-    half = tokens.shape[0] // NC
-    share = D // (NX * NY)
-    mine = lax.dynamic_slice_in_dim(tokens, c * half, half, 0)
-    blocks = mine.reshape(half, NX * NY, share).transpose(1, 0, 2)
-    own = lax.all_to_all(blocks, PROMPT, 0, 0, tiled=True)
-    own = own.reshape(2, 2, NY, half, share)
-    for axis, bit in enumerate((x // 2, x % 2, y)):
-        own = flipped_if(bit, own, axis)
-    own = lax.optimization_barrier(own.reshape(NX, NY, half, share))
-    return own, paired(own, "c", NC, 1)
+def paired_prompt(array, k):
+    return lax.ppermute(array, PROMPT, [(p, p ^ k) for p in range(NX * NY)])
+
+
+def blocks_kernel(tokens_ref, *out_refs):
+    place = lax.axis_index("x") * NY + lax.axis_index("y")
+    half, share = out_refs[0].shape
+    first = pl.multiple_of(lax.axis_index("c") * half, half)
+    for k, out_ref in enumerate(out_refs):
+        start = pl.multiple_of((place ^ k) * share, share)
+        out_ref[...] = tokens_ref[pl.ds(first, half), pl.ds(start, share)]
+
+
+def tokens_for_block(tokens):
+    count = NX * NY
+    block = jax.ShapeDtypeStruct((tokens.shape[0] // NC, D // count), tokens.dtype)
+    own = pl.pallas_call(blocks_kernel, out_shape=[block] * count)(tokens)
+    own = list(own)
+    for k in (4, 5, 2, 3, 6, 7, 1):
+        own[k] = paired_prompt(own[k], k)
+    own = jnp.stack(own)
+    other = paired(own, "c", NC, 1)
+    return [rows.reshape(NX, NY, *block.shape) for rows in (own, other)]
 
 
 def at(array, index, axis):
@@ -60,14 +69,14 @@
 def step(tokens, gate_weight, up_weight, down_weight, norm_gain, unembed, guidance, logit_bias):
     x, y, z, _, c = (lax.axis_index(axis) for axis in AXES)
     tokens = tokens[0]
-    own, other = tokens_for_block(tokens, x, y, c)
+    own, other = tokens_for_block(tokens)
     both = (gate_weight, up_weight)
 
-    pa = products(own, both)
-    got_a = [paired(joined([p[d] for p in pa]), "x", NX, d) for d in TURNS]
-    pb = products(other, both)
+    pb = products(own, both)
     swap_b = paired(joined([p[:, 1] for p in pb]), "y", NY, 1)
-    got_a, swap_b = lax.optimization_barrier((got_a, swap_b))
+    pa = products(other, both)
+    packed_a = [joined([p[d] for p in pa]) for d in TURNS]
+    got_a = [paired(packed, "x", NX, d) for d, packed in zip(TURNS, packed_a)]
     sum_a = [p[0] + sum(wide(got[i]) for got in got_a) for i, p in enumerate(pa)]
     swap_a = paired(joined([p[1] for p in sum_a]), "y", NY, 1)
     sum_b = [p[:, 0] + wide(got) for p, got in zip(pb, swap_b)]
@@ -91,7 +100,7 @@
     (down_a,) = products(all_a, (down_weight,))
     passed = paired(down_a.astype(BF), "c", NC, 1)
     (down_b,) = products(all_b, (down_weight,))
-    part = down_b + wide(passed)
+    part = (down_b + wide(passed)).astype(BF)
     share = part.shape[-1]
     part = part.reshape(NX * NY, NZ, -1, share)
 
@@ -104,13 +113,13 @@
     far = sent(piece(4), 4)
     relay_up, relay_down = sent(piece(3), 1), sent(piece(5), -1)
     one_up, one_down = sent(piece(1), 1), sent(piece(7), -1)
-    two_up = sent(piece(2) + wide(relay_up), 2)
-    two_down = sent(piece(6) + wide(relay_down), -2)
-    mine = piece(0) + sum(wide(got) for got in (far, one_up, one_down, two_up, two_down))
+    two_up = sent(wide(piece(2)) + wide(relay_up), 2)
+    two_down = sent(wide(piece(6)) + wide(relay_down), -2)
+    mine = wide(piece(0)) + sum(wide(got) for got in (far, one_up, one_down, two_up, two_down))
     mine = mine.astype(BF)
     branch = wide(mine) + wide(shifted(mine, "w", NW, 1))
 
-    residual = at(other.reshape(NX * NY, NZ, -1, share), z, 1)
+    residual = at(own.reshape(NX * NY, NZ, -1, share), z, 1)
     state = wide(residual) + branch
     partial_square = jnp.sum(state * state, axis=2)
     offsets = jnp.arange(NX * NY)
@@ -126,14 +135,11 @@
     scale = jnp.sum(placed_at[:, :, None] * scale[:, None], axis=0)
     mixed = (jnp.sum(state * scale[:, :, None], axis=0) * norm_gain).astype(BF)
 
-    ring = mixed
-    for bit in (1, 2, 4):
-        peer = paired(ring, "z", NZ, bit)
-        low = (z & bit) == 0
-        ring = jnp.concatenate([jnp.where(low, ring, peer), jnp.where(low, peer, ring)])
+    ring = jnp.broadcast_to(mixed[None], (NZ, *mixed.shape))
+    ring = lax.all_to_all(ring, "z", 0, 0, tiled=True).reshape(-1, share)
     peer = paired(ring, "c", NC, 1)
-    first = jnp.where(c == 0, peer, ring)
-    second = jnp.where(c == 0, ring, peer)
+    first = jnp.where(c == 0, ring, peer)
+    second = jnp.where(c == 0, peer, ring)
     rows = jnp.concatenate([first, second])
 
     product = jnp.dot(rows, unembed, preferred_element_type=F32).astype(BF)
@@ -152,6 +158,7 @@
 
 
 TURNS = (2, 1, 3)
+TURNS = (2, 1, 3)
 
 
 def solution(mesh):

time: 212 us -> 203 us (0.958)
  waiting for transfers between devices: 82.5 us -> 71.3 us
  blocking collectives: 41.4 us -> 49.9 us
  other arithmetic: 8.14 us -> 3.51 us
  starting transfers between devices: 58.9 us -> 54.4 us
  Pallas kernels: 0 us -> 2.74 us
    all_to_all x1 -> x0, waiting for transfers between devices: 15.3 us -> none  [tokens_for_block(): own = lax.all_to_all(blocks, PROMPT, 0, 0, tiled=True)]
    all_to_all x0 -> x1, blocking collectives: none -> 13.8 us  [step(): ring = lax.all_to_all(ring, 'z', 0, 0, tiled=True).reshape(-1, share)]
    ppermute x22 -> x19, starting transfers between devices: 36.5 us -> 25.9 us  [paired(): return lax.ppermute(array, axis, [(i, i ^ bit) for i in range(size)])]
    ppermute x0 -> x7, starting transfers between devices: none -> 10 us  [paired_prompt(): return lax.ppermute(array, PROMPT, [(p, p ^ k) for p in range(NX * NY)])]
    ppermute x0 -> x7, waiting for transfers between devices: none -> 7.34 us  [paired_prompt(): return lax.ppermute(array, PROMPT, [(p, p ^ k) for p in range(NX * NY)])]
    all_to_all x1 -> x0, starting transfers between devices: 5.85 us -> none  [tokens_for_block(): own = lax.all_to_all(blocks, PROMPT, 0, 0, tiled=True)]
    all_to_all x1, blocking collectives: 18.6 us -> 15.2 us  [step(): lax.all_to_all(jnp.broadcast_to(part_lse[None, None], (shards, 1, part_ls...]
    unnamed x19 -> x28, local copies, waits for them, and re-layouts: 3.72 us -> 6.52 us
  transfers between devices with their start and end apart: 31 -> 34, of which waited for: 18 -> 20; matrix products, arithmetic and copies ran while one was open for 3% -> 8% of each run, Pallas kernels for 0% -> 0%
where the time goes in v3:
time: 203 us; the launch traced here: 202 us
  waiting for transfers between devices  71.3 us (35%)
  starting transfers between devices  54.4 us (27%)
  blocking collectives  49.9 us (25%)
  matrix products  12.4 us (6%)
  local copies, waits for them, and re-layouts  7.65 us (4%)
  other arithmetic  3.51 us (2%)
  Pallas kernels  2.74 us (1%)
    ppermute x19, waiting for transfers between devices, paired(): return lax.ppermute(array, axis, [(i, i ^ bit) for i in range(size)])  53.6 us
    ppermute x19, starting transfers between devices, paired(): return lax.ppermute(array, axis, [(i, i ^ bit) for i in range(size)])  25.9 us
    ppermute x8, starting transfers between devices, shifted(): lax.ppermute(array, axis, [(i, (i + step) % size) for i in range(size)])  18.5 us
    all_to_all x1, blocking collectives, step(): lax.all_to_all(jnp.broadcast_to(part_lse[None, None], (shards, 1, part_ls...  15.2 us
    all_to_all x1, blocking collectives, step(): ring = lax.all_to_all(ring, 'z', 0, 0, tiled=True).reshape(-1, share)  13.8 us
    all_to_all x1, blocking collectives, step(): tiles = lax.all_to_all(tiles, PROMPT, 0, 0, tiled=True)  13.5 us
    ppermute x8, waiting for transfers between devices, shifted(): lax.ppermute(array, axis, [(i, (i + step) % size) for i in range(size)])  10.3 us
    ppermute x7, starting transfers between devices, paired_prompt(): return lax.ppermute(array, PROMPT, [(p, p ^ k) for p in range(NX * NY)])  10 us
  transfers between devices with their start and end apart: 34, of which 20 were waited for; matrix products, arithmetic and copies ran while one was open for 8% of the time, Pallas kernels for 0%

profile of v3, /device:TPU:1, one launch (start us, length us, event | category | flops | bytes accessed | tf_op | source)
XLA Modules:
  0.0 202.4 jit_solution(7101954859400620437)
XLA Ops:
  0.0 2.7 %shard_map.82 = (bf16[64,1024]{1,0:T(8,128)(2,1)}, bf16[64,1024]{1,0:T(8,128)(2,1)}, bf16[64,1024]{1,0:T(8,128)(2,1)}, bf16[64,1024]{1,0:T(8,128)(2,1)}, bf16[64...) custom-call(bf16[128,8192]{1,0:T(8,128)(2,1)} %bitcast.182), custom_call_target="tpu_custom_call" | custom-call | tf_op jit(solution)/shard_map/pallas_call | solution.py:46
  6.1 2.9 %collective-permute-start.3 = (bf16[64,1024]{1,0:T(8,128)(2,1)}, bf16[64,1024]{1,0:T(8,128)(2,1)S(1)}, u32[]{:S(2)}, u32[]{:S(2)}) collective-permute-start(bf16[64,1024]{1,0:T(8,128)(2,1)} %get-tuple-element.17), channel_id=1, source_target_pairs={{0,128},{32,160},{64,192},{96,224},{128,0},{160,32},{192,64},{224,... | collective-permute-start | bytes 393224 | tf_op jit(solution)/shard_map/ppermute | solution.py:31
  12.8 2.6 %collective-permute-start.5 = (bf16[64,1024]{1,0:T(8,128)(2,1)}, bf16[64,1024]{1,0:T(8,128)(2,1)S(1)}, u32[]{:S(2)}, u32[]{:S(2)}) collective-permute-start(bf16[64,1024]{1,0:T(8,128)(2,1)} %get-tuple-element.19), channel_id=1, source_target_pairs={{0,192},{32,224},{64,128},{96,160},{128,64},{160,96},{192,0},{224,... | collective-permute-start | bytes 393224 | tf_op jit(solution)/shard_map/ppermute | solution.py:31
  20.5 3.3 %collective-permute-done.5 = bf16[64,1024]{1,0:T(8,128)(2,1)S(1)} collective-permute-done((bf16[64,1024]{1,0:T(8,128)(2,1)}, bf16[64,1024]{1,0:T(8,128)(2,1)S(1)}, u32[]{:S(2)}, u32[]{:S(2)}) %collective-permute-start.5) | collective-permute-done | bytes 131104 | tf_op jit(solution)/shard_map/ppermute | solution.py:31
  27.8 2.6 %fusion = f32[4,2,64,896]{3,2,1,0:T(8,128)S(1)} fusion(bf16[4,2,64,1024]{3,2,1,0:T(8,128)(2,1)} %bitcast.200, bf16[1024,896]{1,0:T(8,128)(2,1)S(1)} %copy-done), kind=kOutput, calls=%fused_computation.2 | convolution fusion | flops 939524096 | bytes 4718592 | tf_op jit(solution)/shard_map/dot_general | solution.py:61
  37.0 2.5 %collective-permute-start.18 = (bf16[2,2,64,896]{3,2,1,0:T(8,128)(2,1)S(1)}, bf16[2,2,64,896]{3,2,1,0:T(8,128)(2,1)S(1)}, u32[]{:S(2)}, u32[]{:S(2)}) collective-permute-start(bf16[2,2,64,896]{3,2,1,0:T(8,128)(2,1)S(1)} %pad_maximum_fusion.4), channel_id=1, source_target_pairs={{0,192},{64,128},{128,64},{192,0},{1,193},{65,129},{129,65},{193,1... | collective-permute-start | bytes 1376264 | tf_op jit(solution)/shard_map/ppermute | solution.py:23
  39.7 9.7 %collective-permute-done.16 = bf16[2,2,64,896]{3,2,1,0:T(8,128)(2,1)S(1)} collective-permute-done((bf16[2,2,64,896]{3,2,1,0:T(8,128)(2,1)S(1)}, bf16[2,2,64,896]{3,2,1,0:T(8,128)(2,1)S(1)}, u32[]{:S(2)}, u32[]{:S(2)}) %collective-permute-start.16) | collective-permute-done | bytes 458784 | tf_op jit(solution)/shard_map/ppermute | solution.py:23
  49.4 7.7 %collective-permute-done.17 = bf16[2,2,64,896]{3,2,1,0:T(8,128)(2,1)S(1)} collective-permute-done((bf16[2,2,64,896]{3,2,1,0:T(8,128)(2,1)S(1)}, bf16[2,2,64,896]{3,2,1,0:T(8,128)(2,1)S(1)}, u32[]{:S(2)}, u32[]{:S(2)}) %collective-permute-start.17) | collective-permute-done | bytes 458784 | tf_op jit(solution)/shard_map/ppermute | solution.py:23
  57.1 2.8 %collective-permute-done.18 = bf16[2,2,64,896]{3,2,1,0:T(8,128)(2,1)S(1)} collective-permute-done((bf16[2,2,64,896]{3,2,1,0:T(8,128)(2,1)S(1)}, bf16[2,2,64,896]{3,2,1,0:T(8,128)(2,1)S(1)}, u32[]{:S(2)}, u32[]{:S(2)}) %collective-permute-start.18) | collective-permute-done | bytes 458784 | tf_op jit(solution)/shard_map/ppermute | solution.py:23
  60.7 6.2 %collective-permute-done.19 = bf16[2,64,896]{2,1,0:T(8,128)(2,1)S(1)} collective-permute-done((bf16[2,64,896]{2,1,0:T(8,128)(2,1)S(1)}, bf16[2,64,896]{2,1,0:T(8,128)(2,1)S(1)}, u32[]{:S(2)}, u32[]{:S(2)}) %collective-permute-start.19) | collective-permute-done | bytes 229408 | tf_op jit(solution)/shard_map/ppermute | solution.py:23
  68.5 2.6 %collective-permute-start.22 = (bf16[64,896]{1,0:T(8,128)(2,1)S(1)}, bf16[64,896]{1,0:T(8,128)(2,1)S(1)}, u32[]{:S(2)}, u32[]{:S(2)}) collective-permute-start(bf16[64,896]{1,0:T(8,128)(2,1)S(1)} %fusion.32), channel_id=1, source_target_pairs={{0,192},{64,128},{128,64},{192,0},{1,193},{65,129},{129,65},{193,1... | collective-permute-start | bytes 344072 | tf_op jit(solution)/shard_map/ppermute | solution.py:23
  71.2 2.4 %collective-permute-done.21 = bf16[64,896]{1,0:T(8,128)(2,1)S(1)} collective-permute-done((bf16[64,896]{1,0:T(8,128)(2,1)S(1)}, bf16[64,896]{1,0:T(8,128)(2,1)S(1)}, u32[]{:S(2)}, u32[]{:S(2)}) %collective-permute-start.21) | collective-permute-done | bytes 114720 | tf_op jit(solution)/shard_map/ppermute | solution.py:23
  73.6 2.3 %collective-permute-done.22 = bf16[64,896]{1,0:T(8,128)(2,1)S(1)} collective-permute-done((bf16[64,896]{1,0:T(8,128)(2,1)S(1)}, bf16[64,896]{1,0:T(8,128)(2,1)S(1)}, u32[]{:S(2)}, u32[]{:S(2)}) %collective-permute-start.22) | collective-permute-done | bytes 114720 | tf_op jit(solution)/shard_map/ppermute | solution.py:23
  76.9 2.3 %collective-permute-start.9 = (bf16[2,64,896]{2,1,0:T(8,128)(2,1)S(1)}, bf16[2,64,896]{2,1,0:T(8,128)(2,1)S(1)}, u32[]{:S(2)}, u32[]{:S(2)}) collective-permute-start(bf16[2,64,896]{2,1,0:T(8,128)(2,1)S(1)} %pad_maximum_fusion.7), channel_id=1, source_target_pairs={{0,64},{64,0},{128,192},{192,128},{1,65},{65,1},{129,193},{193,129... | collective-permute-start | bytes 688136 | tf_op jit(solution)/shard_map/ppermute | solution.py:23
  80.4 6.4 %collective-permute-done.23 = bf16[4,64,896]{2,1,0:T(8,128)(2,1)S(1)} collective-permute-done((bf16[4,64,896]{2,1,0:T(8,128)(2,1)S(1)}, bf16[4,64,896]{2,1,0:T(8,128)(2,1)S(1)}, u32[]{:S(2)}, u32[]{:S(2)}) %collective-permute-start.23) | collective-permute-done | bytes 458784 | tf_op jit(solution)/shard_map/ppermute | solution.py:23
  91.4 2.8 %collective-permute-done.11 = bf16[64,896]{1,0:T(8,128)(2,1)S(1)} collective-permute-done((bf16[64,896]{1,0:T(8,128)(2,1)S(1)}, bf16[64,896]{1,0:T(8,128)(2,1)S(1)}, u32[]{:S(2)}, u32[]{:S(2)}) %collective-permute-start.11) | collective-permute-done | bytes 114720 | tf_op jit(solution)/shard_map/ppermute | solution.py:23
  94.4 3.8 %collective-permute-start.13 = (bf16[2,64,896]{2,1,0:T(8,128)(2,1)S(1)}, bf16[2,64,896]{2,1,0:T(8,128)(2,1)S(1)}, u32[]{:S(2)}, u32[]{:S(2)}) collective-permute-start(bf16[2,64,896]{2,1,0:T(8,128)(2,1)S(1)} %get-tuple-element.55), channel_id=1, source_target_pairs={{0,128},{64,192},{128,0},{192,64},{1,129},{65,193},{129,1},{193,65... | collective-permute-start | bytes 688136 | tf_op jit(solution)/shard_map/ppermute | solution.py:23
  99.3 8.3 %collective-permute-done.13 = bf16[2,64,896]{2,1,0:T(8,128)(2,1)S(1)} collective-permute-done((bf16[2,64,896]{2,1,0:T(8,128)(2,1)S(1)}, bf16[2,64,896]{2,1,0:T(8,128)(2,1)S(1)}, u32[]{:S(2)}, u32[]{:S(2)}) %collective-permute-start.13) | collective-permute-done | bytes 229408 | tf_op jit(solution)/shard_map/ppermute | solution.py:23
  107.6 3.0 %collective-permute-done.14 = bf16[2,64,896]{2,1,0:T(8,128)(2,1)S(1)} collective-permute-done((bf16[2,64,896]{2,1,0:T(8,128)(2,1)S(1)}, bf16[2,64,896]{2,1,0:T(8,128)(2,1)S(1)}, u32[]{:S(2)}, u32[]{:S(2)}) %collective-permute-start.14) | collective-permute-done | bytes 229408 | tf_op jit(solution)/shard_map/ppermute | solution.py:23
  113.7 4.0 %collective-permute-start.30 = (bf16[8,8,1024]{2,1,0:T(8,128)(2,1)S(1)}, bf16[8,8,1024]{2,1,0:T(8,128)(2,1)S(1)}, u32[]{:S(2)}, u32[]{:S(2)}) collective-permute-start(bf16[8,8,1024]{2,1,0:T(8,128)(2,1)S(1)} %get-tuple-element.31), channel_id=1, source_target_pairs={{0,28},{4,0},{8,4},{12,8},{16,12},{20,16},{24,20},{28,24},{1,29},{... | collective-permute-start | bytes 393224 | tf_op jit(solution)/shard_map/ppermute | solution.py:19
  117.7 4.0 %collective-permute-start.25 = (bf16[8,8,1024]{2,1,0:T(8,128)(2,1)S(1)}, bf16[8,8,1024]{2,1,0:T(8,128)(2,1)S(1)}, u32[]{:S(2)}, u32[]{:S(2)}) collective-permute-start(bf16[8,8,1024]{2,1,0:T(8,128)(2,1)S(1)} %get-tuple-element.29), channel_id=1, source_target_pairs={{0,16},{4,20},{8,24},{12,28},{16,0},{20,4},{24,8},{28,12},{1,17},{... | collective-permute-start | bytes 393224 | tf_op jit(solution)/shard_map/ppermute | solution.py:19
  121.8 2.7 %collective-permute-start.27 = (bf16[8,8,1024]{2,1,0:T(8,128)(2,1)S(1)}, bf16[8,8,1024]{2,1,0:T(8,128)(2,1)S(1)}, u32[]{:S(2)}, u32[]{:S(2)}) collective-permute-start(bf16[8,8,1024]{2,1,0:T(8,128)(2,1)S(1)} %get-tuple-element.32), channel_id=1, source_target_pairs={{0,28},{4,0},{8,4},{12,8},{16,12},{20,16},{24,20},{28,24},{1,29},{... | collective-permute-start | bytes 393224 | tf_op jit(solution)/shard_map/ppermute | solution.py:19
  124.6 3.6 %collective-permute-start.31 = (bf16[8,8,1024]{2,1,0:T(8,128)(2,1)S(1)}, bf16[8,8,1024]{2,1,0:T(8,128)(2,1)S(1)}, u32[]{:S(2)}, u32[]{:S(2)}) collective-permute-start(bf16[8,8,1024]{2,1,0:T(8,128)(2,1)S(1)} %get-tuple-element.35), channel_id=1, source_target_pairs={{0,24},{4,28},{8,0},{12,4},{16,8},{20,12},{24,16},{28,20},{1,25},{... | collective-permute-start | bytes 393224 | tf_op jit(solution)/shard_map/ppermute | solution.py:19
  128.2 2.4 %collective-permute-done.26 = bf16[8,8,1024]{2,1,0:T(8,128)(2,1)S(1)} collective-permute-done((bf16[8,8,1024]{2,1,0:T(8,128)(2,1)S(1)}, bf16[8,8,1024]{2,1,0:T(8,128)(2,1)S(1)}, u32[]{:S(2)}, u32[]{:S(2)}) %collective-permute-start.26) | collective-permute-done | bytes 131104 | tf_op jit(solution)/shard_map/ppermute | solution.py:19
  135.6 2.4 %collective-permute-start.32 = (bf16[8,8,1024]{2,1,0:T(8,128)(2,1)S(1)}, bf16[8,8,1024]{2,1,0:T(8,128)(2,1)S(1)}, u32[]{:S(2)}, u32[]{:S(2)}) collective-permute-start(bf16[8,8,1024]{2,1,0:T(8,128)(2,1)S(1)} %fusion.31), channel_id=1, source_target_pairs={{0,2},{2,0},{1,3},{3,1},{4,6},{6,4},{5,7},{7,5},{8,10},{10,8},{9,1... | collective-permute-start | bytes 393224 | tf_op jit(solution)/shard_map/ppermute | solution.py:19
  138.0 3.0 %collective-permute-done.32 = bf16[8,8,1024]{2,1,0:T(8,128)(2,1)S(1)} collective-permute-done((bf16[8,8,1024]{2,1,0:T(8,128)(2,1)S(1)}, bf16[8,8,1024]{2,1,0:T(8,128)(2,1)S(1)}, u32[]{:S(2)}, u32[]{:S(2)}) %collective-permute-start.32) | collective-permute-done | bytes 131104 | tf_op jit(solution)/shard_map/ppermute | solution.py:19
  141.3 7.4 %all_to_all.20 = f32[8,8,8]{2,1,0:T(8,128)S(1)} all-to-all(f32[8,8,8]{2,1,0:T(8,128)S(1)} %broadcast_in_dim.6), channel_id=1, replica_groups=mesh['x'=4,'y'=2,'z'=8,'w'=2,'c'=2] {'x','y'}, dimensions={0} | all-to-all | bytes 4096 | tf_op jit(solution)/shard_map/all_to_all | solution.py:129
  149.0 13.8 %all_to_all.21 = bf16[8,8,1024]{2,1,0:T(8,128)(2,1)S(1)} all-to-all(bf16[8,8,1024]{2,1,0:T(8,128)(2,1)S(1)} %broadcast_in_dim.7), channel_id=1, replica_groups=mesh['x'=4,'y'=2,'z'=8,'w'=2,'c'=2] {'z'}, dimensions={0} | all-to-all | bytes 262144 | tf_op jit(solution)/shard_map/all_to_all | solution.py:139
  162.8 5.0 %collective-permute-start.33 = (bf16[64,1024]{1,0:T(8,128)(2,1)S(1)}, bf16[64,1024]{1,0:T(8,128)(2,1)S(1)}, u32[]{:S(2)}, u32[]{:S(2)}) collective-permute-start(bf16[64,1024]{1,0:T(8,128)(2,1)S(1)} %bitcast.194), channel_id=1, source_target_pairs={{0,1},{1,0},{2,3},{3,2},{4,5},{5,4},{6,7},{7,6},{8,9},{9,8},{10,11... | collective-permute-start | bytes 393224 | tf_op jit(solution)/shard_map/ppermute | solution.py:23
  168.8 3.5 %convolution_convert_fusion = bf16[128,2688]{1,0:T(8,128)(2,1)S(1)} fusion(bf16[1024,2688]{1,0:T(8,128)(2,1)} %param.13, bf16[64,1024]{1,0:T(8,128)(2,1)S(1)} %get-tuple-element.53, bf16[64,1024]{1,0:T(8,128)(2,1)S(1)} %get-tuple-element.52), kind=kOutput, calls=%fused_computation | convolution fusion | flops 705511424 | bytes 6455296 | tf_op jit(solution)/shard_map/dot_general | solution.py:145
  172.4 13.5 %all_to_all.22 = bf16[8,16,2688]{2,1,0:T(8,128)(2,1)S(1)} all-to-all(bf16[8,16,2688]{2,1,0:T(8,128)(2,1)S(1)} %bitcast.181), channel_id=1, replica_groups=mesh['x'=4,'y'=2,'z'=8,'w'=2,'c'=2] {'x','y'}, dimensions={0} | all-to-all | bytes 1376256 | tf_op jit(solution)/shard_map/all_to_all | solution.py:147
  186.3 15.2 %all_to_all.23 = f32[32,1,16]{2,1,0:T(1,128)S(1)} all-to-all(f32[32,1,16]{2,1,0:T(1,128)S(1)} %broadcast_in_dim.8), channel_id=1, replica_groups=mesh['x'=4,'y'=2,'z'=8,'w'=2,'c'=2] {'z','w','c'}, dimensions={0} | all-to-all | bytes 4096 | tf_op jit(solution)/shard_map/all_to_all | solution.py:152
  (128 shorter events, 44.4 us)
Async XLA Ops:
  2.7 10.0 %collective-permute-start = (bf16[64,1024]{1,0:T(8,128)(2,1)}, bf16[64,1024]{1,0:T(8,128)(2,1)S(1)}, u32[]{:S(2)}, u32[]{:S(2)}) collective-permute-start(bf16[64,1024]{1,0:T(8,128)(2,1)} %get-tuple-element.14), channel_id=1, source_target_pairs={{0,32},{32,0},{64,96},{96,64},{128,160},{160,128},{192,224},{224,1... | collective-permute-start | bytes 393224 | tf_op jit(solution)/shard_map/ppermute | solution.py:31
  4.9 11.1 %collective-permute-start.1 = (bf16[64,1024]{1,0:T(8,128)(2,1)}, bf16[64,1024]{1,0:T(8,128)(2,1)S(1)}, u32[]{:S(2)}, u32[]{:S(2)}) collective-permute-start(bf16[64,1024]{1,0:T(8,128)(2,1)} %get-tuple-element.15), channel_id=1, source_target_pairs={{0,64},{32,96},{64,0},{96,32},{128,192},{160,224},{192,128},{224,1... | collective-permute-start | bytes 393224 | tf_op jit(solution)/shard_map/ppermute | solution.py:31
  6.1 10.6 %collective-permute-start.2 = (bf16[64,1024]{1,0:T(8,128)(2,1)}, bf16[64,1024]{1,0:T(8,128)(2,1)S(1)}, u32[]{:S(2)}, u32[]{:S(2)}) collective-permute-start(bf16[64,1024]{1,0:T(8,128)(2,1)} %get-tuple-element.16), channel_id=1, source_target_pairs={{0,96},{32,64},{64,32},{96,0},{128,224},{160,192},{192,160},{224,1... | collective-permute-start | bytes 393224 | tf_op jit(solution)/shard_map/ppermute | solution.py:31
  6.1 11.2 %collective-permute-start.3 = (bf16[64,1024]{1,0:T(8,128)(2,1)}, bf16[64,1024]{1,0:T(8,128)(2,1)S(1)}, u32[]{:S(2)}, u32[]{:S(2)}) collective-permute-start(bf16[64,1024]{1,0:T(8,128)(2,1)} %get-tuple-element.17), channel_id=1, source_target_pairs={{0,128},{32,160},{64,192},{96,224},{128,0},{160,32},{192,64},{224,... | collective-permute-start | bytes 393224 | tf_op jit(solution)/shard_map/ppermute | solution.py:31
  9.0 10.9 %collective-permute-start.4 = (bf16[64,1024]{1,0:T(8,128)(2,1)}, bf16[64,1024]{1,0:T(8,128)(2,1)S(1)}, u32[]{:S(2)}, u32[]{:S(2)}) collective-permute-start(bf16[64,1024]{1,0:T(8,128)(2,1)} %get-tuple-element.18), channel_id=1, source_target_pairs={{0,160},{32,128},{64,224},{96,192},{128,32},{160,0},{192,96},{224,... | collective-permute-start | bytes 393224 | tf_op jit(solution)/shard_map/ppermute | solution.py:31
  12.8 11.1 %collective-permute-start.5 = (bf16[64,1024]{1,0:T(8,128)(2,1)}, bf16[64,1024]{1,0:T(8,128)(2,1)S(1)}, u32[]{:S(2)}, u32[]{:S(2)}) collective-permute-start(bf16[64,1024]{1,0:T(8,128)(2,1)} %get-tuple-element.19), channel_id=1, source_target_pairs={{0,192},{32,224},{64,128},{96,160},{128,64},{160,96},{192,0},{224,... | collective-permute-start | bytes 393224 | tf_op jit(solution)/shard_map/ppermute | solution.py:31
  16.0 10.6 %collective-permute-start.6 = (bf16[64,1024]{1,0:T(8,128)(2,1)}, bf16[64,1024]{1,0:T(8,128)(2,1)S(1)}, u32[]{:S(2)}, u32[]{:S(2)}) collective-permute-start(bf16[64,1024]{1,0:T(8,128)(2,1)} %get-tuple-element.20), channel_id=1, source_target_pairs={{0,224},{32,192},{64,160},{96,128},{128,96},{160,64},{192,32},{224... | collective-permute-start | bytes 393224 | tf_op jit(solution)/shard_map/ppermute | solution.py:31
  27.3 6.0 %collective-permute-start.15 = (bf16[8,64,1024]{2,1,0:T(8,128)(2,1)}, bf16[8,64,1024]{2,1,0:T(8,128)(2,1)S(1)}, u32[]{:S(2)}, u32[]{:S(2)}) collective-permute-start(bf16[8,64,1024]{2,1,0:T(8,128)(2,1)} %bitcast_dynamic-update-slice_fusion), channel_id=1, source_target_pairs={{0,1},{1,0},{2,3},{3,2},{4,5},{5,4},{6,7},{7,6},{8,9},{9,8},{10,11... | collective-permute-start | bytes 3145736 | tf_op jit(solution)/shard_map/ppermute | solution.py:23
  31.9 28.5 %collective-permute-start.7 = (bf16[2,4,64,896]{3,2,1,0:T(8,128)(2,1)S(1)}, bf16[2,4,64,896]{3,2,1,0:T(8,128)(2,1)S(1)}, u32[]{:S(2)}, u32[]{:S(2)}) collective-permute-start(bf16[2,4,64,896]{3,2,1,0:T(8,128)(2,1)S(1)} %pad_maximum_fusion), channel_id=1, source_target_pairs={{0,32},{32,0},{1,33},{33,1},{2,34},{34,2},{3,35},{35,3},{4,36},{36... | collective-permute-start | bytes 2752520 | tf_op jit(solution)/shard_map/ppermute | solution.py:23
  36.0 13.4 %collective-permute-start.16 = (bf16[2,2,64,896]{3,2,1,0:T(8,128)(2,1)S(1)}, bf16[2,2,64,896]{3,2,1,0:T(8,128)(2,1)S(1)}, u32[]{:S(2)}, u32[]{:S(2)}) collective-permute-start(bf16[2,2,64,896]{3,2,1,0:T(8,128)(2,1)S(1)} %pad_maximum_fusion.2), channel_id=1, source_target_pairs={{0,128},{64,192},{128,0},{192,64},{1,129},{65,193},{129,1},{193,65... | collective-permute-start | bytes 1376264 | tf_op jit(solution)/shard_map/ppermute | solution.py:23
  36.7 20.4 %collective-permute-start.17 = (bf16[2,2,64,896]{3,2,1,0:T(8,128)(2,1)S(1)}, bf16[2,2,64,896]{3,2,1,0:T(8,128)(2,1)S(1)}, u32[]{:S(2)}, u32[]{:S(2)}) collective-permute-start(bf16[2,2,64,896]{3,2,1,0:T(8,128)(2,1)S(1)} %pad_maximum_fusion.3), channel_id=1, source_target_pairs={{0,64},{64,0},{128,192},{192,128},{1,65},{65,1},{129,193},{193,129... | collective-permute-start | bytes 1376264 | tf_op jit(solution)/shard_map/ppermute | solution.py:23
  37.0 22.8 %collective-permute-start.18 = (bf16[2,2,64,896]{3,2,1,0:T(8,128)(2,1)S(1)}, bf16[2,2,64,896]{3,2,1,0:T(8,128)(2,1)S(1)}, u32[]{:S(2)}, u32[]{:S(2)}) collective-permute-start(bf16[2,2,64,896]{3,2,1,0:T(8,128)(2,1)S(1)} %pad_maximum_fusion.4), channel_id=1, source_target_pairs={{0,192},{64,128},{128,64},{192,0},{1,193},{65,129},{129,65},{193,1... | collective-permute-start | bytes 1376264 | tf_op jit(solution)/shard_map/ppermute | solution.py:23
  60.1 6.8 %collective-permute-start.19 = (bf16[2,64,896]{2,1,0:T(8,128)(2,1)S(1)}, bf16[2,64,896]{2,1,0:T(8,128)(2,1)S(1)}, u32[]{:S(2)}, u32[]{:S(2)}) collective-permute-start(bf16[2,64,896]{2,1,0:T(8,128)(2,1)S(1)} %pad_maximum_fusion.10), channel_id=1, source_target_pairs={{0,32},{32,0},{1,33},{33,1},{2,34},{34,2},{3,35},{35,3},{4,36},{36... | collective-permute-start | bytes 688136 | tf_op jit(solution)/shard_map/ppermute | solution.py:23
  67.2 6.3 %collective-permute-start.21 = (bf16[64,896]{1,0:T(8,128)(2,1)S(1)}, bf16[64,896]{1,0:T(8,128)(2,1)S(1)}, u32[]{:S(2)}, u32[]{:S(2)}) collective-permute-start(bf16[64,896]{1,0:T(8,128)(2,1)S(1)} %fusion.32), channel_id=1, source_target_pairs={{0,128},{64,192},{128,0},{192,64},{1,129},{65,193},{129,1},{193,65... | collective-permute-start | bytes 344072 | tf_op jit(solution)/shard_map/ppermute | solution.py:23
  68.5 7.4 %collective-permute-start.22 = (bf16[64,896]{1,0:T(8,128)(2,1)S(1)}, bf16[64,896]{1,0:T(8,128)(2,1)S(1)}, u32[]{:S(2)}, u32[]{:S(2)}) collective-permute-start(bf16[64,896]{1,0:T(8,128)(2,1)S(1)} %fusion.32), channel_id=1, source_target_pairs={{0,192},{64,128},{128,64},{192,0},{1,193},{65,129},{129,65},{193,1... | collective-permute-start | bytes 344072 | tf_op jit(solution)/shard_map/ppermute | solution.py:23
  76.0 10.8 %collective-permute-start.23 = (bf16[4,64,896]{2,1,0:T(8,128)(2,1)S(1)}, bf16[4,64,896]{2,1,0:T(8,128)(2,1)S(1)}, u32[]{:S(2)}, u32[]{:S(2)}) collective-permute-start(bf16[4,64,896]{2,1,0:T(8,128)(2,1)S(1)} %get-tuple-element.51), channel_id=1, source_target_pairs={{0,32},{32,0},{1,33},{33,1},{2,34},{34,2},{3,35},{35,3},{4,36},{36... | collective-permute-start | bytes 1376264 | tf_op jit(solution)/shard_map/ppermute | solution.py:23
  76.8 13.6 %collective-permute-start.8 = (bf16[2,64,896]{2,1,0:T(8,128)(2,1)S(1)}, bf16[2,64,896]{2,1,0:T(8,128)(2,1)S(1)}, u32[]{:S(2)}, u32[]{:S(2)}) collective-permute-start(bf16[2,64,896]{2,1,0:T(8,128)(2,1)S(1)} %pad_maximum_fusion.6), channel_id=1, source_target_pairs={{0,128},{64,192},{128,0},{192,64},{1,129},{65,193},{129,1},{193,65... | collective-permute-start | bytes 688136 | tf_op jit(solution)/shard_map/ppermute | solution.py:23
  76.9 13.5 %collective-permute-start.9 = (bf16[2,64,896]{2,1,0:T(8,128)(2,1)S(1)}, bf16[2,64,896]{2,1,0:T(8,128)(2,1)S(1)}, u32[]{:S(2)}, u32[]{:S(2)}) collective-permute-start(bf16[2,64,896]{2,1,0:T(8,128)(2,1)S(1)} %pad_maximum_fusion.7), channel_id=1, source_target_pairs={{0,64},{64,0},{128,192},{192,128},{1,65},{65,1},{129,193},{193,129... | collective-permute-start | bytes 688136 | tf_op jit(solution)/shard_map/ppermute | solution.py:23
  79.3 11.1 %collective-permute-start.10 = (bf16[2,64,896]{2,1,0:T(8,128)(2,1)S(1)}, bf16[2,64,896]{2,1,0:T(8,128)(2,1)S(1)}, u32[]{:S(2)}, u32[]{:S(2)}) collective-permute-start(bf16[2,64,896]{2,1,0:T(8,128)(2,1)S(1)} %pad_maximum_fusion.8), channel_id=1, source_target_pairs={{0,192},{64,128},{128,64},{192,0},{1,193},{65,129},{129,65},{193,1... | collective-permute-start | bytes 688136 | tf_op jit(solution)/shard_map/ppermute | solution.py:23
  88.1 22.6 %collective-permute-start.24 = (bf16[4,2,64,1024]{3,2,1,0:T(8,128)(2,1)S(1)}, bf16[4,2,64,1024]{3,2,1,0:T(8,128)(2,1)S(1)}, u32[]{:S(2)}, u32[]{:S(2)}) collective-permute-start(bf16[4,2,64,1024]{3,2,1,0:T(8,128)(2,1)S(1)} %fusion.8), channel_id=1, source_target_pairs={{0,1},{1,0},{2,3},{3,2},{4,5},{5,4},{6,7},{7,6},{8,9},{9,8},{10,11... | collective-permute-start | bytes 3145736 | tf_op jit(solution)/shard_map/ppermute | solution.py:23
  94.3 5.0 %collective-permute-start.12 = (bf16[2,64,896]{2,1,0:T(8,128)(2,1)S(1)}, bf16[2,64,896]{2,1,0:T(8,128)(2,1)S(1)}, u32[]{:S(2)}, u32[]{:S(2)}) collective-permute-start(bf16[2,64,896]{2,1,0:T(8,128)(2,1)S(1)} %get-tuple-element.55), channel_id=1, source_target_pairs={{0,64},{64,0},{128,192},{192,128},{1,65},{65,1},{129,193},{193,129... | collective-permute-start | bytes 688136 | tf_op jit(solution)/shard_map/ppermute | solution.py:23
  94.4 13.1 %collective-permute-start.13 = (bf16[2,64,896]{2,1,0:T(8,128)(2,1)S(1)}, bf16[2,64,896]{2,1,0:T(8,128)(2,1)S(1)}, u32[]{:S(2)}, u32[]{:S(2)}) collective-permute-start(bf16[2,64,896]{2,1,0:T(8,128)(2,1)S(1)} %get-tuple-element.55), channel_id=1, source_target_pairs={{0,128},{64,192},{128,0},{192,64},{1,129},{65,193},{129,1},{193,65... | collective-permute-start | bytes 688136 | tf_op jit(solution)/shard_map/ppermute | solution.py:23
  98.3 12.4 %collective-permute-start.14 = (bf16[2,64,896]{2,1,0:T(8,128)(2,1)S(1)}, bf16[2,64,896]{2,1,0:T(8,128)(2,1)S(1)}, u32[]{:S(2)}, u32[]{:S(2)}) collective-permute-start(bf16[2,64,896]{2,1,0:T(8,128)(2,1)S(1)} %get-tuple-element.55), channel_id=1, source_target_pairs={{0,192},{64,128},{128,64},{192,0},{1,193},{65,129},{129,65},{193,1... | collective-permute-start | bytes 688136 | tf_op jit(solution)/shard_map/ppermute | solution.py:23
  112.0 12.4 %collective-permute-start.28 = (bf16[8,8,1024]{2,1,0:T(8,128)(2,1)S(1)}, bf16[8,8,1024]{2,1,0:T(8,128)(2,1)S(1)}, u32[]{:S(2)}, u32[]{:S(2)}) collective-permute-start(bf16[8,8,1024]{2,1,0:T(8,128)(2,1)S(1)} %get-tuple-element.30), channel_id=1, source_target_pairs={{0,4},{4,8},{8,12},{12,16},{16,20},{20,24},{24,28},{28,0},{1,5},{5... | collective-permute-start | bytes 393224 | tf_op jit(solution)/shard_map/ppermute | solution.py:19
  113.7 10.7 %collective-permute-start.30 = (bf16[8,8,1024]{2,1,0:T(8,128)(2,1)S(1)}, bf16[8,8,1024]{2,1,0:T(8,128)(2,1)S(1)}, u32[]{:S(2)}, u32[]{:S(2)}) collective-permute-start(bf16[8,8,1024]{2,1,0:T(8,128)(2,1)S(1)} %get-tuple-element.31), channel_id=1, source_target_pairs={{0,28},{4,0},{8,4},{12,8},{16,12},{20,16},{24,20},{28,24},{1,29},{... | collective-permute-start | bytes 393224 | tf_op jit(solution)/shard_map/ppermute | solution.py:19
  117.7 10.4 %collective-permute-start.25 = (bf16[8,8,1024]{2,1,0:T(8,128)(2,1)S(1)}, bf16[8,8,1024]{2,1,0:T(8,128)(2,1)S(1)}, u32[]{:S(2)}, u32[]{:S(2)}) collective-permute-start(bf16[8,8,1024]{2,1,0:T(8,128)(2,1)S(1)} %get-tuple-element.29), channel_id=1, source_target_pairs={{0,16},{4,20},{8,24},{12,28},{16,0},{20,4},{24,8},{28,12},{1,17},{... | collective-permute-start | bytes 393224 | tf_op jit(solution)/shard_map/ppermute | solution.py:19
  121.8 8.9 %collective-permute-start.26 = (bf16[8,8,1024]{2,1,0:T(8,128)(2,1)S(1)}, bf16[8,8,1024]{2,1,0:T(8,128)(2,1)S(1)}, u32[]{:S(2)}, u32[]{:S(2)}) collective-permute-start(bf16[8,8,1024]{2,1,0:T(8,128)(2,1)S(1)} %get-tuple-element.33), channel_id=1, source_target_pairs={{0,4},{4,8},{8,12},{12,16},{16,20},{20,24},{24,28},{28,0},{1,5},{5... | collective-permute-start | bytes 393224 | tf_op jit(solution)/shard_map/ppermute | solution.py:19
  121.8 10.2 %collective-permute-start.27 = (bf16[8,8,1024]{2,1,0:T(8,128)(2,1)S(1)}, bf16[8,8,1024]{2,1,0:T(8,128)(2,1)S(1)}, u32[]{:S(2)}, u32[]{:S(2)}) collective-permute-start(bf16[8,8,1024]{2,1,0:T(8,128)(2,1)S(1)} %get-tuple-element.32), channel_id=1, source_target_pairs={{0,28},{4,0},{8,4},{12,8},{16,12},{20,16},{24,20},{28,24},{1,29},{... | collective-permute-start | bytes 393224 | tf_op jit(solution)/shard_map/ppermute | solution.py:19
  124.5 8.8 %collective-permute-start.29 = (bf16[8,8,1024]{2,1,0:T(8,128)(2,1)S(1)}, bf16[8,8,1024]{2,1,0:T(8,128)(2,1)S(1)}, u32[]{:S(2)}, u32[]{:S(2)}) collective-permute-start(bf16[8,8,1024]{2,1,0:T(8,128)(2,1)S(1)} %get-tuple-element.34), channel_id=1, source_target_pairs={{0,8},{4,12},{8,16},{12,20},{16,24},{20,28},{24,0},{28,4},{1,9},{5... | collective-permute-start | bytes 393224 | tf_op jit(solution)/shard_map/ppermute | solution.py:19
  124.6 10.9 %collective-permute-start.31 = (bf16[8,8,1024]{2,1,0:T(8,128)(2,1)S(1)}, bf16[8,8,1024]{2,1,0:T(8,128)(2,1)S(1)}, u32[]{:S(2)}, u32[]{:S(2)}) collective-permute-start(bf16[8,8,1024]{2,1,0:T(8,128)(2,1)S(1)} %get-tuple-element.35), channel_id=1, source_target_pairs={{0,24},{4,28},{8,0},{12,4},{16,8},{20,12},{24,16},{28,20},{1,25},{... | collective-permute-start | bytes 393224 | tf_op jit(solution)/shard_map/ppermute | solution.py:19
  135.6 5.4 %collective-permute-start.32 = (bf16[8,8,1024]{2,1,0:T(8,128)(2,1)S(1)}, bf16[8,8,1024]{2,1,0:T(8,128)(2,1)S(1)}, u32[]{:S(2)}, u32[]{:S(2)}) collective-permute-start(bf16[8,8,1024]{2,1,0:T(8,128)(2,1)S(1)} %fusion.31), channel_id=1, source_target_pairs={{0,2},{2,0},{1,3},{3,1},{4,6},{6,4},{5,7},{7,5},{8,10},{10,8},{9,1... | collective-permute-start | bytes 393224 | tf_op jit(solution)/shard_map/ppermute | solution.py:19
  162.8 6.0 %collective-permute-start.33 = (bf16[64,1024]{1,0:T(8,128)(2,1)S(1)}, bf16[64,1024]{1,0:T(8,128)(2,1)S(1)}, u32[]{:S(2)}, u32[]{:S(2)}) collective-permute-start(bf16[64,1024]{1,0:T(8,128)(2,1)S(1)} %bitcast.194), channel_id=1, source_target_pairs={{0,1},{1,0},{2,3},{3,2},{4,5},{5,4},{6,7},{7,6},{8,9},{9,8},{10,11... | collective-permute-start | bytes 393224 | tf_op jit(solution)/shard_map/ppermute | solution.py:23
  (9 other events, 139.4 us)

commit v4 on v3

--- a/solution.py
+++ b/solution.py
@@ -108,14 +108,19 @@
         return lax.dynamic_index_in_dim(part, (z + k) % NZ, 1, keepdims=False)
 
     def sent(block, step):
-        return shifted(block.astype(BF), "z", NZ, step)
+        return shifted(block, "z", NZ, step)
 
-    far = sent(piece(4), 4)
+    cut = NX * NY // 2
+    far = piece(4)
+    far_up, far_down = sent(far[:cut], 2), sent(far[cut:], -2)
     relay_up, relay_down = sent(piece(3), 1), sent(piece(5), -1)
+    two_up = wide(piece(2)) + wide(relay_up)
+    two_up = jnp.concatenate([two_up[:cut] + wide(far_up), two_up[cut:]]).astype(BF)
+    two_down = wide(piece(6)) + wide(relay_down)
+    two_down = jnp.concatenate([two_down[:cut], two_down[cut:] + wide(far_down)]).astype(BF)
+    two_up, two_down = sent(two_up, 2), sent(two_down, -2)
     one_up, one_down = sent(piece(1), 1), sent(piece(7), -1)
-    two_up = sent(wide(piece(2)) + wide(relay_up), 2)
-    two_down = sent(wide(piece(6)) + wide(relay_down), -2)
-    mine = wide(piece(0)) + sum(wide(got) for got in (far, one_up, one_down, two_up, two_down))
+    mine = wide(piece(0)) + sum(wide(got) for got in (one_up, one_down, two_up, two_down))
     mine = mine.astype(BF)
     branch = wide(mine) + wide(shifted(mine, "w", NW, 1))
 
@@ -126,11 +131,8 @@
     variant_at = offsets ^ (x * NY + y)
     placed_at = (variant_at[None, :] == offsets[:, None]).astype(F32)
     by_variant = jnp.sum(placed_at[:, :, None] * partial_square[None], axis=1)
-    everyone = lax.all_to_all(
-        jnp.broadcast_to(by_variant[None], (NX * NY, *by_variant.shape)),
-        PROMPT, 0, 0, tiled=True,
-    )
-    square = everyone.sum(axis=0)
+    square = by_variant + paired(by_variant, "y", NY, 1)
+    square = square + sum([paired(square, "x", NX, d) for d in TURNS])
     scale = lax.rsqrt(square / D + EPS) * guidance[:, None]
     scale = jnp.sum(placed_at[:, :, None] * scale[:, None], axis=0)
     mixed = (jnp.sum(state * scale[:, :, None], axis=0) * norm_gain).astype(BF)

time: 203 us -> 204 us (level)
  blocking collectives: 49.9 us -> 43.2 us
  starting transfers between devices: 54.4 us -> 59.7 us
  waiting for transfers between devices: 71.3 us -> 73.6 us
    all_to_all x1 -> x0, blocking collectives: 7.44 us -> none  [step(): lax.all_to_all(jnp.broadcast_to(by_variant[None], (NX * NY, *by_variant.s...]
    ppermute x19 -> x23, starting transfers between devices: 25.9 us -> 31.5 us  [paired(): return lax.ppermute(array, axis, [(i, i ^ bit) for i in range(size)])]
    ppermute x19 -> x23, waiting for transfers between devices: 53.6 us -> 57.9 us  [paired(): return lax.ppermute(array, axis, [(i, i ^ bit) for i in range(size)])]
    ppermute x8 -> x9, waiting for transfers between devices: 10.3 us -> 8.29 us  [shifted(): lax.ppermute(array, axis, [(i, (i + step) % size) for i in range(size)])]
    ppermute x8 -> x9, starting transfers between devices: 18.5 us -> 18.2 us  [shifted(): lax.ppermute(array, axis, [(i, (i + step) % size) for i in range(size)])]
  transfers between devices with their start and end apart: 34 -> 39, of which waited for: 20 -> 22; matrix products, arithmetic and copies ran while one was open for 8% -> 8% of each run, Pallas kernels for 0% -> 0%
where the time goes in v4:
time: 204 us; the launch traced here: 203 us
  waiting for transfers between devices  73.6 us (36%)
  starting transfers between devices  59.7 us (29%)
  blocking collectives  43.2 us (21%)
  matrix products  12.4 us (6%)
  local copies, waits for them, and re-layouts  7.67 us (4%)
  other arithmetic  3.51 us (2%)
  Pallas kernels  2.75 us (1%)
    ppermute x23, waiting for transfers between devices, paired(): return lax.ppermute(array, axis, [(i, i ^ bit) for i in range(size)])  57.9 us
    ppermute x23, starting transfers between devices, paired(): return lax.ppermute(array, axis, [(i, i ^ bit) for i in range(size)])  31.5 us
    ppermute x9, starting transfers between devices, shifted(): lax.ppermute(array, axis, [(i, (i + step) % size) for i in range(size)])  18.2 us
    all_to_all x1, blocking collectives, step(): lax.all_to_all(jnp.broadcast_to(part_lse[None, None], (shards, 1, part_ls...  15.3 us
    all_to_all x1, blocking collectives, step(): tiles = lax.all_to_all(tiles, PROMPT, 0, 0, tiled=True)  14 us
    all_to_all x1, blocking collectives, step(): ring = lax.all_to_all(ring, 'z', 0, 0, tiled=True).reshape(-1, share)  13.8 us
    ppermute x7, starting transfers between devices, paired_prompt(): return lax.ppermute(array, PROMPT, [(p, p ^ k) for p in range(NX * NY)])  10 us
    dot_general x6, matrix products, products(): jnp.dot(flat, weight, preferred_element_type=F32)  8.89 us
  transfers between devices with their start and end apart: 39, of which 22 were waited for; matrix products, arithmetic and copies ran while one was open for 8% of the time, Pallas kernels for 0%

profile of v4, /device:TPU:1, one launch (start us, length us, event | category | flops | bytes accessed | tf_op | source)
XLA Modules:
  0.0 203.4 jit_solution(1877631689839486711)
XLA Ops:
  0.0 2.7 %shard_map.82 = (bf16[64,1024]{1,0:T(8,128)(2,1)}, bf16[64,1024]{1,0:T(8,128)(2,1)}, bf16[64,1024]{1,0:T(8,128)(2,1)}, bf16[64,1024]{1,0:T(8,128)(2,1)}, bf16[64...) custom-call(bf16[128,8192]{1,0:T(8,128)(2,1)} %bitcast.189), custom_call_target="tpu_custom_call" | custom-call | tf_op jit(solution)/shard_map/pallas_call | solution.py:46
  6.1 2.9 %collective-permute-start.3 = (bf16[64,1024]{1,0:T(8,128)(2,1)}, bf16[64,1024]{1,0:T(8,128)(2,1)S(1)}, u32[]{:S(2)}, u32[]{:S(2)}) collective-permute-start(bf16[64,1024]{1,0:T(8,128)(2,1)} %get-tuple-element.17), channel_id=1, source_target_pairs={{0,128},{32,160},{64,192},{96,224},{128,0},{160,32},{192,64},{224,... | collective-permute-start | bytes 393224 | tf_op jit(solution)/shard_map/ppermute | solution.py:31
  12.8 2.6 %collective-permute-start.5 = (bf16[64,1024]{1,0:T(8,128)(2,1)}, bf16[64,1024]{1,0:T(8,128)(2,1)S(1)}, u32[]{:S(2)}, u32[]{:S(2)}) collective-permute-start(bf16[64,1024]{1,0:T(8,128)(2,1)} %get-tuple-element.19), channel_id=1, source_target_pairs={{0,192},{32,224},{64,128},{96,160},{128,64},{160,96},{192,0},{224,... | collective-permute-start | bytes 393224 | tf_op jit(solution)/shard_map/ppermute | solution.py:31
  20.6 3.3 %collective-permute-done.5 = bf16[64,1024]{1,0:T(8,128)(2,1)S(1)} collective-permute-done((bf16[64,1024]{1,0:T(8,128)(2,1)}, bf16[64,1024]{1,0:T(8,128)(2,1)S(1)}, u32[]{:S(2)}, u32[]{:S(2)}) %collective-permute-start.5) | collective-permute-done | bytes 131104 | tf_op jit(solution)/shard_map/ppermute | solution.py:31
  27.8 2.6 %fusion = f32[4,2,64,896]{3,2,1,0:T(8,128)S(1)} fusion(bf16[4,2,64,1024]{3,2,1,0:T(8,128)(2,1)} %bitcast.208, bf16[1024,896]{1,0:T(8,128)(2,1)S(1)} %copy-done), kind=kOutput, calls=%fused_computation.2 | convolution fusion | flops 939524096 | bytes 4718592 | tf_op jit(solution)/shard_map/dot_general | solution.py:61
  37.0 2.5 %collective-permute-start.18 = (bf16[2,2,64,896]{3,2,1,0:T(8,128)(2,1)S(1)}, bf16[2,2,64,896]{3,2,1,0:T(8,128)(2,1)S(1)}, u32[]{:S(2)}, u32[]{:S(2)}) collective-permute-start(bf16[2,2,64,896]{3,2,1,0:T(8,128)(2,1)S(1)} %pad_maximum_fusion.4), channel_id=1, source_target_pairs={{0,192},{64,128},{128,64},{192,0},{1,193},{65,129},{129,65},{193,1... | collective-permute-start | bytes 1376264 | tf_op jit(solution)/shard_map/ppermute | solution.py:23
  39.7 9.7 %collective-permute-done.16 = bf16[2,2,64,896]{3,2,1,0:T(8,128)(2,1)S(1)} collective-permute-done((bf16[2,2,64,896]{3,2,1,0:T(8,128)(2,1)S(1)}, bf16[2,2,64,896]{3,2,1,0:T(8,128)(2,1)S(1)}, u32[]{:S(2)}, u32[]{:S(2)}) %collective-permute-start.16) | collective-permute-done | bytes 458784 | tf_op jit(solution)/shard_map/ppermute | solution.py:23
  49.4 7.7 %collective-permute-done.17 = bf16[2,2,64,896]{3,2,1,0:T(8,128)(2,1)S(1)} collective-permute-done((bf16[2,2,64,896]{3,2,1,0:T(8,128)(2,1)S(1)}, bf16[2,2,64,896]{3,2,1,0:T(8,128)(2,1)S(1)}, u32[]{:S(2)}, u32[]{:S(2)}) %collective-permute-start.17) | collective-permute-done | bytes 458784 | tf_op jit(solution)/shard_map/ppermute | solution.py:23
  57.0 2.8 %collective-permute-done.18 = bf16[2,2,64,896]{3,2,1,0:T(8,128)(2,1)S(1)} collective-permute-done((bf16[2,2,64,896]{3,2,1,0:T(8,128)(2,1)S(1)}, bf16[2,2,64,896]{3,2,1,0:T(8,128)(2,1)S(1)}, u32[]{:S(2)}, u32[]{:S(2)}) %collective-permute-start.18) | collective-permute-done | bytes 458784 | tf_op jit(solution)/shard_map/ppermute | solution.py:23
  60.7 6.2 %collective-permute-done.19 = bf16[2,64,896]{2,1,0:T(8,128)(2,1)S(1)} collective-permute-done((bf16[2,64,896]{2,1,0:T(8,128)(2,1)S(1)}, bf16[2,64,896]{2,1,0:T(8,128)(2,1)S(1)}, u32[]{:S(2)}, u32[]{:S(2)}) %collective-permute-start.19) | collective-permute-done | bytes 229408 | tf_op jit(solution)/shard_map/ppermute | solution.py:23
  68.5 2.6 %collective-permute-start.22 = (bf16[64,896]{1,0:T(8,128)(2,1)S(1)}, bf16[64,896]{1,0:T(8,128)(2,1)S(1)}, u32[]{:S(2)}, u32[]{:S(2)}) collective-permute-start(bf16[64,896]{1,0:T(8,128)(2,1)S(1)} %fusion.30), channel_id=1, source_target_pairs={{0,192},{64,128},{128,64},{192,0},{1,193},{65,129},{129,65},{193,1... | collective-permute-start | bytes 344072 | tf_op jit(solution)/shard_map/ppermute | solution.py:23
  71.2 2.4 %collective-permute-done.21 = bf16[64,896]{1,0:T(8,128)(2,1)S(1)} collective-permute-done((bf16[64,896]{1,0:T(8,128)(2,1)S(1)}, bf16[64,896]{1,0:T(8,128)(2,1)S(1)}, u32[]{:S(2)}, u32[]{:S(2)}) %collective-permute-start.21) | collective-permute-done | bytes 114720 | tf_op jit(solution)/shard_map/ppermute | solution.py:23
  73.6 2.3 %collective-permute-done.22 = bf16[64,896]{1,0:T(8,128)(2,1)S(1)} collective-permute-done((bf16[64,896]{1,0:T(8,128)(2,1)S(1)}, bf16[64,896]{1,0:T(8,128)(2,1)S(1)}, u32[]{:S(2)}, u32[]{:S(2)}) %collective-permute-start.22) | collective-permute-done | bytes 114720 | tf_op jit(solution)/shard_map/ppermute | solution.py:23
  76.9 2.3 %collective-permute-start.9 = (bf16[2,64,896]{2,1,0:T(8,128)(2,1)S(1)}, bf16[2,64,896]{2,1,0:T(8,128)(2,1)S(1)}, u32[]{:S(2)}, u32[]{:S(2)}) collective-permute-start(bf16[2,64,896]{2,1,0:T(8,128)(2,1)S(1)} %pad_maximum_fusion.7), channel_id=1, source_target_pairs={{0,64},{64,0},{128,192},{192,128},{1,65},{65,1},{129,193},{193,129... | collective-permute-start | bytes 688136 | tf_op jit(solution)/shard_map/ppermute | solution.py:23
  80.4 6.4 %collective-permute-done.23 = bf16[4,64,896]{2,1,0:T(8,128)(2,1)S(1)} collective-permute-done((bf16[4,64,896]{2,1,0:T(8,128)(2,1)S(1)}, bf16[4,64,896]{2,1,0:T(8,128)(2,1)S(1)}, u32[]{:S(2)}, u32[]{:S(2)}) %collective-permute-start.23) | collective-permute-done | bytes 458784 | tf_op jit(solution)/shard_map/ppermute | solution.py:23
  91.4 2.9 %collective-permute-done.11 = bf16[64,896]{1,0:T(8,128)(2,1)S(1)} collective-permute-done((bf16[64,896]{1,0:T(8,128)(2,1)S(1)}, bf16[64,896]{1,0:T(8,128)(2,1)S(1)}, u32[]{:S(2)}, u32[]{:S(2)}) %collective-permute-start.11) | collective-permute-done | bytes 114720 | tf_op jit(solution)/shard_map/ppermute | solution.py:23
  94.4 3.8 %collective-permute-start.13 = (bf16[2,64,896]{2,1,0:T(8,128)(2,1)S(1)}, bf16[2,64,896]{2,1,0:T(8,128)(2,1)S(1)}, u32[]{:S(2)}, u32[]{:S(2)}) collective-permute-start(bf16[2,64,896]{2,1,0:T(8,128)(2,1)S(1)} %get-tuple-element.56), channel_id=1, source_target_pairs={{0,128},{64,192},{128,0},{192,64},{1,129},{65,193},{129,1},{193,65... | collective-permute-start | bytes 688136 | tf_op jit(solution)/shard_map/ppermute | solution.py:23
  99.3 8.3 %collective-permute-done.13 = bf16[2,64,896]{2,1,0:T(8,128)(2,1)S(1)} collective-permute-done((bf16[2,64,896]{2,1,0:T(8,128)(2,1)S(1)}, bf16[2,64,896]{2,1,0:T(8,128)(2,1)S(1)}, u32[]{:S(2)}, u32[]{:S(2)}) %collective-permute-start.13) | collective-permute-done | bytes 229408 | tf_op jit(solution)/shard_map/ppermute | solution.py:23
  107.5 3.1 %collective-permute-done.14 = bf16[2,64,896]{2,1,0:T(8,128)(2,1)S(1)} collective-permute-done((bf16[2,64,896]{2,1,0:T(8,128)(2,1)S(1)}, bf16[2,64,896]{2,1,0:T(8,128)(2,1)S(1)}, u32[]{:S(2)}, u32[]{:S(2)}) %collective-permute-start.14) | collective-permute-done | bytes 229408 | tf_op jit(solution)/shard_map/ppermute | solution.py:23
  113.7 4.0 %collective-permute-start.30 = (bf16[8,8,1024]{2,1,0:T(8,128)(2,1)S(1)}, bf16[8,8,1024]{2,1,0:T(8,128)(2,1)S(1)}, u32[]{:S(2)}, u32[]{:S(2)}) collective-permute-start(bf16[8,8,1024]{2,1,0:T(8,128)(2,1)S(1)} %get-tuple-element.31), channel_id=1, source_target_pairs={{0,28},{4,0},{8,4},{12,8},{16,12},{20,16},{24,20},{28,24},{1,29},{... | collective-permute-start | bytes 393224 | tf_op jit(solution)/shard_map/ppermute | solution.py:19
  117.8 3.6 %collective-permute-start.31 = (bf16[4,8,1024]{2,1,0:T(8,128)(2,1)S(1)}, bf16[4,8,1024]{2,1,0:T(8,128)(2,1)S(1)}, u32[]{:S(2)}, u32[]{:S(2)}) collective-permute-start(bf16[4,8,1024]{2,1,0:T(8,128)(2,1)S(1)} %get-tuple-element.34), channel_id=1, source_target_pairs={{0,24},{4,28},{8,0},{12,4},{16,8},{20,12},{24,16},{28,20},{1,25},{... | collective-permute-start | bytes 196616 | tf_op jit(solution)/shard_map/ppermute | solution.py:19
  121.4 2.7 %collective-permute-start.26 = (bf16[8,8,1024]{2,1,0:T(8,128)(2,1)S(1)}, bf16[8,8,1024]{2,1,0:T(8,128)(2,1)S(1)}, u32[]{:S(2)}, u32[]{:S(2)}) collective-permute-start(bf16[8,8,1024]{2,1,0:T(8,128)(2,1)S(1)} %get-tuple-element.32), channel_id=1, source_target_pairs={{0,28},{4,0},{8,4},{12,8},{16,12},{20,16},{24,20},{28,24},{1,29},{... | collective-permute-start | bytes 393224 | tf_op jit(solution)/shard_map/ppermute | solution.py:19
  124.6 3.6 %collective-permute-start.32 = (bf16[8,8,1024]{2,1,0:T(8,128)(2,1)S(1)}, bf16[8,8,1024]{2,1,0:T(8,128)(2,1)S(1)}, u32[]{:S(2)}, u32[]{:S(2)}) collective-permute-start(bf16[8,8,1024]{2,1,0:T(8,128)(2,1)S(1)} %pad_maximum_fusion.12), channel_id=1, source_target_pairs={{0,24},{4,28},{8,0},{12,4},{16,8},{20,12},{24,16},{28,20},{1,25},{... | collective-permute-start | bytes 393224 | tf_op jit(solution)/shard_map/ppermute | solution.py:19
  128.3 3.5 %collective-permute-done.29 = bf16[8,8,1024]{2,1,0:T(8,128)(2,1)S(1)} collective-permute-done((bf16[8,8,1024]{2,1,0:T(8,128)(2,1)S(1)}, bf16[8,8,1024]{2,1,0:T(8,128)(2,1)S(1)}, u32[]{:S(2)}, u32[]{:S(2)}) %collective-permute-start.29) | collective-permute-done | bytes 131104 | tf_op jit(solution)/shard_map/ppermute | solution.py:19
  133.5 2.5 %collective-permute-start.33 = (bf16[8,8,1024]{2,1,0:T(8,128)(2,1)S(1)}, bf16[8,8,1024]{2,1,0:T(8,128)(2,1)S(1)}, u32[]{:S(2)}, u32[]{:S(2)}) collective-permute-start(bf16[8,8,1024]{2,1,0:T(8,128)(2,1)S(1)} %fusion.29), channel_id=1, source_target_pairs={{0,2},{2,0},{1,3},{3,1},{4,6},{6,4},{5,7},{7,5},{8,10},{10,8},{9,1... | collective-permute-start | bytes 393224 | tf_op jit(solution)/shard_map/ppermute | solution.py:19
  135.9 2.9 %collective-permute-done.33 = bf16[8,8,1024]{2,1,0:T(8,128)(2,1)S(1)} collective-permute-done((bf16[8,8,1024]{2,1,0:T(8,128)(2,1)S(1)}, bf16[8,8,1024]{2,1,0:T(8,128)(2,1)S(1)}, u32[]{:S(2)}, u32[]{:S(2)}) %collective-permute-start.33) | collective-permute-done | bytes 131104 | tf_op jit(solution)/shard_map/ppermute | solution.py:19
  139.2 2.8 %collective-permute-done.34 = f32[8,8]{1,0:T(8,128)S(1)} collective-permute-done((f32[8,8]{1,0:T(8,128)S(1)}, f32[8,8]{1,0:T(8,128)S(1)}, u32[]{:S(2)}, u32[]{:S(2)}) %collective-permute-start.34) | collective-permute-done | bytes 288 | tf_op jit(solution)/shard_map/ppermute | solution.py:23
  147.1 13.8 %all_to_all.15 = bf16[8,8,1024]{2,1,0:T(8,128)(2,1)S(1)} all-to-all(bf16[8,8,1024]{2,1,0:T(8,128)(2,1)S(1)} %broadcast_in_dim.4), channel_id=1, replica_groups=mesh['x'=4,'y'=2,'z'=8,'w'=2,'c'=2] {'z'}, dimensions={0} | all-to-all | bytes 262144 | tf_op jit(solution)/shard_map/all_to_all | solution.py:141
  160.9 7.2 %collective-permute-start.38 = (bf16[64,1024]{1,0:T(8,128)(2,1)S(1)}, bf16[64,1024]{1,0:T(8,128)(2,1)S(1)}, u32[]{:S(2)}, u32[]{:S(2)}) collective-permute-start(bf16[64,1024]{1,0:T(8,128)(2,1)S(1)} %bitcast.202), channel_id=1, source_target_pairs={{0,1},{1,0},{2,3},{3,2},{4,5},{5,4},{6,7},{7,6},{8,9},{9,8},{10,11... | collective-permute-start | bytes 393224 | tf_op jit(solution)/shard_map/ppermute | solution.py:23
  169.2 3.5 %convolution_convert_fusion = bf16[128,2688]{1,0:T(8,128)(2,1)S(1)} fusion(bf16[1024,2688]{1,0:T(8,128)(2,1)} %param.13, bf16[64,1024]{1,0:T(8,128)(2,1)S(1)} %get-tuple-element.54, bf16[64,1024]{1,0:T(8,128)(2,1)S(1)} %get-tuple-element.53), kind=kOutput, calls=%fused_computation | convolution fusion | flops 705511424 | bytes 6455296 | tf_op jit(solution)/shard_map/dot_general | solution.py:147
  172.7 14.0 %all_to_all.16 = bf16[8,16,2688]{2,1,0:T(8,128)(2,1)S(1)} all-to-all(bf16[8,16,2688]{2,1,0:T(8,128)(2,1)S(1)} %bitcast.188), channel_id=1, replica_groups=mesh['x'=4,'y'=2,'z'=8,'w'=2,'c'=2] {'x','y'}, dimensions={0} | all-to-all | bytes 1376256 | tf_op jit(solution)/shard_map/all_to_all | solution.py:149
  187.2 15.3 %all_to_all.17 = f32[32,1,16]{2,1,0:T(1,128)S(1)} all-to-all(f32[32,1,16]{2,1,0:T(1,128)S(1)} %broadcast_in_dim.5), channel_id=1, replica_groups=mesh['x'=4,'y'=2,'z'=8,'w'=2,'c'=2] {'z','w','c'}, dimensions={0} | all-to-all | bytes 4096 | tf_op jit(solution)/shard_map/all_to_all | solution.py:154
  (143 shorter events, 46.3 us)
Async XLA Ops:
  2.8 10.0 %collective-permute-start = (bf16[64,1024]{1,0:T(8,128)(2,1)}, bf16[64,1024]{1,0:T(8,128)(2,1)S(1)}, u32[]{:S(2)}, u32[]{:S(2)}) collective-permute-start(bf16[64,1024]{1,0:T(8,128)(2,1)} %get-tuple-element.14), channel_id=1, source_target_pairs={{0,32},{32,0},{64,96},{96,64},{128,160},{160,128},{192,224},{224,1... | collective-permute-start | bytes 393224 | tf_op jit(solution)/shard_map/ppermute | solution.py:31
  4.9 11.1 %collective-permute-start.1 = (bf16[64,1024]{1,0:T(8,128)(2,1)}, bf16[64,1024]{1,0:T(8,128)(2,1)S(1)}, u32[]{:S(2)}, u32[]{:S(2)}) collective-permute-start(bf16[64,1024]{1,0:T(8,128)(2,1)} %get-tuple-element.15), channel_id=1, source_target_pairs={{0,64},{32,96},{64,0},{96,32},{128,192},{160,224},{192,128},{224,1... | collective-permute-start | bytes 393224 | tf_op jit(solution)/shard_map/ppermute | solution.py:31
  6.1 10.6 %collective-permute-start.2 = (bf16[64,1024]{1,0:T(8,128)(2,1)}, bf16[64,1024]{1,0:T(8,128)(2,1)S(1)}, u32[]{:S(2)}, u32[]{:S(2)}) collective-permute-start(bf16[64,1024]{1,0:T(8,128)(2,1)} %get-tuple-element.16), channel_id=1, source_target_pairs={{0,96},{32,64},{64,32},{96,0},{128,224},{160,192},{192,160},{224,1... | collective-permute-start | bytes 393224 | tf_op jit(solution)/shard_map/ppermute | solution.py:31
  6.1 11.2 %collective-permute-start.3 = (bf16[64,1024]{1,0:T(8,128)(2,1)}, bf16[64,1024]{1,0:T(8,128)(2,1)S(1)}, u32[]{:S(2)}, u32[]{:S(2)}) collective-permute-start(bf16[64,1024]{1,0:T(8,128)(2,1)} %get-tuple-element.17), channel_id=1, source_target_pairs={{0,128},{32,160},{64,192},{96,224},{128,0},{160,32},{192,64},{224,... | collective-permute-start | bytes 393224 | tf_op jit(solution)/shard_map/ppermute | solution.py:31
  9.0 10.9 %collective-permute-start.4 = (bf16[64,1024]{1,0:T(8,128)(2,1)}, bf16[64,1024]{1,0:T(8,128)(2,1)S(1)}, u32[]{:S(2)}, u32[]{:S(2)}) collective-permute-start(bf16[64,1024]{1,0:T(8,128)(2,1)} %get-tuple-element.18), channel_id=1, source_target_pairs={{0,160},{32,128},{64,224},{96,192},{128,32},{160,0},{192,96},{224,... | collective-permute-start | bytes 393224 | tf_op jit(solution)/shard_map/ppermute | solution.py:31
  12.8 11.1 %collective-permute-start.5 = (bf16[64,1024]{1,0:T(8,128)(2,1)}, bf16[64,1024]{1,0:T(8,128)(2,1)S(1)}, u32[]{:S(2)}, u32[]{:S(2)}) collective-permute-start(bf16[64,1024]{1,0:T(8,128)(2,1)} %get-tuple-element.19), channel_id=1, source_target_pairs={{0,192},{32,224},{64,128},{96,160},{128,64},{160,96},{192,0},{224,... | collective-permute-start | bytes 393224 | tf_op jit(solution)/shard_map/ppermute | solution.py:31
  16.0 10.6 %collective-permute-start.6 = (bf16[64,1024]{1,0:T(8,128)(2,1)}, bf16[64,1024]{1,0:T(8,128)(2,1)S(1)}, u32[]{:S(2)}, u32[]{:S(2)}) collective-permute-start(bf16[64,1024]{1,0:T(8,128)(2,1)} %get-tuple-element.20), channel_id=1, source_target_pairs={{0,224},{32,192},{64,160},{96,128},{128,96},{160,64},{192,32},{224... | collective-permute-start | bytes 393224 | tf_op jit(solution)/shard_map/ppermute | solution.py:31
  27.3 6.0 %collective-permute-start.15 = (bf16[8,64,1024]{2,1,0:T(8,128)(2,1)}, bf16[8,64,1024]{2,1,0:T(8,128)(2,1)S(1)}, u32[]{:S(2)}, u32[]{:S(2)}) collective-permute-start(bf16[8,64,1024]{2,1,0:T(8,128)(2,1)} %bitcast_dynamic-update-slice_fusion), channel_id=1, source_target_pairs={{0,1},{1,0},{2,3},{3,2},{4,5},{5,4},{6,7},{7,6},{8,9},{9,8},{10,11... | collective-permute-start | bytes 3145736 | tf_op jit(solution)/shard_map/ppermute | solution.py:23
  31.9 28.5 %collective-permute-start.7 = (bf16[2,4,64,896]{3,2,1,0:T(8,128)(2,1)S(1)}, bf16[2,4,64,896]{3,2,1,0:T(8,128)(2,1)S(1)}, u32[]{:S(2)}, u32[]{:S(2)}) collective-permute-start(bf16[2,4,64,896]{3,2,1,0:T(8,128)(2,1)S(1)} %pad_maximum_fusion), channel_id=1, source_target_pairs={{0,32},{32,0},{1,33},{33,1},{2,34},{34,2},{3,35},{35,3},{4,36},{36... | collective-permute-start | bytes 2752520 | tf_op jit(solution)/shard_map/ppermute | solution.py:23
  36.0 13.4 %collective-permute-start.16 = (bf16[2,2,64,896]{3,2,1,0:T(8,128)(2,1)S(1)}, bf16[2,2,64,896]{3,2,1,0:T(8,128)(2,1)S(1)}, u32[]{:S(2)}, u32[]{:S(2)}) collective-permute-start(bf16[2,2,64,896]{3,2,1,0:T(8,128)(2,1)S(1)} %pad_maximum_fusion.2), channel_id=1, source_target_pairs={{0,128},{64,192},{128,0},{192,64},{1,129},{65,193},{129,1},{193,65... | collective-permute-start | bytes 1376264 | tf_op jit(solution)/shard_map/ppermute | solution.py:23
  36.6 20.4 %collective-permute-start.17 = (bf16[2,2,64,896]{3,2,1,0:T(8,128)(2,1)S(1)}, bf16[2,2,64,896]{3,2,1,0:T(8,128)(2,1)S(1)}, u32[]{:S(2)}, u32[]{:S(2)}) collective-permute-start(bf16[2,2,64,896]{3,2,1,0:T(8,128)(2,1)S(1)} %pad_maximum_fusion.3), channel_id=1, source_target_pairs={{0,64},{64,0},{128,192},{192,128},{1,65},{65,1},{129,193},{193,129... | collective-permute-start | bytes 1376264 | tf_op jit(solution)/shard_map/ppermute | solution.py:23
  37.0 22.8 %collective-permute-start.18 = (bf16[2,2,64,896]{3,2,1,0:T(8,128)(2,1)S(1)}, bf16[2,2,64,896]{3,2,1,0:T(8,128)(2,1)S(1)}, u32[]{:S(2)}, u32[]{:S(2)}) collective-permute-start(bf16[2,2,64,896]{3,2,1,0:T(8,128)(2,1)S(1)} %pad_maximum_fusion.4), channel_id=1, source_target_pairs={{0,192},{64,128},{128,64},{192,0},{1,193},{65,129},{129,65},{193,1... | collective-permute-start | bytes 1376264 | tf_op jit(solution)/shard_map/ppermute | solution.py:23
  60.1 6.8 %collective-permute-start.19 = (bf16[2,64,896]{2,1,0:T(8,128)(2,1)S(1)}, bf16[2,64,896]{2,1,0:T(8,128)(2,1)S(1)}, u32[]{:S(2)}, u32[]{:S(2)}) collective-permute-start(bf16[2,64,896]{2,1,0:T(8,128)(2,1)S(1)} %pad_maximum_fusion.10), channel_id=1, source_target_pairs={{0,32},{32,0},{1,33},{33,1},{2,34},{34,2},{3,35},{35,3},{4,36},{36... | collective-permute-start | bytes 688136 | tf_op jit(solution)/shard_map/ppermute | solution.py:23
  67.2 6.3 %collective-permute-start.21 = (bf16[64,896]{1,0:T(8,128)(2,1)S(1)}, bf16[64,896]{1,0:T(8,128)(2,1)S(1)}, u32[]{:S(2)}, u32[]{:S(2)}) collective-permute-start(bf16[64,896]{1,0:T(8,128)(2,1)S(1)} %fusion.30), channel_id=1, source_target_pairs={{0,128},{64,192},{128,0},{192,64},{1,129},{65,193},{129,1},{193,65... | collective-permute-start | bytes 344072 | tf_op jit(solution)/shard_map/ppermute | solution.py:23
  68.5 7.4 %collective-permute-start.22 = (bf16[64,896]{1,0:T(8,128)(2,1)S(1)}, bf16[64,896]{1,0:T(8,128)(2,1)S(1)}, u32[]{:S(2)}, u32[]{:S(2)}) collective-permute-start(bf16[64,896]{1,0:T(8,128)(2,1)S(1)} %fusion.30), channel_id=1, source_target_pairs={{0,192},{64,128},{128,64},{192,0},{1,193},{65,129},{129,65},{193,1... | collective-permute-start | bytes 344072 | tf_op jit(solution)/shard_map/ppermute | solution.py:23
  76.0 10.8 %collective-permute-start.23 = (bf16[4,64,896]{2,1,0:T(8,128)(2,1)S(1)}, bf16[4,64,896]{2,1,0:T(8,128)(2,1)S(1)}, u32[]{:S(2)}, u32[]{:S(2)}) collective-permute-start(bf16[4,64,896]{2,1,0:T(8,128)(2,1)S(1)} %get-tuple-element.52), channel_id=1, source_target_pairs={{0,32},{32,0},{1,33},{33,1},{2,34},{34,2},{3,35},{35,3},{4,36},{36... | collective-permute-start | bytes 1376264 | tf_op jit(solution)/shard_map/ppermute | solution.py:23
  76.8 13.6 %collective-permute-start.8 = (bf16[2,64,896]{2,1,0:T(8,128)(2,1)S(1)}, bf16[2,64,896]{2,1,0:T(8,128)(2,1)S(1)}, u32[]{:S(2)}, u32[]{:S(2)}) collective-permute-start(bf16[2,64,896]{2,1,0:T(8,128)(2,1)S(1)} %pad_maximum_fusion.6), channel_id=1, source_target_pairs={{0,128},{64,192},{128,0},{192,64},{1,129},{65,193},{129,1},{193,65... | collective-permute-start | bytes 688136 | tf_op jit(solution)/shard_map/ppermute | solution.py:23
  76.9 13.4 %collective-permute-start.9 = (bf16[2,64,896]{2,1,0:T(8,128)(2,1)S(1)}, bf16[2,64,896]{2,1,0:T(8,128)(2,1)S(1)}, u32[]{:S(2)}, u32[]{:S(2)}) collective-permute-start(bf16[2,64,896]{2,1,0:T(8,128)(2,1)S(1)} %pad_maximum_fusion.7), channel_id=1, source_target_pairs={{0,64},{64,0},{128,192},{192,128},{1,65},{65,1},{129,193},{193,129... | collective-permute-start | bytes 688136 | tf_op jit(solution)/shard_map/ppermute | solution.py:23
  79.3 11.1 %collective-permute-start.10 = (bf16[2,64,896]{2,1,0:T(8,128)(2,1)S(1)}, bf16[2,64,896]{2,1,0:T(8,128)(2,1)S(1)}, u32[]{:S(2)}, u32[]{:S(2)}) collective-permute-start(bf16[2,64,896]{2,1,0:T(8,128)(2,1)S(1)} %pad_maximum_fusion.8), channel_id=1, source_target_pairs={{0,192},{64,128},{128,64},{192,0},{1,193},{65,129},{129,65},{193,1... | collective-permute-start | bytes 688136 | tf_op jit(solution)/shard_map/ppermute | solution.py:23
  88.0 22.6 %collective-permute-start.24 = (bf16[4,2,64,1024]{3,2,1,0:T(8,128)(2,1)S(1)}, bf16[4,2,64,1024]{3,2,1,0:T(8,128)(2,1)S(1)}, u32[]{:S(2)}, u32[]{:S(2)}) collective-permute-start(bf16[4,2,64,1024]{3,2,1,0:T(8,128)(2,1)S(1)} %fusion.8), channel_id=1, source_target_pairs={{0,1},{1,0},{2,3},{3,2},{4,5},{5,4},{6,7},{7,6},{8,9},{9,8},{10,11... | collective-permute-start | bytes 3145736 | tf_op jit(solution)/shard_map/ppermute | solution.py:23
  94.4 13.1 %collective-permute-start.13 = (bf16[2,64,896]{2,1,0:T(8,128)(2,1)S(1)}, bf16[2,64,896]{2,1,0:T(8,128)(2,1)S(1)}, u32[]{:S(2)}, u32[]{:S(2)}) collective-permute-start(bf16[2,64,896]{2,1,0:T(8,128)(2,1)S(1)} %get-tuple-element.56), channel_id=1, source_target_pairs={{0,128},{64,192},{128,0},{192,64},{1,129},{65,193},{129,1},{193,65... | collective-permute-start | bytes 688136 | tf_op jit(solution)/shard_map/ppermute | solution.py:23
  98.2 12.4 %collective-permute-start.14 = (bf16[2,64,896]{2,1,0:T(8,128)(2,1)S(1)}, bf16[2,64,896]{2,1,0:T(8,128)(2,1)S(1)}, u32[]{:S(2)}, u32[]{:S(2)}) collective-permute-start(bf16[2,64,896]{2,1,0:T(8,128)(2,1)S(1)} %get-tuple-element.56), channel_id=1, source_target_pairs={{0,192},{64,128},{128,64},{192,0},{1,193},{65,129},{129,65},{193,1... | collective-permute-start | bytes 688136 | tf_op jit(solution)/shard_map/ppermute | solution.py:23
  111.9 9.4 %collective-permute-start.27 = (bf16[8,8,1024]{2,1,0:T(8,128)(2,1)S(1)}, bf16[8,8,1024]{2,1,0:T(8,128)(2,1)S(1)}, u32[]{:S(2)}, u32[]{:S(2)}) collective-permute-start(bf16[8,8,1024]{2,1,0:T(8,128)(2,1)S(1)} %get-tuple-element.30), channel_id=1, source_target_pairs={{0,4},{4,8},{8,12},{12,16},{16,20},{20,24},{24,28},{28,0},{1,5},{5... | collective-permute-start | bytes 393224 | tf_op jit(solution)/shard_map/ppermute | solution.py:19
  113.7 10.4 %collective-permute-start.30 = (bf16[8,8,1024]{2,1,0:T(8,128)(2,1)S(1)}, bf16[8,8,1024]{2,1,0:T(8,128)(2,1)S(1)}, u32[]{:S(2)}, u32[]{:S(2)}) collective-permute-start(bf16[8,8,1024]{2,1,0:T(8,128)(2,1)S(1)} %get-tuple-element.31), channel_id=1, source_target_pairs={{0,28},{4,0},{8,4},{12,8},{16,12},{20,16},{24,20},{28,24},{1,29},{... | collective-permute-start | bytes 393224 | tf_op jit(solution)/shard_map/ppermute | solution.py:19
  117.7 6.7 %collective-permute-start.28 = (bf16[4,8,1024]{2,1,0:T(8,128)(2,1)S(1)}, bf16[4,8,1024]{2,1,0:T(8,128)(2,1)S(1)}, u32[]{:S(2)}, u32[]{:S(2)}) collective-permute-start(bf16[4,8,1024]{2,1,0:T(8,128)(2,1)S(1)} %get-tuple-element.33), channel_id=1, source_target_pairs={{0,8},{4,12},{8,16},{12,20},{16,24},{20,28},{24,0},{28,4},{1,9},{5... | collective-permute-start | bytes 196616 | tf_op jit(solution)/shard_map/ppermute | solution.py:19
  117.8 6.7 %collective-permute-start.31 = (bf16[4,8,1024]{2,1,0:T(8,128)(2,1)S(1)}, bf16[4,8,1024]{2,1,0:T(8,128)(2,1)S(1)}, u32[]{:S(2)}, u32[]{:S(2)}) collective-permute-start(bf16[4,8,1024]{2,1,0:T(8,128)(2,1)S(1)} %get-tuple-element.34), channel_id=1, source_target_pairs={{0,24},{4,28},{8,0},{12,4},{16,8},{20,12},{24,16},{28,20},{1,25},{... | collective-permute-start | bytes 196616 | tf_op jit(solution)/shard_map/ppermute | solution.py:19
  121.4 6.9 %collective-permute-start.25 = (bf16[8,8,1024]{2,1,0:T(8,128)(2,1)S(1)}, bf16[8,8,1024]{2,1,0:T(8,128)(2,1)S(1)}, u32[]{:S(2)}, u32[]{:S(2)}) collective-permute-start(bf16[8,8,1024]{2,1,0:T(8,128)(2,1)S(1)} %get-tuple-element.29), channel_id=1, source_target_pairs={{0,4},{4,8},{8,12},{12,16},{16,20},{20,24},{24,28},{28,0},{1,5},{5... | collective-permute-start | bytes 393224 | tf_op jit(solution)/shard_map/ppermute | solution.py:19
  121.4 6.9 %collective-permute-start.26 = (bf16[8,8,1024]{2,1,0:T(8,128)(2,1)S(1)}, bf16[8,8,1024]{2,1,0:T(8,128)(2,1)S(1)}, u32[]{:S(2)}, u32[]{:S(2)}) collective-permute-start(bf16[8,8,1024]{2,1,0:T(8,128)(2,1)S(1)} %get-tuple-element.32), channel_id=1, source_target_pairs={{0,28},{4,0},{8,4},{12,8},{16,12},{20,16},{24,20},{28,24},{1,29},{... | collective-permute-start | bytes 393224 | tf_op jit(solution)/shard_map/ppermute | solution.py:19
  124.4 7.4 %collective-permute-start.29 = (bf16[8,8,1024]{2,1,0:T(8,128)(2,1)S(1)}, bf16[8,8,1024]{2,1,0:T(8,128)(2,1)S(1)}, u32[]{:S(2)}, u32[]{:S(2)}) collective-permute-start(bf16[8,8,1024]{2,1,0:T(8,128)(2,1)S(1)} %pad_maximum_fusion.11), channel_id=1, source_target_pairs={{0,8},{4,12},{8,16},{12,20},{16,24},{20,28},{24,0},{28,4},{1,9},{5... | collective-permute-start | bytes 393224 | tf_op jit(solution)/shard_map/ppermute | solution.py:19
  124.6 8.8 %collective-permute-start.32 = (bf16[8,8,1024]{2,1,0:T(8,128)(2,1)S(1)}, bf16[8,8,1024]{2,1,0:T(8,128)(2,1)S(1)}, u32[]{:S(2)}, u32[]{:S(2)}) collective-permute-start(bf16[8,8,1024]{2,1,0:T(8,128)(2,1)S(1)} %pad_maximum_fusion.12), channel_id=1, source_target_pairs={{0,24},{4,28},{8,0},{12,4},{16,8},{20,12},{24,16},{28,20},{1,25},{... | collective-permute-start | bytes 393224 | tf_op jit(solution)/shard_map/ppermute | solution.py:19
  133.5 5.4 %collective-permute-start.33 = (bf16[8,8,1024]{2,1,0:T(8,128)(2,1)S(1)}, bf16[8,8,1024]{2,1,0:T(8,128)(2,1)S(1)}, u32[]{:S(2)}, u32[]{:S(2)}) collective-permute-start(bf16[8,8,1024]{2,1,0:T(8,128)(2,1)S(1)} %fusion.29), channel_id=1, source_target_pairs={{0,2},{2,0},{1,3},{3,1},{4,6},{6,4},{5,7},{7,5},{8,10},{10,8},{9,1... | collective-permute-start | bytes 393224 | tf_op jit(solution)/shard_map/ppermute | solution.py:19
  160.9 8.2 %collective-permute-start.38 = (bf16[64,1024]{1,0:T(8,128)(2,1)S(1)}, bf16[64,1024]{1,0:T(8,128)(2,1)S(1)}, u32[]{:S(2)}, u32[]{:S(2)}) collective-permute-start(bf16[64,1024]{1,0:T(8,128)(2,1)S(1)} %bitcast.202), channel_id=1, source_target_pairs={{0,1},{1,0},{2,3},{3,2},{4,5},{5,4},{6,7},{7,6},{8,9},{9,8},{10,11... | collective-permute-start | bytes 393224 | tf_op jit(solution)/shard_map/ppermute | solution.py:23
  (14 other events, 133.9 us)

commit v5 on v4

--- a/solution.py
+++ b/solution.py
@@ -131,8 +131,11 @@
     variant_at = offsets ^ (x * NY + y)
     placed_at = (variant_at[None, :] == offsets[:, None]).astype(F32)
     by_variant = jnp.sum(placed_at[:, :, None] * partial_square[None], axis=1)
-    square = by_variant + paired(by_variant, "y", NY, 1)
-    square = square + sum([paired(square, "x", NX, d) for d in TURNS])
+    everyone = lax.all_to_all(
+        jnp.broadcast_to(by_variant[None], (NX * NY, *by_variant.shape)),
+        PROMPT, 0, 0, tiled=True,
+    )
+    square = everyone.sum(axis=0)
     scale = lax.rsqrt(square / D + EPS) * guidance[:, None]
     scale = jnp.sum(placed_at[:, :, None] * scale[:, None], axis=0)
     mixed = (jnp.sum(state * scale[:, :, None], axis=0) * norm_gain).astype(BF)

time: 204 us -> 201 us (0.985)
  blocking collectives: 43.2 us -> 50.1 us
  starting transfers between devices: 59.7 us -> 54.6 us
  waiting for transfers between devices: 73.6 us -> 69.2 us
    all_to_all x0 -> x1, blocking collectives: none -> 7.44 us  [step(): lax.all_to_all(jnp.broadcast_to(by_variant[None], (NX * NY, *by_variant.s...]
    ppermute x23 -> x19, starting transfers between devices: 31.5 us -> 26.4 us  [paired(): return lax.ppermute(array, axis, [(i, i ^ bit) for i in range(size)])]
    ppermute x23 -> x19, waiting for transfers between devices: 57.9 us -> 53.6 us  [paired(): return lax.ppermute(array, axis, [(i, i ^ bit) for i in range(size)])]
  transfers between devices with their start and end apart: 39 -> 35, of which waited for: 22 -> 19; matrix products, arithmetic and copies ran while one was open for 8% -> 8% of each run, Pallas kernels for 0% -> 0%
where the time goes in v5:
time: 201 us
  waiting for transfers between devices  69.2 us (34%)
  starting transfers between devices  54.6 us (27%)
  blocking collectives  50.1 us (25%)
  matrix products  12.4 us (6%)
  local copies, waits for them, and re-layouts  7.65 us (4%)
  other arithmetic  3.55 us (2%)
  Pallas kernels  2.74 us (1%)
    ppermute x19, waiting for transfers between devices, paired(): return lax.ppermute(array, axis, [(i, i ^ bit) for i in range(size)])  53.6 us
    ppermute x19, starting transfers between devices, paired(): return lax.ppermute(array, axis, [(i, i ^ bit) for i in range(size)])  26.4 us
    ppermute x9, starting transfers between devices, shifted(): lax.ppermute(array, axis, [(i, (i + step) % size) for i in range(size)])  18.2 us
    all_to_all x1, blocking collectives, step(): lax.all_to_all(jnp.broadcast_to(part_lse[None, None], (shards, 1, part_ls...  14.9 us
    all_to_all x1, blocking collectives, step(): ring = lax.all_to_all(ring, 'z', 0, 0, tiled=True).reshape(-1, share)  14.3 us
    all_to_all x1, blocking collectives, step(): tiles = lax.all_to_all(tiles, PROMPT, 0, 0, tiled=True)  13.5 us
    ppermute x7, starting transfers between devices, paired_prompt(): return lax.ppermute(array, PROMPT, [(p, p ^ k) for p in range(NX * NY)])  10 us
    dot_general x6, matrix products, products(): jnp.dot(flat, weight, preferred_element_type=F32)  8.89 us
  transfers between devices with their start and end apart: 35, of which 19 were waited for; matrix products, arithmetic and copies ran while one was open for 8% of the time, Pallas kernels for 0%

profile of v5, /device:TPU:1, one launch (start us, length us, event | category | flops | bytes accessed | tf_op | source)
XLA Modules:
  0.0 200.8 jit_solution(9767383985058829939)
XLA Ops:
  0.0 2.7 %shard_map.82 = (bf16[64,1024]{1,0:T(8,128)(2,1)}, bf16[64,1024]{1,0:T(8,128)(2,1)}, bf16[64,1024]{1,0:T(8,128)(2,1)}, bf16[64,1024]{1,0:T(8,128)(2,1)}, bf16[64...) custom-call(bf16[128,8192]{1,0:T(8,128)(2,1)} %bitcast.189), custom_call_target="tpu_custom_call" | custom-call | tf_op jit(solution)/shard_map/pallas_call | solution.py:46
  6.1 2.9 %collective-permute-start.3 = (bf16[64,1024]{1,0:T(8,128)(2,1)}, bf16[64,1024]{1,0:T(8,128)(2,1)S(1)}, u32[]{:S(2)}, u32[]{:S(2)}) collective-permute-start(bf16[64,1024]{1,0:T(8,128)(2,1)} %get-tuple-element.17), channel_id=1, source_target_pairs={{0,128},{32,160},{64,192},{96,224},{128,0},{160,32},{192,64},{224,... | collective-permute-start | bytes 393224 | tf_op jit(solution)/shard_map/ppermute | solution.py:31
  12.8 2.6 %collective-permute-start.5 = (bf16[64,1024]{1,0:T(8,128)(2,1)}, bf16[64,1024]{1,0:T(8,128)(2,1)S(1)}, u32[]{:S(2)}, u32[]{:S(2)}) collective-permute-start(bf16[64,1024]{1,0:T(8,128)(2,1)} %get-tuple-element.19), channel_id=1, source_target_pairs={{0,192},{32,224},{64,128},{96,160},{128,64},{160,96},{192,0},{224,... | collective-permute-start | bytes 393224 | tf_op jit(solution)/shard_map/ppermute | solution.py:31
  20.5 3.3 %collective-permute-done.5 = bf16[64,1024]{1,0:T(8,128)(2,1)S(1)} collective-permute-done((bf16[64,1024]{1,0:T(8,128)(2,1)}, bf16[64,1024]{1,0:T(8,128)(2,1)S(1)}, u32[]{:S(2)}, u32[]{:S(2)}) %collective-permute-start.5) | collective-permute-done | bytes 131104 | tf_op jit(solution)/shard_map/ppermute | solution.py:31
  27.8 2.6 %fusion = f32[4,2,64,896]{3,2,1,0:T(8,128)S(1)} fusion(bf16[4,2,64,1024]{3,2,1,0:T(8,128)(2,1)} %bitcast.208, bf16[1024,896]{1,0:T(8,128)(2,1)S(1)} %copy-done), kind=kOutput, calls=%fused_computation.2 | convolution fusion | flops 939524096 | bytes 4718592 | tf_op jit(solution)/shard_map/dot_general | solution.py:61
  37.0 2.5 %collective-permute-start.18 = (bf16[2,2,64,896]{3,2,1,0:T(8,128)(2,1)S(1)}, bf16[2,2,64,896]{3,2,1,0:T(8,128)(2,1)S(1)}, u32[]{:S(2)}, u32[]{:S(2)}) collective-permute-start(bf16[2,2,64,896]{3,2,1,0:T(8,128)(2,1)S(1)} %pad_maximum_fusion.4), channel_id=1, source_target_pairs={{0,192},{64,128},{128,64},{192,0},{1,193},{65,129},{129,65},{193,1... | collective-permute-start | bytes 1376264 | tf_op jit(solution)/shard_map/ppermute | solution.py:23
  39.7 9.7 %collective-permute-done.16 = bf16[2,2,64,896]{3,2,1,0:T(8,128)(2,1)S(1)} collective-permute-done((bf16[2,2,64,896]{3,2,1,0:T(8,128)(2,1)S(1)}, bf16[2,2,64,896]{3,2,1,0:T(8,128)(2,1)S(1)}, u32[]{:S(2)}, u32[]{:S(2)}) %collective-permute-start.16) | collective-permute-done | bytes 458784 | tf_op jit(solution)/shard_map/ppermute | solution.py:23
  49.4 7.7 %collective-permute-done.17 = bf16[2,2,64,896]{3,2,1,0:T(8,128)(2,1)S(1)} collective-permute-done((bf16[2,2,64,896]{3,2,1,0:T(8,128)(2,1)S(1)}, bf16[2,2,64,896]{3,2,1,0:T(8,128)(2,1)S(1)}, u32[]{:S(2)}, u32[]{:S(2)}) %collective-permute-start.17) | collective-permute-done | bytes 458784 | tf_op jit(solution)/shard_map/ppermute | solution.py:23
  57.1 2.8 %collective-permute-done.18 = bf16[2,2,64,896]{3,2,1,0:T(8,128)(2,1)S(1)} collective-permute-done((bf16[2,2,64,896]{3,2,1,0:T(8,128)(2,1)S(1)}, bf16[2,2,64,896]{3,2,1,0:T(8,128)(2,1)S(1)}, u32[]{:S(2)}, u32[]{:S(2)}) %collective-permute-start.18) | collective-permute-done | bytes 458784 | tf_op jit(solution)/shard_map/ppermute | solution.py:23
  60.7 6.2 %collective-permute-done.19 = bf16[2,64,896]{2,1,0:T(8,128)(2,1)S(1)} collective-permute-done((bf16[2,64,896]{2,1,0:T(8,128)(2,1)S(1)}, bf16[2,64,896]{2,1,0:T(8,128)(2,1)S(1)}, u32[]{:S(2)}, u32[]{:S(2)}) %collective-permute-start.19) | collective-permute-done | bytes 229408 | tf_op jit(solution)/shard_map/ppermute | solution.py:23
  68.5 2.6 %collective-permute-start.22 = (bf16[64,896]{1,0:T(8,128)(2,1)S(1)}, bf16[64,896]{1,0:T(8,128)(2,1)S(1)}, u32[]{:S(2)}, u32[]{:S(2)}) collective-permute-start(bf16[64,896]{1,0:T(8,128)(2,1)S(1)} %fusion.30), channel_id=1, source_target_pairs={{0,192},{64,128},{128,64},{192,0},{1,193},{65,129},{129,65},{193,1... | collective-permute-start | bytes 344072 | tf_op jit(solution)/shard_map/ppermute | solution.py:23
  71.2 2.4 %collective-permute-done.21 = bf16[64,896]{1,0:T(8,128)(2,1)S(1)} collective-permute-done((bf16[64,896]{1,0:T(8,128)(2,1)S(1)}, bf16[64,896]{1,0:T(8,128)(2,1)S(1)}, u32[]{:S(2)}, u32[]{:S(2)}) %collective-permute-start.21) | collective-permute-done | bytes 114720 | tf_op jit(solution)/shard_map/ppermute | solution.py:23
  73.6 2.3 %collective-permute-done.22 = bf16[64,896]{1,0:T(8,128)(2,1)S(1)} collective-permute-done((bf16[64,896]{1,0:T(8,128)(2,1)S(1)}, bf16[64,896]{1,0:T(8,128)(2,1)S(1)}, u32[]{:S(2)}, u32[]{:S(2)}) %collective-permute-start.22) | collective-permute-done | bytes 114720 | tf_op jit(solution)/shard_map/ppermute | solution.py:23
  76.9 2.3 %collective-permute-start.9 = (bf16[2,64,896]{2,1,0:T(8,128)(2,1)S(1)}, bf16[2,64,896]{2,1,0:T(8,128)(2,1)S(1)}, u32[]{:S(2)}, u32[]{:S(2)}) collective-permute-start(bf16[2,64,896]{2,1,0:T(8,128)(2,1)S(1)} %pad_maximum_fusion.7), channel_id=1, source_target_pairs={{0,64},{64,0},{128,192},{192,128},{1,65},{65,1},{129,193},{193,129... | collective-permute-start | bytes 688136 | tf_op jit(solution)/shard_map/ppermute | solution.py:23
  80.4 6.4 %collective-permute-done.23 = bf16[4,64,896]{2,1,0:T(8,128)(2,1)S(1)} collective-permute-done((bf16[4,64,896]{2,1,0:T(8,128)(2,1)S(1)}, bf16[4,64,896]{2,1,0:T(8,128)(2,1)S(1)}, u32[]{:S(2)}, u32[]{:S(2)}) %collective-permute-start.23) | collective-permute-done | bytes 458784 | tf_op jit(solution)/shard_map/ppermute | solution.py:23
  91.4 2.8 %collective-permute-done.11 = bf16[64,896]{1,0:T(8,128)(2,1)S(1)} collective-permute-done((bf16[64,896]{1,0:T(8,128)(2,1)S(1)}, bf16[64,896]{1,0:T(8,128)(2,1)S(1)}, u32[]{:S(2)}, u32[]{:S(2)}) %collective-permute-start.11) | collective-permute-done | bytes 114720 | tf_op jit(solution)/shard_map/ppermute | solution.py:23
  94.4 3.8 %collective-permute-start.13 = (bf16[2,64,896]{2,1,0:T(8,128)(2,1)S(1)}, bf16[2,64,896]{2,1,0:T(8,128)(2,1)S(1)}, u32[]{:S(2)}, u32[]{:S(2)}) collective-permute-start(bf16[2,64,896]{2,1,0:T(8,128)(2,1)S(1)} %get-tuple-element.56), channel_id=1, source_target_pairs={{0,128},{64,192},{128,0},{192,64},{1,129},{65,193},{129,1},{193,65... | collective-permute-start | bytes 688136 | tf_op jit(solution)/shard_map/ppermute | solution.py:23
  99.3 8.3 %collective-permute-done.13 = bf16[2,64,896]{2,1,0:T(8,128)(2,1)S(1)} collective-permute-done((bf16[2,64,896]{2,1,0:T(8,128)(2,1)S(1)}, bf16[2,64,896]{2,1,0:T(8,128)(2,1)S(1)}, u32[]{:S(2)}, u32[]{:S(2)}) %collective-permute-start.13) | collective-permute-done | bytes 229408 | tf_op jit(solution)/shard_map/ppermute | solution.py:23
  107.6 3.0 %collective-permute-done.14 = bf16[2,64,896]{2,1,0:T(8,128)(2,1)S(1)} collective-permute-done((bf16[2,64,896]{2,1,0:T(8,128)(2,1)S(1)}, bf16[2,64,896]{2,1,0:T(8,128)(2,1)S(1)}, u32[]{:S(2)}, u32[]{:S(2)}) %collective-permute-start.14) | collective-permute-done | bytes 229408 | tf_op jit(solution)/shard_map/ppermute | solution.py:23
  113.7 4.0 %collective-permute-start.30 = (bf16[8,8,1024]{2,1,0:T(8,128)(2,1)S(1)}, bf16[8,8,1024]{2,1,0:T(8,128)(2,1)S(1)}, u32[]{:S(2)}, u32[]{:S(2)}) collective-permute-start(bf16[8,8,1024]{2,1,0:T(8,128)(2,1)S(1)} %get-tuple-element.31), channel_id=1, source_target_pairs={{0,28},{4,0},{8,4},{12,8},{16,12},{20,16},{24,20},{28,24},{1,29},{... | collective-permute-start | bytes 393224 | tf_op jit(solution)/shard_map/ppermute | solution.py:19
  117.8 3.6 %collective-permute-start.31 = (bf16[4,8,1024]{2,1,0:T(8,128)(2,1)S(1)}, bf16[4,8,1024]{2,1,0:T(8,128)(2,1)S(1)}, u32[]{:S(2)}, u32[]{:S(2)}) collective-permute-start(bf16[4,8,1024]{2,1,0:T(8,128)(2,1)S(1)} %get-tuple-element.34), channel_id=1, source_target_pairs={{0,24},{4,28},{8,0},{12,4},{16,8},{20,12},{24,16},{28,20},{1,25},{... | collective-permute-start | bytes 196616 | tf_op jit(solution)/shard_map/ppermute | solution.py:19
  121.4 2.7 %collective-permute-start.26 = (bf16[8,8,1024]{2,1,0:T(8,128)(2,1)S(1)}, bf16[8,8,1024]{2,1,0:T(8,128)(2,1)S(1)}, u32[]{:S(2)}, u32[]{:S(2)}) collective-permute-start(bf16[8,8,1024]{2,1,0:T(8,128)(2,1)S(1)} %get-tuple-element.32), channel_id=1, source_target_pairs={{0,28},{4,0},{8,4},{12,8},{16,12},{20,16},{24,20},{28,24},{1,29},{... | collective-permute-start | bytes 393224 | tf_op jit(solution)/shard_map/ppermute | solution.py:19
  124.6 3.6 %collective-permute-start.32 = (bf16[8,8,1024]{2,1,0:T(8,128)(2,1)S(1)}, bf16[8,8,1024]{2,1,0:T(8,128)(2,1)S(1)}, u32[]{:S(2)}, u32[]{:S(2)}) collective-permute-start(bf16[8,8,1024]{2,1,0:T(8,128)(2,1)S(1)} %pad_maximum_fusion.12), channel_id=1, source_target_pairs={{0,24},{4,28},{8,0},{12,4},{16,8},{20,12},{24,16},{28,20},{1,25},{... | collective-permute-start | bytes 393224 | tf_op jit(solution)/shard_map/ppermute | solution.py:19
  128.3 3.5 %collective-permute-done.29 = bf16[8,8,1024]{2,1,0:T(8,128)(2,1)S(1)} collective-permute-done((bf16[8,8,1024]{2,1,0:T(8,128)(2,1)S(1)}, bf16[8,8,1024]{2,1,0:T(8,128)(2,1)S(1)}, u32[]{:S(2)}, u32[]{:S(2)}) %collective-permute-start.29) | collective-permute-done | bytes 131104 | tf_op jit(solution)/shard_map/ppermute | solution.py:19
  133.4 2.4 %collective-permute-start.33 = (bf16[8,8,1024]{2,1,0:T(8,128)(2,1)S(1)}, bf16[8,8,1024]{2,1,0:T(8,128)(2,1)S(1)}, u32[]{:S(2)}, u32[]{:S(2)}) collective-permute-start(bf16[8,8,1024]{2,1,0:T(8,128)(2,1)S(1)} %fusion.29), channel_id=1, source_target_pairs={{0,2},{2,0},{1,3},{3,1},{4,6},{6,4},{5,7},{7,5},{8,10},{10,8},{9,1... | collective-permute-start | bytes 393224 | tf_op jit(solution)/shard_map/ppermute | solution.py:19
  135.9 3.0 %collective-permute-done.33 = bf16[8,8,1024]{2,1,0:T(8,128)(2,1)S(1)} collective-permute-done((bf16[8,8,1024]{2,1,0:T(8,128)(2,1)S(1)}, bf16[8,8,1024]{2,1,0:T(8,128)(2,1)S(1)}, u32[]{:S(2)}, u32[]{:S(2)}) %collective-permute-start.33) | collective-permute-done | bytes 131104 | tf_op jit(solution)/shard_map/ppermute | solution.py:19
  139.1 7.4 %all_to_all.20 = f32[8,8,8]{2,1,0:T(8,128)S(1)} all-to-all(f32[8,8,8]{2,1,0:T(8,128)S(1)} %broadcast_in_dim.6), channel_id=1, replica_groups=mesh['x'=4,'y'=2,'z'=8,'w'=2,'c'=2] {'x','y'}, dimensions={0} | all-to-all | bytes 4096 | tf_op jit(solution)/shard_map/all_to_all | solution.py:134
  146.8 14.3 %all_to_all.21 = bf16[8,8,1024]{2,1,0:T(8,128)(2,1)S(1)} all-to-all(bf16[8,8,1024]{2,1,0:T(8,128)(2,1)S(1)} %broadcast_in_dim.7), channel_id=1, replica_groups=mesh['x'=4,'y'=2,'z'=8,'w'=2,'c'=2] {'z'}, dimensions={0} | all-to-all | bytes 262144 | tf_op jit(solution)/shard_map/all_to_all | solution.py:144
  161.1 5.4 %collective-permute-start.34 = (bf16[64,1024]{1,0:T(8,128)(2,1)S(1)}, bf16[64,1024]{1,0:T(8,128)(2,1)S(1)}, u32[]{:S(2)}, u32[]{:S(2)}) collective-permute-start(bf16[64,1024]{1,0:T(8,128)(2,1)S(1)} %bitcast.202), channel_id=1, source_target_pairs={{0,1},{1,0},{2,3},{3,2},{4,5},{5,4},{6,7},{7,6},{8,9},{9,8},{10,11... | collective-permute-start | bytes 393224 | tf_op jit(solution)/shard_map/ppermute | solution.py:23
  167.6 3.5 %convolution_convert_fusion = bf16[128,2688]{1,0:T(8,128)(2,1)S(1)} fusion(bf16[1024,2688]{1,0:T(8,128)(2,1)} %param.13, bf16[64,1024]{1,0:T(8,128)(2,1)S(1)} %get-tuple-element.54, bf16[64,1024]{1,0:T(8,128)(2,1)S(1)} %get-tuple-element.53), kind=kOutput, calls=%fused_computation | convolution fusion | flops 705511424 | bytes 6455296 | tf_op jit(solution)/shard_map/dot_general | solution.py:150
  171.1 13.5 %all_to_all.22 = bf16[8,16,2688]{2,1,0:T(8,128)(2,1)S(1)} all-to-all(bf16[8,16,2688]{2,1,0:T(8,128)(2,1)S(1)} %bitcast.188), channel_id=1, replica_groups=mesh['x'=4,'y'=2,'z'=8,'w'=2,'c'=2] {'x','y'}, dimensions={0} | all-to-all | bytes 1376256 | tf_op jit(solution)/shard_map/all_to_all | solution.py:152
  185.1 14.9 %all_to_all.23 = f32[32,1,16]{2,1,0:T(1,128)S(1)} all-to-all(f32[32,1,16]{2,1,0:T(1,128)S(1)} %broadcast_in_dim.8), channel_id=1, replica_groups=mesh['x'=4,'y'=2,'z'=8,'w'=2,'c'=2] {'z','w','c'}, dimensions={0} | all-to-all | bytes 4096 | tf_op jit(solution)/shard_map/all_to_all | solution.py:157
  (137 shorter events, 41.3 us)
Async XLA Ops:
  2.7 10.0 %collective-permute-start = (bf16[64,1024]{1,0:T(8,128)(2,1)}, bf16[64,1024]{1,0:T(8,128)(2,1)S(1)}, u32[]{:S(2)}, u32[]{:S(2)}) collective-permute-start(bf16[64,1024]{1,0:T(8,128)(2,1)} %get-tuple-element.14), channel_id=1, source_target_pairs={{0,32},{32,0},{64,96},{96,64},{128,160},{160,128},{192,224},{224,1... | collective-permute-start | bytes 393224 | tf_op jit(solution)/shard_map/ppermute | solution.py:31
  4.9 11.1 %collective-permute-start.1 = (bf16[64,1024]{1,0:T(8,128)(2,1)}, bf16[64,1024]{1,0:T(8,128)(2,1)S(1)}, u32[]{:S(2)}, u32[]{:S(2)}) collective-permute-start(bf16[64,1024]{1,0:T(8,128)(2,1)} %get-tuple-element.15), channel_id=1, source_target_pairs={{0,64},{32,96},{64,0},{96,32},{128,192},{160,224},{192,128},{224,1... | collective-permute-start | bytes 393224 | tf_op jit(solution)/shard_map/ppermute | solution.py:31
  6.1 10.6 %collective-permute-start.2 = (bf16[64,1024]{1,0:T(8,128)(2,1)}, bf16[64,1024]{1,0:T(8,128)(2,1)S(1)}, u32[]{:S(2)}, u32[]{:S(2)}) collective-permute-start(bf16[64,1024]{1,0:T(8,128)(2,1)} %get-tuple-element.16), channel_id=1, source_target_pairs={{0,96},{32,64},{64,32},{96,0},{128,224},{160,192},{192,160},{224,1... | collective-permute-start | bytes 393224 | tf_op jit(solution)/shard_map/ppermute | solution.py:31
  6.1 11.2 %collective-permute-start.3 = (bf16[64,1024]{1,0:T(8,128)(2,1)}, bf16[64,1024]{1,0:T(8,128)(2,1)S(1)}, u32[]{:S(2)}, u32[]{:S(2)}) collective-permute-start(bf16[64,1024]{1,0:T(8,128)(2,1)} %get-tuple-element.17), channel_id=1, source_target_pairs={{0,128},{32,160},{64,192},{96,224},{128,0},{160,32},{192,64},{224,... | collective-permute-start | bytes 393224 | tf_op jit(solution)/shard_map/ppermute | solution.py:31
  9.0 10.9 %collective-permute-start.4 = (bf16[64,1024]{1,0:T(8,128)(2,1)}, bf16[64,1024]{1,0:T(8,128)(2,1)S(1)}, u32[]{:S(2)}, u32[]{:S(2)}) collective-permute-start(bf16[64,1024]{1,0:T(8,128)(2,1)} %get-tuple-element.18), channel_id=1, source_target_pairs={{0,160},{32,128},{64,224},{96,192},{128,32},{160,0},{192,96},{224,... | collective-permute-start | bytes 393224 | tf_op jit(solution)/shard_map/ppermute | solution.py:31
  12.8 11.1 %collective-permute-start.5 = (bf16[64,1024]{1,0:T(8,128)(2,1)}, bf16[64,1024]{1,0:T(8,128)(2,1)S(1)}, u32[]{:S(2)}, u32[]{:S(2)}) collective-permute-start(bf16[64,1024]{1,0:T(8,128)(2,1)} %get-tuple-element.19), channel_id=1, source_target_pairs={{0,192},{32,224},{64,128},{96,160},{128,64},{160,96},{192,0},{224,... | collective-permute-start | bytes 393224 | tf_op jit(solution)/shard_map/ppermute | solution.py:31
  16.0 10.6 %collective-permute-start.6 = (bf16[64,1024]{1,0:T(8,128)(2,1)}, bf16[64,1024]{1,0:T(8,128)(2,1)S(1)}, u32[]{:S(2)}, u32[]{:S(2)}) collective-permute-start(bf16[64,1024]{1,0:T(8,128)(2,1)} %get-tuple-element.20), channel_id=1, source_target_pairs={{0,224},{32,192},{64,160},{96,128},{128,96},{160,64},{192,32},{224... | collective-permute-start | bytes 393224 | tf_op jit(solution)/shard_map/ppermute | solution.py:31
  27.3 6.0 %collective-permute-start.15 = (bf16[8,64,1024]{2,1,0:T(8,128)(2,1)}, bf16[8,64,1024]{2,1,0:T(8,128)(2,1)S(1)}, u32[]{:S(2)}, u32[]{:S(2)}) collective-permute-start(bf16[8,64,1024]{2,1,0:T(8,128)(2,1)} %bitcast_dynamic-update-slice_fusion), channel_id=1, source_target_pairs={{0,1},{1,0},{2,3},{3,2},{4,5},{5,4},{6,7},{7,6},{8,9},{9,8},{10,11... | collective-permute-start | bytes 3145736 | tf_op jit(solution)/shard_map/ppermute | solution.py:23
  31.9 28.5 %collective-permute-start.7 = (bf16[2,4,64,896]{3,2,1,0:T(8,128)(2,1)S(1)}, bf16[2,4,64,896]{3,2,1,0:T(8,128)(2,1)S(1)}, u32[]{:S(2)}, u32[]{:S(2)}) collective-permute-start(bf16[2,4,64,896]{3,2,1,0:T(8,128)(2,1)S(1)} %pad_maximum_fusion), channel_id=1, source_target_pairs={{0,32},{32,0},{1,33},{33,1},{2,34},{34,2},{3,35},{35,3},{4,36},{36... | collective-permute-start | bytes 2752520 | tf_op jit(solution)/shard_map/ppermute | solution.py:23
  36.0 13.4 %collective-permute-start.16 = (bf16[2,2,64,896]{3,2,1,0:T(8,128)(2,1)S(1)}, bf16[2,2,64,896]{3,2,1,0:T(8,128)(2,1)S(1)}, u32[]{:S(2)}, u32[]{:S(2)}) collective-permute-start(bf16[2,2,64,896]{3,2,1,0:T(8,128)(2,1)S(1)} %pad_maximum_fusion.2), channel_id=1, source_target_pairs={{0,128},{64,192},{128,0},{192,64},{1,129},{65,193},{129,1},{193,65... | collective-permute-start | bytes 1376264 | tf_op jit(solution)/shard_map/ppermute | solution.py:23
  36.7 20.4 %collective-permute-start.17 = (bf16[2,2,64,896]{3,2,1,0:T(8,128)(2,1)S(1)}, bf16[2,2,64,896]{3,2,1,0:T(8,128)(2,1)S(1)}, u32[]{:S(2)}, u32[]{:S(2)}) collective-permute-start(bf16[2,2,64,896]{3,2,1,0:T(8,128)(2,1)S(1)} %pad_maximum_fusion.3), channel_id=1, source_target_pairs={{0,64},{64,0},{128,192},{192,128},{1,65},{65,1},{129,193},{193,129... | collective-permute-start | bytes 1376264 | tf_op jit(solution)/shard_map/ppermute | solution.py:23
  37.0 22.8 %collective-permute-start.18 = (bf16[2,2,64,896]{3,2,1,0:T(8,128)(2,1)S(1)}, bf16[2,2,64,896]{3,2,1,0:T(8,128)(2,1)S(1)}, u32[]{:S(2)}, u32[]{:S(2)}) collective-permute-start(bf16[2,2,64,896]{3,2,1,0:T(8,128)(2,1)S(1)} %pad_maximum_fusion.4), channel_id=1, source_target_pairs={{0,192},{64,128},{128,64},{192,0},{1,193},{65,129},{129,65},{193,1... | collective-permute-start | bytes 1376264 | tf_op jit(solution)/shard_map/ppermute | solution.py:23
  60.1 6.8 %collective-permute-start.19 = (bf16[2,64,896]{2,1,0:T(8,128)(2,1)S(1)}, bf16[2,64,896]{2,1,0:T(8,128)(2,1)S(1)}, u32[]{:S(2)}, u32[]{:S(2)}) collective-permute-start(bf16[2,64,896]{2,1,0:T(8,128)(2,1)S(1)} %pad_maximum_fusion.10), channel_id=1, source_target_pairs={{0,32},{32,0},{1,33},{33,1},{2,34},{34,2},{3,35},{35,3},{4,36},{36... | collective-permute-start | bytes 688136 | tf_op jit(solution)/shard_map/ppermute | solution.py:23
  67.2 6.3 %collective-permute-start.21 = (bf16[64,896]{1,0:T(8,128)(2,1)S(1)}, bf16[64,896]{1,0:T(8,128)(2,1)S(1)}, u32[]{:S(2)}, u32[]{:S(2)}) collective-permute-start(bf16[64,896]{1,0:T(8,128)(2,1)S(1)} %fusion.30), channel_id=1, source_target_pairs={{0,128},{64,192},{128,0},{192,64},{1,129},{65,193},{129,1},{193,65... | collective-permute-start | bytes 344072 | tf_op jit(solution)/shard_map/ppermute | solution.py:23
  68.5 7.4 %collective-permute-start.22 = (bf16[64,896]{1,0:T(8,128)(2,1)S(1)}, bf16[64,896]{1,0:T(8,128)(2,1)S(1)}, u32[]{:S(2)}, u32[]{:S(2)}) collective-permute-start(bf16[64,896]{1,0:T(8,128)(2,1)S(1)} %fusion.30), channel_id=1, source_target_pairs={{0,192},{64,128},{128,64},{192,0},{1,193},{65,129},{129,65},{193,1... | collective-permute-start | bytes 344072 | tf_op jit(solution)/shard_map/ppermute | solution.py:23
  76.0 10.8 %collective-permute-start.23 = (bf16[4,64,896]{2,1,0:T(8,128)(2,1)S(1)}, bf16[4,64,896]{2,1,0:T(8,128)(2,1)S(1)}, u32[]{:S(2)}, u32[]{:S(2)}) collective-permute-start(bf16[4,64,896]{2,1,0:T(8,128)(2,1)S(1)} %get-tuple-element.52), channel_id=1, source_target_pairs={{0,32},{32,0},{1,33},{33,1},{2,34},{34,2},{3,35},{35,3},{4,36},{36... | collective-permute-start | bytes 1376264 | tf_op jit(solution)/shard_map/ppermute | solution.py:23
  76.8 13.6 %collective-permute-start.8 = (bf16[2,64,896]{2,1,0:T(8,128)(2,1)S(1)}, bf16[2,64,896]{2,1,0:T(8,128)(2,1)S(1)}, u32[]{:S(2)}, u32[]{:S(2)}) collective-permute-start(bf16[2,64,896]{2,1,0:T(8,128)(2,1)S(1)} %pad_maximum_fusion.6), channel_id=1, source_target_pairs={{0,128},{64,192},{128,0},{192,64},{1,129},{65,193},{129,1},{193,65... | collective-permute-start | bytes 688136 | tf_op jit(solution)/shard_map/ppermute | solution.py:23
  76.9 13.4 %collective-permute-start.9 = (bf16[2,64,896]{2,1,0:T(8,128)(2,1)S(1)}, bf16[2,64,896]{2,1,0:T(8,128)(2,1)S(1)}, u32[]{:S(2)}, u32[]{:S(2)}) collective-permute-start(bf16[2,64,896]{2,1,0:T(8,128)(2,1)S(1)} %pad_maximum_fusion.7), channel_id=1, source_target_pairs={{0,64},{64,0},{128,192},{192,128},{1,65},{65,1},{129,193},{193,129... | collective-permute-start | bytes 688136 | tf_op jit(solution)/shard_map/ppermute | solution.py:23
  79.3 11.1 %collective-permute-start.10 = (bf16[2,64,896]{2,1,0:T(8,128)(2,1)S(1)}, bf16[2,64,896]{2,1,0:T(8,128)(2,1)S(1)}, u32[]{:S(2)}, u32[]{:S(2)}) collective-permute-start(bf16[2,64,896]{2,1,0:T(8,128)(2,1)S(1)} %pad_maximum_fusion.8), channel_id=1, source_target_pairs={{0,192},{64,128},{128,64},{192,0},{1,193},{65,129},{129,65},{193,1... | collective-permute-start | bytes 688136 | tf_op jit(solution)/shard_map/ppermute | solution.py:23
  88.0 22.6 %collective-permute-start.24 = (bf16[4,2,64,1024]{3,2,1,0:T(8,128)(2,1)S(1)}, bf16[4,2,64,1024]{3,2,1,0:T(8,128)(2,1)S(1)}, u32[]{:S(2)}, u32[]{:S(2)}) collective-permute-start(bf16[4,2,64,1024]{3,2,1,0:T(8,128)(2,1)S(1)} %fusion.8), channel_id=1, source_target_pairs={{0,1},{1,0},{2,3},{3,2},{4,5},{5,4},{6,7},{7,6},{8,9},{9,8},{10,11... | collective-permute-start | bytes 3145736 | tf_op jit(solution)/shard_map/ppermute | solution.py:23
  94.4 13.2 %collective-permute-start.13 = (bf16[2,64,896]{2,1,0:T(8,128)(2,1)S(1)}, bf16[2,64,896]{2,1,0:T(8,128)(2,1)S(1)}, u32[]{:S(2)}, u32[]{:S(2)}) collective-permute-start(bf16[2,64,896]{2,1,0:T(8,128)(2,1)S(1)} %get-tuple-element.56), channel_id=1, source_target_pairs={{0,128},{64,192},{128,0},{192,64},{1,129},{65,193},{129,1},{193,65... | collective-permute-start | bytes 688136 | tf_op jit(solution)/shard_map/ppermute | solution.py:23
  98.3 12.4 %collective-permute-start.14 = (bf16[2,64,896]{2,1,0:T(8,128)(2,1)S(1)}, bf16[2,64,896]{2,1,0:T(8,128)(2,1)S(1)}, u32[]{:S(2)}, u32[]{:S(2)}) collective-permute-start(bf16[2,64,896]{2,1,0:T(8,128)(2,1)S(1)} %get-tuple-element.56), channel_id=1, source_target_pairs={{0,192},{64,128},{128,64},{192,0},{1,193},{65,129},{129,65},{193,1... | collective-permute-start | bytes 688136 | tf_op jit(solution)/shard_map/ppermute | solution.py:23
  112.0 9.4 %collective-permute-start.27 = (bf16[8,8,1024]{2,1,0:T(8,128)(2,1)S(1)}, bf16[8,8,1024]{2,1,0:T(8,128)(2,1)S(1)}, u32[]{:S(2)}, u32[]{:S(2)}) collective-permute-start(bf16[8,8,1024]{2,1,0:T(8,128)(2,1)S(1)} %get-tuple-element.30), channel_id=1, source_target_pairs={{0,4},{4,8},{8,12},{12,16},{16,20},{20,24},{24,28},{28,0},{1,5},{5... | collective-permute-start | bytes 393224 | tf_op jit(solution)/shard_map/ppermute | solution.py:19
  113.7 10.4 %collective-permute-start.30 = (bf16[8,8,1024]{2,1,0:T(8,128)(2,1)S(1)}, bf16[8,8,1024]{2,1,0:T(8,128)(2,1)S(1)}, u32[]{:S(2)}, u32[]{:S(2)}) collective-permute-start(bf16[8,8,1024]{2,1,0:T(8,128)(2,1)S(1)} %get-tuple-element.31), channel_id=1, source_target_pairs={{0,28},{4,0},{8,4},{12,8},{16,12},{20,16},{24,20},{28,24},{1,29},{... | collective-permute-start | bytes 393224 | tf_op jit(solution)/shard_map/ppermute | solution.py:19
  117.7 6.7 %collective-permute-start.28 = (bf16[4,8,1024]{2,1,0:T(8,128)(2,1)S(1)}, bf16[4,8,1024]{2,1,0:T(8,128)(2,1)S(1)}, u32[]{:S(2)}, u32[]{:S(2)}) collective-permute-start(bf16[4,8,1024]{2,1,0:T(8,128)(2,1)S(1)} %get-tuple-element.33), channel_id=1, source_target_pairs={{0,8},{4,12},{8,16},{12,20},{16,24},{20,28},{24,0},{28,4},{1,9},{5... | collective-permute-start | bytes 196616 | tf_op jit(solution)/shard_map/ppermute | solution.py:19
  117.8 6.7 %collective-permute-start.31 = (bf16[4,8,1024]{2,1,0:T(8,128)(2,1)S(1)}, bf16[4,8,1024]{2,1,0:T(8,128)(2,1)S(1)}, u32[]{:S(2)}, u32[]{:S(2)}) collective-permute-start(bf16[4,8,1024]{2,1,0:T(8,128)(2,1)S(1)} %get-tuple-element.34), channel_id=1, source_target_pairs={{0,24},{4,28},{8,0},{12,4},{16,8},{20,12},{24,16},{28,20},{1,25},{... | collective-permute-start | bytes 196616 | tf_op jit(solution)/shard_map/ppermute | solution.py:19
  121.4 6.9 %collective-permute-start.25 = (bf16[8,8,1024]{2,1,0:T(8,128)(2,1)S(1)}, bf16[8,8,1024]{2,1,0:T(8,128)(2,1)S(1)}, u32[]{:S(2)}, u32[]{:S(2)}) collective-permute-start(bf16[8,8,1024]{2,1,0:T(8,128)(2,1)S(1)} %get-tuple-element.29), channel_id=1, source_target_pairs={{0,4},{4,8},{8,12},{12,16},{16,20},{20,24},{24,28},{28,0},{1,5},{5... | collective-permute-start | bytes 393224 | tf_op jit(solution)/shard_map/ppermute | solution.py:19
  121.4 6.9 %collective-permute-start.26 = (bf16[8,8,1024]{2,1,0:T(8,128)(2,1)S(1)}, bf16[8,8,1024]{2,1,0:T(8,128)(2,1)S(1)}, u32[]{:S(2)}, u32[]{:S(2)}) collective-permute-start(bf16[8,8,1024]{2,1,0:T(8,128)(2,1)S(1)} %get-tuple-element.32), channel_id=1, source_target_pairs={{0,28},{4,0},{8,4},{12,8},{16,12},{20,16},{24,20},{28,24},{1,29},{... | collective-permute-start | bytes 393224 | tf_op jit(solution)/shard_map/ppermute | solution.py:19
  124.5 7.4 %collective-permute-start.29 = (bf16[8,8,1024]{2,1,0:T(8,128)(2,1)S(1)}, bf16[8,8,1024]{2,1,0:T(8,128)(2,1)S(1)}, u32[]{:S(2)}, u32[]{:S(2)}) collective-permute-start(bf16[8,8,1024]{2,1,0:T(8,128)(2,1)S(1)} %pad_maximum_fusion.11), channel_id=1, source_target_pairs={{0,8},{4,12},{8,16},{12,20},{16,24},{20,28},{24,0},{28,4},{1,9},{5... | collective-permute-start | bytes 393224 | tf_op jit(solution)/shard_map/ppermute | solution.py:19
  124.6 8.7 %collective-permute-start.32 = (bf16[8,8,1024]{2,1,0:T(8,128)(2,1)S(1)}, bf16[8,8,1024]{2,1,0:T(8,128)(2,1)S(1)}, u32[]{:S(2)}, u32[]{:S(2)}) collective-permute-start(bf16[8,8,1024]{2,1,0:T(8,128)(2,1)S(1)} %pad_maximum_fusion.12), channel_id=1, source_target_pairs={{0,24},{4,28},{8,0},{12,4},{16,8},{20,12},{24,16},{28,20},{1,25},{... | collective-permute-start | bytes 393224 | tf_op jit(solution)/shard_map/ppermute | solution.py:19
  133.4 5.4 %collective-permute-start.33 = (bf16[8,8,1024]{2,1,0:T(8,128)(2,1)S(1)}, bf16[8,8,1024]{2,1,0:T(8,128)(2,1)S(1)}, u32[]{:S(2)}, u32[]{:S(2)}) collective-permute-start(bf16[8,8,1024]{2,1,0:T(8,128)(2,1)S(1)} %fusion.29), channel_id=1, source_target_pairs={{0,2},{2,0},{1,3},{3,1},{4,6},{6,4},{5,7},{7,5},{8,10},{10,8},{9,1... | collective-permute-start | bytes 393224 | tf_op jit(solution)/shard_map/ppermute | solution.py:19
  161.1 6.4 %collective-permute-start.34 = (bf16[64,1024]{1,0:T(8,128)(2,1)S(1)}, bf16[64,1024]{1,0:T(8,128)(2,1)S(1)}, u32[]{:S(2)}, u32[]{:S(2)}) collective-permute-start(bf16[64,1024]{1,0:T(8,128)(2,1)S(1)} %bitcast.202), channel_id=1, source_target_pairs={{0,1},{1,0},{2,3},{3,2},{4,5},{5,4},{6,7},{7,6},{8,9},{9,8},{10,11... | collective-permute-start | bytes 393224 | tf_op jit(solution)/shard_map/ppermute | solution.py:23
  (10 other events, 115.6 us)
